TPU v7x, 256 devices: a whole 4x4x8 slice. The times are simulated.
256 devices in a mesh: rows: 4 (over y), cand: 64 (over x, z, core).
Axes of the slice: x: 4, y: 4, z: 8, core: 2. Of those that a mesh axis runs over, the one named last changes fastest.
Arguments:
- whitened: float32 [256, 2048], P('cand', 'rows'), may hold values from -6 to 6
- factor_rows: float32 [2048, 2048], P('rows'), as said below
- diag_inv: float32 [2048, 512], P('rows'), as said below
- observed: float32 [22, 2048], P(None, 'rows'), may hold values from 0 to 1
- inv_length: float32 [22], replicated, may hold values from 0.4 to 2
- grid_coords: int32 [22, 262144], P(None, 'cand'), may hold values from 0 to 20
- frequencies: float32 [22, 8192], P(None, 'rows'), may hold values from -8 to 8
- phases: float32 [8192], P('rows'), may hold values from -3.140625 to 3.140625
- prior_coef: bfloat16 [256, 8192], P('cand', 'rows'), may hold values from -6 to 6
Outputs:
- samples_at: float32 [262144, 256], P('cand', 'rows')
Inputs may be any that keep to these rules, and one draw needn't show every extreme that they name: `factor_rows`: entries in and above the diagonal blocks of 512 x 512 are zero. `diag_inv`: each block of 512 rows is lower triangular with a positive diagonal.
All inputs are finite; a program needn't handle non-finite values.
Results may differ from a plain program's by a relative error of at most 0.004.
Values may be sent and summed in bfloat16 or wider, within the bound.
No kernel may reach another device: no remote copies, remote signals or barrier semaphores. Data moves between devices by JAX's collectives and lax.ppermute only.
A program may use at most 320 MiB of HBM per device.

v0:
```python
import jax
import jax.numpy as jnp
from jax import lax
from jax.sharding import PartitionSpec as P

FEAT = 8192
GRID = 21


def from_behind(shard, axis, by):
    peers = lax.axis_size(axis)
    pairs = [(i, i + by) for i in range(peers) if 0 <= i + by < peers]
    return lax.ppermute(shard, axis, pairs)


def solve_chain(whitened, factor_rows, diag_inv):
    sections = lax.axis_size("rows")
    position = lax.axis_index("rows")
    rows_dev = factor_rows.shape[0]
    block_width = diag_inv.shape[1]
    offset = position * rows_dev
    carried = jnp.zeros((whitened.shape[0], factor_rows.shape[1]), jnp.float32)
    weights = jnp.zeros_like(whitened)

    def solve_own(state):
        incoming, earlier = state
        remaining = whitened - lax.dynamic_slice_in_dim(incoming, offset, rows_dev, 1)
        pieces = []
        for block_id in reversed(range(rows_dev // block_width)):
            first_col = block_id * block_width
            solved = jnp.dot(
                remaining[:, first_col : first_col + block_width],
                diag_inv,
                precision=lax.Precision.HIGHEST,
                preferred_element_type=jnp.float32,
            )
            own_columns = lax.dynamic_slice_in_dim(factor_rows, offset, rows_dev, 1)
            remaining = remaining - jnp.dot(
                solved,
                own_columns,
                precision=lax.Precision.HIGHEST,
                preferred_element_type=jnp.float32,
            )
            pieces.append(solved)
        solved_all = jnp.concatenate(pieces[::-1], axis=1)
        updated = incoming + jnp.dot(
            solved_all,
            factor_rows,
            precision=lax.Precision.HIGHEST,
            preferred_element_type=jnp.float32,
        )
        return (updated, solved_all)

    def pass_on(state):
        return state

    for section_id in range(sections):
        carried, weights = lax.cond(
            position == sections - 1 - section_id, solve_own, pass_on, (carried, weights)
        )
        if section_id + 1 < sections:
            carried = from_behind(carried, "rows", -1)
    return weights


def prior_slab(mixture, frequencies, phases, coef_slab):
    angles = (
        lax.dot_general(
            mixture,
            frequencies,
            (((0,), (0,)), ((), ())),
            precision=lax.Precision.HIGHEST,
            preferred_element_type=jnp.float32,
        )
        + phases[None, :]
    )
    features_map = (jnp.sqrt(2.0 / FEAT) * jnp.cos(angles)).astype(jnp.bfloat16)
    return lax.dot_general(
        features_map, coef_slab, (((1,), (1,)), ((), ())), preferred_element_type=jnp.float32
    )


def cross_part(mixture, observed, inv_length, weights_wire):
    squared = jnp.zeros((mixture.shape[1], observed.shape[1]), jnp.float32)
    for column in range(mixture.shape[0]):
        gap = (mixture[column][:, None] - observed[column][None, :]) * inv_length[column]
        squared = squared + gap * gap
    kernel_tile = jnp.exp(-0.5 * squared).astype(jnp.bfloat16)
    return lax.dot_general(
        kernel_tile, weights_wire, (((1,), (1,)), ((), ())), preferred_element_type=jnp.float32
    )


def body(
    whitened,
    factor_rows,
    diag_inv,
    observed,
    inv_length,
    grid_coords,
    frequencies,
    phases,
    prior_coef,
):
    coef_all = lax.all_gather(prior_coef, "cand", axis=0, tiled=True)
    weights = lax.all_gather(
        solve_chain(whitened, factor_rows, diag_inv).astype(jnp.bfloat16),
        "cand",
        axis=0,
        tiled=True,
    )
    mixture = grid_coords.astype(jnp.float32) / (GRID - 1)
    summed = prior_slab(mixture, frequencies, phases, coef_all) + cross_part(
        mixture, observed, inv_length, weights
    )
    return lax.psum_scatter(summed, "rows", scatter_dimension=1, tiled=True)


def solution(mesh):
    in_specs = (
        P("cand", "rows"),
        P("rows", None),
        P("rows", None),
        P(None, "rows"),
        P(),
        P(None, "cand"),
        P(None, "rows"),
        P("rows"),
        P("cand", "rows"),
    )
    out_specs = P("cand", "rows")
    return jax.shard_map(body, mesh=mesh, in_specs=in_specs, out_specs=out_specs, check_vma=False)
```

profile of v0, /device:TPU:1, one launch (start us, length us, event | category | flops | bytes accessed | tf_op | source)
XLA Modules:
  0.0 327.4 jit_solution(7780740695992511488)
XLA Ops:
  6.5 0.0 copy-start
  6.5 0.0 all-gather.4.cloned.1.call-start
  6.5 0.7 all-gather.4.cloned.1.call-update
  7.3 0.0 reduce-scatter.2.cloned.1.call-start
  7.3 0.6 conditional.4
  7.3 0.6 broadcast_in_dim.6
  7.9 1.3 collective-permute-start
  9.2 1.0 convert_multiply_fusion
  10.3 0.0 copy-start.3
  10.3 0.3 fusion.85
  10.6 0.8 fusion.88
  11.4 1.2 fusion.87
  12.6 2.1 fusion.89
  14.6 1.4 fusion.90
  16.1 0.0 collective-permute-done
  16.1 1.3 collective-permute-start.1
  17.4 44.7 %exponential_convert_fusion.4 = bf16[4096,512]{1,0:T(8,128)(2,1)} fusion(f32[]{:T(128)} %bitcast.66, f32[512]{0:T(512)S(1)} %bitcast.129, f32[4096]{0:T(1024)S(1)} %bitcast.107, f32[]{:T(128)} %bitcast.63, f32[512]{0:T(512)S(1)} %bitcast.130, f32[4096]{0:T(1024)S(1)} %bitcast.87, f32[]{:T(128)} %bitcast.60, f32[512]{0:T(512)S(1)} %bitcast.110, ...), kind=kLoop, calls=%fused_computation.18.clone.clone.1 | loop fusion | flops 186646528 | bytes 4599896 | tf_op jit(solution)/shard_map/dot_general | solution.py:89
  62.0 0.0 collective-permute-done.1
  62.0 0.0 copy-start.2
  62.0 0.0 copy-start.4
  62.0 0.0 copy-start.5
  62.1 1.6 collective-permute-start.2
  63.7 0.0 copy-done
  63.7 0.0 copy-done.3
  63.7 30.3 %fusion.84 = f32[4096,2048]{1,0:T(8,128)} fusion(f32[22,2048]{1,0:T(8,128)S(1)} %copy-done, s32[22,4096]{1,0:T(8,128)S(1)} %copy-done.3), kind=kOutput, calls=%fused_computation.91 | convolution fusion | flops 2214772736 | bytes 34095104 | tf_op jit(solution)/shard_map/dot_general | solution.py:68
  94.0 0.0 collective-permute-done.2
  94.0 0.0 copy-done.2
  94.0 0.0 copy-done.4
  94.0 1.2 conditional.7
  94.0 1.2 fusion.8
  95.3 0.7 convert_bitcast_fusion
  96.0 48.9 %all-gather.1 = bf16[64,4,512]{2,1,0:T(4,128)(2,1)S(1)} all-gather(bf16[1,4,512]{2,1,0:T(4,128)(2,1)S(1)} %convert_bitcast_fusion), channel_id=1, replica_groups=mesh['rows'=4,'cand'=64] {'cand'}, dimensions={0}, use_global_device_ids=true | all-gather | bytes 266240 | tf_op jit(solution)/shard_map/all_gather | solution.py:106
  144.8 0.1 reshape.26
  144.9 0.0 all-gather.4.cloned.1.call-done
  144.9 1.3 reshape.24
  146.3 0.0 copy-done.5
  146.3 0.0 copy-start.1
  146.3 114.3 %fusion.12 = f32[4096,256]{0,1:T(8,128)S(1)} fusion(bf16[256,2048]{1,0:T(8,128)(2,1)S(1)} %reshape.24, f32[4096,2048]{1,0:T(8,128)} %fusion.84, f32[2048]{0:T(1024)S(1)} %copy-done.5), kind=kOutput, calls=%fused_computation.15 | convolution fusion | flops 4320133120 | bytes 38805504 | tf_op jit(solution)/shard_map/dot_general | solution.py:78
  260.6 0.0 copy-done.1
  260.6 3.4 %convolution_add_fusion.2 = f32[4096,256]{0,1:T(8,128)} fusion(f32[4096,256]{0,1:T(8,128)S(1)} %fusion.12, bf16[256,512]{1,0:T(8,128)(2,1)S(1)} %reshape.26, bf16[4096,512]{1,0:T(8,128)(2,1)S(1)} %copy-done.1), kind=kOutput, calls=%fused_computation.19 | convolution fusion | flops 1074790400 | bytes 12845056 | tf_op jit(solution)/shard_map/dot_general | solution.py:89
  264.0 0.0 reduce-scatter.2.cloned.1.call-update
  264.0 56.5 %reduce-scatter.2.cloned.1.call-done = f32[4096,64]{0,1:T(8,128)} async-done(((f32[4096,256]{0,1:T(8,128)}), f32[4096,64]{0,1:T(8,128)}) %reduce-scatter.2.cloned.1.call-update) | async-done | bytes 1048592 | tf_op jit(solution)/shard_map/reduce_scatter | solution.py:116
  (4 shorter events, 0.0 us)
Async XLA Ops:
  6.5 57.1 %copy-start = (f32[22,2048]{1,0:T(8,128)S(1)}, f32[22,2048]{1,0:T(8,128)}, u32[]{:S(2)}) copy-start(f32[22,2048]{1,0:T(8,128)} %param.23) | copy-start | bytes 540676
  6.5 138.4 %all-gather.4.cloned.1.call-start = ((), (), s32[]{:S(2)}) async-start(), calls=%async_computation.2 | async-start | bytes 1064960 | tf_op jit(solution)/shard_map/all_gather | solution.py:105
  7.3 313.3 %reduce-scatter.2.cloned.1.call-start = ((), (), s32[]{:S(2)}) async-start(), calls=%async_computation.1 | async-start | bytes 5242880 | tf_op jit(solution)/shard_map/reduce_scatter | solution.py:116
  7.9 8.1 %collective-permute-start = (f32[4,2048]{1,0:T(4,128)S(1)}, f32[4,2048]{1,0:T(4,128)S(1)}, u32[]{:S(2)}, u32[]{:S(2)}) collective-permute-start(f32[4,2048]{1,0:T(4,128)S(1)} %get-tuple-element.77), channel_id=1, source_target_pairs={{64,0},{128,64},{192,128},{65,1},{129,65},{193,129},{66,2},{130,66... | collective-permute-start | bytes 98312 | tf_op jit(solution)/shard_map/ppermute | solution.py:13
  10.3 53.4 %copy-start.3 = (s32[22,4096]{1,0:T(8,128)S(1)}, s32[22,4096]{1,0:T(8,128)}, u32[]{:S(2)}) copy-start(s32[22,4096]{1,0:T(8,128)} %param.22) | copy-start | bytes 1081348
  16.1 45.9 %collective-permute-start.1 = (f32[4,2048]{1,0:T(4,128)S(1)}, f32[4,2048]{1,0:T(4,128)S(1)}, u32[]{:S(2)}, u32[]{:S(2)}) collective-permute-start(f32[4,2048]{1,0:T(4,128)S(1)} %get-tuple-element.79), channel_id=1, source_target_pairs={{64,0},{128,64},{192,128},{65,1},{129,65},{193,129},{66,2},{130,66... | collective-permute-start | bytes 98312 | tf_op jit(solution)/shard_map/ppermute | solution.py:13
  62.0 32.0 %copy-start.2 = (f32[512,512]{1,0:T(8,128)S(1)}, f32[512,512]{1,0:T(8,128)}, u32[]{:S(2)}) copy-start(f32[512,512]{1,0:T(8,128)} %param.19) | copy-start | bytes 3145732
  62.0 32.0 %copy-start.4 = (f32[4,512]{1,0:T(4,128)S(1)}, f32[4,512]{1,0:T(4,128)}, u32[]{:S(2)}) copy-start(f32[4,512]{1,0:T(4,128)} %param.17) | copy-start | bytes 24580
  62.0 84.2 %copy-start.5 = (f32[2048]{0:T(1024)S(1)}, f32[2048]{0:T(1024)}, u32[]{:S(2)}) copy-start(f32[2048]{0:T(1024)} %param.24) | copy-start | bytes 24580
  62.1 32.0 %collective-permute-start.2 = (f32[4,2048]{1,0:T(4,128)S(1)}, f32[4,2048]{1,0:T(4,128)S(1)}, u32[]{:S(2)}, u32[]{:S(2)}) collective-permute-start(f32[4,2048]{1,0:T(4,128)S(1)} %get-tuple-element.82), channel_id=1, source_target_pairs={{64,0},{128,64},{192,128},{65,1},{129,65},{193,129},{66,2},{130,66... | collective-permute-start | bytes 98312 | tf_op jit(solution)/shard_map/ppermute | solution.py:13
  146.3 114.3 %copy-start.1 = (bf16[4096,512]{1,0:T(8,128)(2,1)S(1)}, bf16[4096,512]{1,0:T(8,128)(2,1)}, u32[]{:S(2)}) copy-start(bf16[4096,512]{1,0:T(8,128)(2,1)} %exponential_convert_fusion.4) | copy-start | bytes 12582916
Sparse Core Ops, SparseCore 0:
  10.1 80.9 all-gather.3
  264.1 56.3 reduce-scatter.1
where the time goes:
time: 328 us; the launch traced here: 327 us
  matrix products  149 us (45%)
  waiting for transfers between devices  57.3 us (17%)
  blocking collectives  48.9 us (15%)
  other arithmetic  46.4 us (14%)
  between operations  13.6 us (4%)
  local copies, waits for them, and re-layouts  7.82 us (2%)
  starting transfers between devices  4.21 us (1%)
    dot_general x1, matrix products, prior_slab(): lax.dot_general(features_map, coef_slab, (((1,), (1,)), ((), ())), prefer...  114 us
    reduce_scatter x1, waiting for transfers between devices, body(): return lax.psum_scatter(summed, 'rows', scatter_dimension=1, tiled=True)  56.5 us
    all_gather x1, blocking collectives, body(): lax.all_gather(solve_chain(whitened, factor_rows, diag_inv).astype(jnp.bf...  48.9 us
    dot_general x1, other arithmetic, cross_part(): lax.dot_general(kernel_tile, weights_wire, (((1,), (1,)), ((), ())), pref...  44.7 us
    dot_general x1, matrix products, prior_slab(): lax.dot_general(mixture, frequencies, (((0,), (0,)), ((), ())), precision...  30.3 us
  transfers between devices with their start and end apart: 5, of which 1 were waited for; matrix products, arithmetic and copies ran while one was open for 26% of the time, Pallas kernels for 0%

commit v1 on v0

v1 whole, which is shorter than its diff:
```python
import jax
import jax.numpy as jnp
from jax import lax
from jax.experimental import pallas as pl
from jax.experimental.pallas import tpu as pltpu
from jax.sharding import PartitionSpec as P

F32 = jnp.float32
BF16 = jnp.bfloat16
GRID = 21
DIM = 22
CORES = 2
DEPTHS = 8
WIDTHS = 4
LANES = 128
STRIPE = 24
ROW_CHUNK = 256
CAND_TILE = 256
CHUNKS = 8
PARTS = 2
VMEM_BYTES = 16 * 2**20
LOG2E = 1.4426950408889634
INV_TURN = 0.15915494309189535
SINE = (0.55535848, -0.91343016, 0.4493464, -0.09804192)


def params(limit=VMEM_BYTES):
    return pltpu.CompilerParams(vmem_limit_bytes=limit)


def whole():
    return pl.BlockSpec(memory_space=pltpu.VMEM)


def three_pieces(values):
    high = values.astype(BF16).astype(F32)
    rest = values - high
    middle = rest.astype(BF16).astype(F32)
    return high, middle, (rest - middle).astype(BF16).astype(F32)


def stack_pieces(scratch, values, tail):
    scratch[...] = jnp.zeros_like(scratch)
    for piece, part in enumerate(values):
        scratch[piece * STRIPE : piece * STRIPE + DIM, :] = part
    row = lax.broadcasted_iota(jnp.int32, (8, scratch.shape[1]), 0)
    block = jnp.zeros((8, scratch.shape[1]), F32)
    for index, line in enumerate(tail):
        block = jnp.where(row == index, line, block)
    scratch[3 * STRIPE : 3 * STRIPE + 8, :] = block


def prepare_kernel(
    freq_ref, phase_ref, observed_ref, scale_ref, grid_ref,
    turns_ref, exponent_ref, levels_ref, wide, narrow, tall,
):
    stack_pieces(
        wide,
        three_pieces(freq_ref[...] * (INV_TURN / (GRID - 1))),
        three_pieces(phase_ref[...] * INV_TURN),
    )
    for start in range(0, wide.shape[1], 512):
        turns_ref[start : start + 512, :] = wide[:, start : start + 512].T.astype(BF16)
    squares = scale_ref[...] * scale_ref[...]
    observed = observed_ref[...]
    ones = jnp.ones((1, narrow.shape[1]), F32)
    norm = jnp.sum(observed * observed * squares, axis=0, keepdims=True) * (-0.5 * LOG2E)
    stack_pieces(
        narrow,
        three_pieces(observed * squares * (LOG2E / (GRID - 1))),
        three_pieces(norm) + (ones, ones, ones),
    )
    exponent_ref[...] = narrow[...].T.astype(BF16)
    levels = grid_ref[...].astype(F32)
    ones = jnp.ones((1, tall.shape[1]), F32)
    norm = jnp.sum(levels * levels * squares, axis=0, keepdims=True) * (
        -0.5 * LOG2E / (GRID - 1) ** 2
    )
    stack_pieces(tall, (levels, levels, levels), (ones, ones, ones) + three_pieces(norm))
    levels_ref[...] = tall[...].astype(BF16)


def prepare(frequencies, phases, observed, inv_length, grid_coords):
    feats, obs, cands = frequencies.shape[1], observed.shape[1], grid_coords.shape[1]
    return pl.pallas_call(
        prepare_kernel,
        out_shape=(
            jax.ShapeDtypeStruct((feats, LANES), BF16),
            jax.ShapeDtypeStruct((obs, LANES), BF16),
            jax.ShapeDtypeStruct((LANES, cands), BF16),
        ),
        in_specs=[whole()] * 5,
        out_specs=(whole(),) * 3,
        scratch_shapes=[
            pltpu.VMEM((LANES, feats), F32),
            pltpu.VMEM((LANES, obs), F32),
            pltpu.VMEM((LANES, cands), F32),
        ],
        compiler_params=params(),
        cost_estimate=pl.CostEstimate(flops=10**7, transcendentals=0, bytes_accessed=4 * 2**20),
        name="prepare",
    )(frequencies, phases[None, :], observed, inv_length[:, None], grid_coords)


def cosine(turns):
    near = turns - jnp.round(turns)
    square = near * near
    poly = ((SINE[3] * square + SINE[2]) * square + SINE[1]) * square + SINE[0]
    sine = near * poly
    return (0.015625 - sine * sine).astype(BF16)


def tile_kernel(turns_ref, exponent_ref, levels_ref, features_ref, kernel_ref):
    levels = levels_ref[...]
    for start in range(0, turns_ref.shape[0], ROW_CHUNK):
        rows = slice(start, start + ROW_CHUNK)
        turns = jnp.dot(turns_ref[rows, :], levels, preferred_element_type=F32)
        features_ref[rows, :] = cosine(turns)
    for start in range(0, exponent_ref.shape[0], ROW_CHUNK):
        rows = slice(start, start + ROW_CHUNK)
        exponent = jnp.dot(exponent_ref[rows, :], levels, preferred_element_type=F32)
        kernel_ref[rows, :] = jnp.exp2(exponent).astype(BF16)


def tiles(turns, exponent, levels, chunk):
    feats, obs = turns.shape[0], exponent.shape[0]
    cands = levels.shape[1] // CHUNKS
    steps = cands // CAND_TILE
    return pl.pallas_call(
        tile_kernel,
        out_shape=(
            jax.ShapeDtypeStruct((feats, cands), BF16),
            jax.ShapeDtypeStruct((obs, cands), BF16),
        ),
        grid=(steps,),
        in_specs=[
            whole(),
            whole(),
            pl.BlockSpec((LANES, CAND_TILE), lambda i: (0, i + chunk * steps)),
        ],
        out_specs=(
            pl.BlockSpec((feats, CAND_TILE), lambda i: (0, i)),
            pl.BlockSpec((obs, CAND_TILE), lambda i: (0, i)),
        ),
        compiler_params=params(),
        cost_estimate=pl.CostEstimate(
            flops=24 * (feats + obs) * cands,
            transcendentals=obs * cands,
            bytes_accessed=2 * (feats + obs) * cands,
        ),
    )(turns, exponent, levels)


def order_kernel(place_ref, near_ref, far_ref, out_ref):
    rows, half = out_ref.shape[0], near_ref.shape[0]
    block = rows // WIDTHS
    row = lax.broadcasted_iota(jnp.int32, (rows, half), 0)
    column = lax.broadcasted_iota(jnp.int32, (rows, half), 1)
    sample = (row + place_ref[0] * block) & (rows - 1)
    shard = rows // (WIDTHS * DEPTHS * CORES)
    offset = (sample // shard) ^ place_ref[1]
    pieces = WIDTHS * DEPTHS
    source = (offset // CORES + (offset & (CORES - 1)) * pieces) * shard + (sample & (shard - 1))
    near = (source == column).astype(F32).astype(BF16)
    far = (source == column + half).astype(F32).astype(BF16)
    step = 512
    for start in range(0, out_ref.shape[1], step):
        cols = slice(start, start + step)
        out_ref[:, cols] = (
            jnp.dot(near, near_ref[:, cols], preferred_element_type=F32)
            + jnp.dot(far, far_ref[:, cols], preferred_element_type=F32)
        ).astype(BF16)


def in_order(place, near, far):
    return pl.pallas_call(
        order_kernel,
        out_shape=jax.ShapeDtypeStruct((2 * near.shape[0], near.shape[1]), BF16),
        in_specs=[pl.BlockSpec(memory_space=pltpu.SMEM), whole(), whole()],
        out_specs=whole(),
        compiler_params=params(),
        cost_estimate=pl.CostEstimate(
            flops=4 * near.shape[0] ** 2 * near.shape[1] * 2,
            transcendentals=0,
            bytes_accessed=8 * near.size,
        ),
    )(place, near, far)


def product_kernel(coef_ref, weight_ref, *refs):
    count = (len(refs) - WIDTHS) // 2
    features, kernels, outs = refs[:count], refs[count : 2 * count], refs[2 * count :]
    block = coef_ref.shape[0] // WIDTHS
    for chunk in range(count):
        @pl.when(pl.program_id(0) == chunk)
        def _(chunk=chunk):
            total = jnp.dot(coef_ref[...], features[chunk][...], preferred_element_type=F32)
            total = total + jnp.dot(
                weight_ref[...], kernels[chunk][...], preferred_element_type=F32
            )
            for target, out in enumerate(outs):
                out[...] = total[target * block : (target + 1) * block].astype(out.dtype)


def products(coefs, weights, features, kernels):
    count, cands = len(features), features[0].shape[1]
    block = coefs.shape[0] // WIDTHS
    feats, obs = features[0].shape[0], kernels[0].shape[0]
    shape = (block, count * cands)
    out_shapes = (jax.ShapeDtypeStruct(shape, F32),) + (jax.ShapeDtypeStruct(shape, BF16),) * (
        WIDTHS - 1
    )
    return pl.pallas_call(
        product_kernel,
        out_shape=out_shapes,
        grid=(count,),
        in_specs=[whole(), whole()]
        + [pl.BlockSpec((feats, cands), lambda i: (0, 0))] * count
        + [pl.BlockSpec((obs, cands), lambda i: (0, 0))] * count,
        out_specs=tuple(pl.BlockSpec((block, cands), lambda i: (0, i)) for _ in out_shapes),
        compiler_params=params(40 * 2**20),
        cost_estimate=pl.CostEstimate(
            flops=2 * coefs.shape[0] * (feats + obs) * count * cands,
            transcendentals=0,
            bytes_accessed=2 * (feats + obs) * count * cands,
        ),
    )(coefs, weights, *features, *kernels)


def exchange_pairs(mask):
    devices = WIDTHS * DEPTHS * CORES
    return [(i, i ^ mask) for i in range(devices)]


def spread(piece):
    def swap(held, mask):
        return lax.ppermute(held, "cand", exchange_pairs(mask))

    held = piece
    for hop in (1, 2, 4):
        other = swap(held, hop * CORES)
        held = lax.optimization_barrier(jnp.concatenate([held, other], axis=0))
    others = [swap(held, hop * DEPTHS * CORES) for hop in range(1, WIDTHS)]
    held = lax.optimization_barrier(jnp.concatenate([held] + others, axis=0))
    return held, swap(held, 1)


def exact_dot(left, right):
    return jnp.dot(
        left, right, precision=lax.Precision.HIGHEST, preferred_element_type=jnp.float32
    )


def solve_chain(whitened, factor_rows, diag_inv):
    sections = lax.axis_size("rows")
    position = lax.axis_index("rows")
    width = diag_inv.shape[1]
    weights = jnp.zeros_like(whitened)
    carried = None
    for section in reversed(range(sections)):
        earlier = section * width

        def solve_own(carried, weights):
            remaining = whitened if carried is None else whitened - carried[:, earlier:]
            solved = exact_dot(remaining, diag_inv)
            if section == 0:
                return None, solved
            update = exact_dot(solved, factor_rows[:, :earlier])
            if carried is not None:
                update = carried[:, :earlier] + update
            return update, solved

        def pass_on(carried, weights):
            if section == 0:
                return None, weights
            shape = (whitened.shape[0], earlier)
            return (jnp.zeros(shape, jnp.float32) if carried is None else carried[:, :earlier]), weights

        carried, weights = lax.cond(position == section, solve_own, pass_on, carried, weights)
        if section > 0:
            pairs = [(section, section - 1)]
            carried = lax.ppermute(carried, "rows", pairs)
    return weights


def body(
    whitened,
    factor_rows,
    diag_inv,
    observed,
    inv_length,
    grid_coords,
    frequencies,
    phases,
    prior_coef,
):
    place = jnp.stack([lax.axis_index("rows"), lax.axis_index("cand")]).astype(jnp.int32)
    coef_near, coef_far = spread(prior_coef)
    weights = solve_chain(whitened, factor_rows, diag_inv).astype(BF16)
    weight_near, weight_far = spread(weights)
    turns, exponent, levels = prepare(frequencies, phases, observed, inv_length, grid_coords)
    made = [tiles(turns, exponent, levels, chunk) for chunk in range(CHUNKS)]
    coefs = in_order(place, coef_near, coef_far)
    solved = in_order(place, weight_near, weight_far)
    rows = lax.axis_size("rows")
    each = CHUNKS // PARTS
    sums = []
    for part in range(PARTS):
        mine = made[part * each : (part + 1) * each]
        own, *away = products(coefs, solved, [m[0] for m in mine], [m[1] for m in mine])
        total = own
        for shift, block in enumerate(away, 1):
            pairs = [(i, (i + shift) % rows) for i in range(rows)]
            total = total + lax.ppermute(block, "rows", pairs).astype(F32)
        sums.append(total)
    return jnp.concatenate(sums, axis=1).T


def solution(mesh):
    in_specs = (
        P("cand", "rows"),
        P("rows", None),
        P("rows", None),
        P(None, "rows"),
        P(),
        P(None, "cand"),
        P(None, "rows"),
        P("rows"),
        P("cand", "rows"),
    )
    out_specs = P("cand", "rows")

    return jax.shard_map(body, mesh=mesh, in_specs=in_specs, out_specs=out_specs, check_vma=False)
```

time: 328 us -> 123 us (0.38)
  matrix products: 149 us -> 2.45 us
  blocking collectives: 48.9 us -> 0 us
  other arithmetic: 46.4 us -> 2.88 us
  starting transfers between devices: 4.21 us -> 43.4 us
  Pallas kernels: 0 us -> 29.1 us
  waiting for transfers between devices: 57.3 us -> 43.7 us
  between operations: 13.6 us -> 0.28 us
  local copies, waits for them, and re-layouts: 7.82 us -> 0.73 us
    dot_general x4 -> x1, matrix products: 149 us -> 2.45 us  [exact_dot(): jnp.dot(left, right, precision=lax.Precision.HIGHEST, preferred_element_t...]
    reduce_scatter x1 -> x0, waiting for transfers between devices: 56.5 us -> none  [body(): return lax.psum_scatter(summed, 'rows', scatter_dimension=1, tiled=True)]
    all_gather x1 -> x0, blocking collectives: 48.9 us -> none  [body(): lax.all_gather(solve_chain(whitened, factor_rows, diag_inv).astype(jnp.bf...]
    dot_general x1 -> x0, other arithmetic: 44.7 us -> none  [cross_part(): lax.dot_general(kernel_tile, weights_wire, (((1,), (1,)), ((), ())), pref...]
    ppermute x3 -> x23, waiting for transfers between devices: 0.01 us -> 43.7 us  [the longest x3 19.4 us: solve_chain(): carried = lax.ppermute(carried, 'rows', pairs)]
    ppermute x3 -> x23, starting transfers between devices: 4.17 us -> 43.4 us  [the longest x14 33.4 us: swap(): return lax.ppermute(held, 'cand', exchange_pairs(mask))]
    pallas_call x0 -> x13, Pallas kernels: none -> 29.1 us  [the longest x8 19 us: tiles(): pl.pallas_call(tile_kernel, out_shape=(jax.ShapeDtypeStruct((feats, cands...]
    slice x6 -> x2, local copies, waits for them, and re-layouts: 5.77 us -> 0.01 us  [pass_on(): carried[:, :earlier]]
  transfers between devices with their start and end apart: 5 -> 23, of which waited for: 1 -> 10; matrix products, arithmetic and copies ran while one was open for 26% -> 3% of each run, Pallas kernels for 0% -> 20%
where the time goes in v1:
time: 123 us
  waiting for transfers between devices  43.7 us (36%)
  starting transfers between devices  43.4 us (35%)
  Pallas kernels  29.1 us (24%)
  other arithmetic  2.88 us (2%)
  matrix products  2.45 us (2%)
    ppermute x14, starting transfers between devices, swap(): return lax.ppermute(held, 'cand', exchange_pairs(mask))  33.4 us
    ppermute x3, waiting for transfers between devices, solve_chain(): carried = lax.ppermute(carried, 'rows', pairs)  19.4 us
    pallas_call x8, Pallas kernels, tiles(): pl.pallas_call(tile_kernel, out_shape=(jax.ShapeDtypeStruct((feats, cands...  19 us
    ppermute x14, waiting for transfers between devices, swap(): return lax.ppermute(held, 'cand', exchange_pairs(mask))  14.3 us
    ppermute x6, waiting for transfers between devices, body(): total = total + lax.ppermute(block, 'rows', pairs).astype(F32)  10 us
    ppermute x6, starting transfers between devices, body(): total = total + lax.ppermute(block, 'rows', pairs).astype(F32)  7.25 us
    pallas_call x2, Pallas kernels, products(): pl.pallas_call(product_kernel, out_shape=out_shapes, grid=(count,), in_sp...  7.16 us
    ppermute x3, starting transfers between devices, solve_chain(): carried = lax.ppermute(carried, 'rows', pairs)  2.74 us
  transfers between devices with their start and end apart: 23, of which 10 were waited for; matrix products, arithmetic and copies ran while one was open for 3% of the time, Pallas kernels for 20%

profile of v1, /device:TPU:1, one launch (start us, length us, event | category | flops | bytes accessed | tf_op | source)
XLA Modules:
  0.0 122.6 jit_solution(10435423062405988055)
XLA Ops:
  0.0 2.5 %collective-permute-start = (bf16[4,2048]{1,0:T(4,128)(2,1)}, bf16[4,2048]{1,0:T(4,128)(2,1)S(1)}, u32[]{:S(2)}, u32[]{:S(2)}) collective-permute-start(bf16[4,2048]{1,0:T(4,128)(2,1)} %param.25), channel_id=1, source_target_pairs={{0,2},{1,3},{2,0},{3,1},{4,6},{5,7},{6,4},{7,5},{8,10},{9,11},{10,... | collective-permute-start | bytes 49160 | tf_op jit(solution)/shard_map/ppermute | solution.py:237
  2.5 1.3 %collective-permute-done = bf16[4,2048]{1,0:T(4,128)(2,1)S(1)} collective-permute-done((bf16[4,2048]{1,0:T(4,128)(2,1)}, bf16[4,2048]{1,0:T(4,128)(2,1)S(1)}, u32[]{:S(2)}, u32[]{:S(2)}) %collective-permute-start) | collective-permute-done | bytes 16416 | tf_op jit(solution)/shard_map/ppermute | solution.py:237
  3.8 0.7 pad_maximum_fusion.4
  4.5 3.1 %collective-permute-start.1 = (bf16[8,2048]{1,0:T(8,128)(2,1)S(1)}, bf16[8,2048]{1,0:T(8,128)(2,1)S(1)}, u32[]{:S(2)}, u32[]{:S(2)}) collective-permute-start(bf16[8,2048]{1,0:T(8,128)(2,1)S(1)} %pad_maximum_fusion.4), channel_id=1, source_target_pairs={{0,4},{1,5},{2,6},{3,7},{4,0},{5,1},{6,2},{7,3},{8,12},{9,13},{10,... | collective-permute-start | bytes 98312 | tf_op jit(solution)/shard_map/ppermute | solution.py:237
  7.6 1.3 %collective-permute-done.1 = bf16[8,2048]{1,0:T(8,128)(2,1)S(1)} collective-permute-done((bf16[8,2048]{1,0:T(8,128)(2,1)S(1)}, bf16[8,2048]{1,0:T(8,128)(2,1)S(1)}, u32[]{:S(2)}, u32[]{:S(2)}) %collective-permute-start.1) | collective-permute-done | bytes 32800 | tf_op jit(solution)/shard_map/ppermute | solution.py:237
  8.9 6.1 %collective-permute-start.2 = (bf16[16,2048]{1,0:T(8,128)(2,1)S(1)}, bf16[16,2048]{1,0:T(8,128)(2,1)S(1)}, u32[]{:S(2)}, u32[]{:S(2)}) collective-permute-start(bf16[16,2048]{1,0:T(8,128)(2,1)S(1)} %pad_maximum_fusion.3), channel_id=1, source_target_pairs={{0,8},{1,9},{2,10},{3,11},{4,12},{5,13},{6,14},{7,15},{8,0},{9,1},... | collective-permute-start | bytes 196616 | tf_op jit(solution)/shard_map/ppermute | solution.py:237
  15.0 0.6 conditional.4
  15.0 0.6 broadcast_in_dim.6
  15.6 0.7 collective-permute-start.7
  16.3 0.7 collective-permute-start.8
  17.0 2.6 %collective-permute-start.5 = (bf16[32,2048]{1,0:T(8,128)(2,1)S(1)}, bf16[32,2048]{1,0:T(8,128)(2,1)S(1)}, u32[]{:S(2)}, u32[]{:S(2)}) collective-permute-start(bf16[32,2048]{1,0:T(8,128)(2,1)S(1)} %pad_maximum_fusion.1), channel_id=1, source_target_pairs={{0,48},{1,49},{2,50},{3,51},{4,52},{5,53},{6,54},{7,55},{8,56},{9,... | collective-permute-start | bytes 393224 | tf_op jit(solution)/shard_map/ppermute | solution.py:237
  19.6 0.5 collective-permute-start.4
  20.4 1.4 %collective-permute-start.9 = (f32[4,512]{1,0:T(4,128)S(1)}, f32[4,512]{1,0:T(4,128)S(1)}, u32[]{:S(2)}, u32[]{:S(2)}) collective-permute-start(f32[4,512]{1,0:T(4,128)S(1)} %get-tuple-element.107), channel_id=1, source_target_pairs={{64,0},{65,1},{66,2},{67,3},{68,4},{69,5},{70,6},{71,7},{72,8},{73... | collective-permute-start | bytes 24584 | tf_op jit(solution)/shard_map/ppermute | solution.py:282
  21.9 19.4 %collective-permute-done.9 = f32[4,512]{1,0:T(4,128)S(1)} collective-permute-done((f32[4,512]{1,0:T(4,128)S(1)}, f32[4,512]{1,0:T(4,128)S(1)}, u32[]{:S(2)}, u32[]{:S(2)}) %collective-permute-start.9) | collective-permute-done | bytes 8224 | tf_op jit(solution)/shard_map/ppermute | solution.py:282
  41.3 2.5 %conditional.7 = (f32[4,512]{1,0:T(4,128)}) conditional(s32[]{:T(128)} %convert_element_type.39, f32[4,512]{1,0:T(4,128)} %get-tuple-element.106, (f32[4,512]{1,0:T(4,128)}, f32[4,512]{1,0:T(4,128)S(1)}, f32[512,512]{1,0:T(8,128)}) %tuple.51), branch_computations={%region_6.0_spmd, %region_7.0_spmd} | conditional | flops 12584960 | bytes 1073160 | solution.py:279
  41.3 2.4 %fusion.14 = f32[4,512]{1,0:T(4,128)} fusion(f32[512,512]{1,0:T(8,128)} %get-tuple-element.68, f32[4,512]{1,0:T(4,128)} %get-tuple-element.66, f32[4,512]{1,0:T(4,128)S(1)} %get-tuple-element.67), kind=kOutput, calls=%fused_computation.13 | convolution fusion | flops 12584960 | bytes 1073152 | tf_op jit(solution)/shard_map/cond/branch_1_fun/dot_general | solution.py:249
  43.7 0.7 convert_element_type.43
  44.4 0.7 collective-permute-start.10
  45.2 1.7 %collective-permute-done.10 = bf16[4,512]{1,0:T(4,128)(2,1)S(1)} collective-permute-done((bf16[4,512]{1,0:T(4,128)(2,1)S(1)}, bf16[4,512]{1,0:T(4,128)(2,1)S(1)}, u32[]{:S(2)}, u32[]{:S(2)}) %collective-permute-start.10) | collective-permute-done | bytes 4128 | tf_op jit(solution)/shard_map/ppermute | solution.py:237
  46.9 1.3 %collective-permute-start.11 = (bf16[8,512]{1,0:T(8,128)(2,1)S(1)}, bf16[8,512]{1,0:T(8,128)(2,1)S(1)}, u32[]{:S(2)}, u32[]{:S(2)}) collective-permute-start(bf16[8,512]{1,0:T(8,128)(2,1)S(1)} %pad_maximum_fusion.7), channel_id=1, source_target_pairs={{0,4},{1,5},{2,6},{3,7},{4,0},{5,1},{6,2},{7,3},{8,12},{9,13},{10,... | collective-permute-start | bytes 24584 | tf_op jit(solution)/shard_map/ppermute | solution.py:237
  48.3 7.5 %collective-permute-start.6 = (bf16[128,2048]{1,0:T(8,128)(2,1)S(1)}, bf16[128,2048]{1,0:T(8,128)(2,1)S(1)}, u32[]{:S(2)}, u32[]{:S(2)}) collective-permute-start(bf16[128,2048]{1,0:T(8,128)(2,1)S(1)} %pad_maximum_fusion.near_ref), channel_id=1, source_target_pairs={{0,1},{1,0},{2,3},{3,2},{4,5},{5,4},{6,7},{7,6},{8,9},{9,8},{10,11... | collective-permute-start | bytes 1572872 | tf_op jit(solution)/shard_map/ppermute | solution.py:237
  55.9 6.4 %collective-permute-done.12 = bf16[16,512]{1,0:T(8,128)(2,1)S(1)} collective-permute-done((bf16[16,512]{1,0:T(8,128)(2,1)S(1)}, bf16[16,512]{1,0:T(8,128)(2,1)S(1)}, u32[]{:S(2)}, u32[]{:S(2)}) %collective-permute-start.12) | collective-permute-done | bytes 16416 | tf_op jit(solution)/shard_map/ppermute | solution.py:237
  62.3 2.5 %collective-permute-start.15 = (bf16[32,512]{1,0:T(8,128)(2,1)S(1)}, bf16[32,512]{1,0:T(8,128)(2,1)S(1)}, u32[]{:S(2)}, u32[]{:S(2)}) collective-permute-start(bf16[32,512]{1,0:T(8,128)(2,1)S(1)} %pad_maximum_fusion.5), channel_id=1, source_target_pairs={{0,48},{1,49},{2,50},{3,51},{4,52},{5,53},{6,54},{7,55},{8,56},{9,... | collective-permute-start | bytes 98312 | tf_op jit(solution)/shard_map/ppermute | solution.py:237
  64.8 0.5 collective-permute-start.14
  65.6 0.7 collective-permute-done.15
  66.3 2.8 %collective-permute-done.14 = bf16[32,512]{1,0:T(8,128)(2,1)S(1)} collective-permute-done((bf16[32,512]{1,0:T(8,128)(2,1)S(1)}, bf16[32,512]{1,0:T(8,128)(2,1)S(1)}, u32[]{:S(2)}, u32[]{:S(2)}) %collective-permute-start.14) | collective-permute-done | bytes 32800 | tf_op jit(solution)/shard_map/ppermute | solution.py:237
  69.1 5.5 %collective-permute-start.16 = (bf16[128,512]{1,0:T(8,128)(2,1)S(1)}, bf16[128,512]{1,0:T(8,128)(2,1)S(1)}, u32[]{:S(2)}, u32[]{:S(2)}) collective-permute-start(bf16[128,512]{1,0:T(8,128)(2,1)S(1)} %pad_maximum_fusion.2.near_ref), channel_id=1, source_target_pairs={{0,1},{1,0},{2,3},{3,2},{4,5},{5,4},{6,7},{7,6},{8,9},{9,8},{10,11... | collective-permute-start | bytes 393224 | tf_op jit(solution)/shard_map/ppermute | solution.py:237
  74.7 0.6 prepare.1
  75.3 2.4 %shard_map.101 = (bf16[2048,512]{1,0:T(8,128)(2,1)S(1)}, bf16[512,512]{1,0:T(8,128)(2,1)S(1)}) custom-call(bf16[2048,128]{1,0:T(8,128)(2,1)S(1)} %get-tuple-element.108.turns_ref, bf16[512,128]{1,0:T(8,128)(2,1)S(1)} %get-tuple-element.109.exponent_ref, bf16[128,4096]{1,0:T(8,128)(2,1)S(1)} %get-tuple-element.110.levels_ref), custom_call_target="tpu_custom_call" | custom-call | flops 31457280 | bytes 2621440 | tf_op jit(solution)/shard_map/pallas_call | solution.py:129
  77.7 2.4 %shard_map.100 = (bf16[2048,512]{1,0:T(8,128)(2,1)S(1)}, bf16[512,512]{1,0:T(8,128)(2,1)S(1)}) custom-call(bf16[2048,128]{1,0:T(8,128)(2,1)S(1)} %get-tuple-element.108.turns_ref, bf16[512,128]{1,0:T(8,128)(2,1)S(1)} %get-tuple-element.109.exponent_ref, bf16[128,4096]{1,0:T(8,128)(2,1)S(1)} %get-tuple-element.110.levels_ref), custom_call_target="tpu_custom_call" | custom-call | flops 31457280 | bytes 2621440 | tf_op jit(solution)/shard_map/pallas_call | solution.py:129
  80.1 2.4 %shard_map.99 = (bf16[2048,512]{1,0:T(8,128)(2,1)S(1)}, bf16[512,512]{1,0:T(8,128)(2,1)S(1)}) custom-call(bf16[2048,128]{1,0:T(8,128)(2,1)S(1)} %get-tuple-element.108.turns_ref, bf16[512,128]{1,0:T(8,128)(2,1)S(1)} %get-tuple-element.109.exponent_ref, bf16[128,4096]{1,0:T(8,128)(2,1)S(1)} %get-tuple-element.110.levels_ref), custom_call_target="tpu_custom_call" | custom-call | flops 31457280 | bytes 2621440 | tf_op jit(solution)/shard_map/pallas_call | solution.py:129
  82.5 2.4 %shard_map.98 = (bf16[2048,512]{1,0:T(8,128)(2,1)S(1)}, bf16[512,512]{1,0:T(8,128)(2,1)S(1)}) custom-call(bf16[2048,128]{1,0:T(8,128)(2,1)S(1)} %get-tuple-element.108.turns_ref, bf16[512,128]{1,0:T(8,128)(2,1)S(1)} %get-tuple-element.109.exponent_ref, bf16[128,4096]{1,0:T(8,128)(2,1)S(1)} %get-tuple-element.110.levels_ref), custom_call_target="tpu_custom_call" | custom-call | flops 31457280 | bytes 2621440 | tf_op jit(solution)/shard_map/pallas_call | solution.py:129
  84.9 0.9 shard_map.92.weight_ref
  85.9 1.4 %shard_map.91.coef_ref = bf16[256,2048]{1,0:T(8,128)(2,1)S(1)} custom-call(s32[2]{0:T(128)S(1)} %pad_add_fusion.place_ref, bf16[128,2048]{1,0:T(8,128)(2,1)S(1)} %pad_maximum_fusion.near_ref, bf16[128,2048]{1,0:T(8,128)(2,1)S(1)} %collective-permute-done.6.far_ref), custom_call_target="tpu_custom_call" | custom-call | flops 268435456 | bytes 2097152 | tf_op jit(solution)/shard_map/pallas_call | solution.py:176
  87.3 3.6 %shard_map.102 = (f32[64,2048]{1,0:T(8,128)S(1)}, bf16[64,2048]{1,0:T(8,128)(2,1)S(1)}, bf16[64,2048]{1,0:T(8,128)(2,1)S(1)}, bf16[64,2048]{1,0:T(8,128)(2,1)S(1)}) custom-call(bf16[256,2048]{1,0:T(8,128)(2,1)S(1)} %shard_map.91.coef_ref, bf16[256,512]{1,0:T(8,128)(2,1)S(1)} %shard_map.92.weight_ref, bf16[2048,512]{1,0:T(8,128)(2,1)S(1)} %get-tuple-element.123.refs_0_, ...), custom_call_target="tpu_custom_call" | custom-call | flops 2684354560 | bytes 10485760 | tf_op jit(solution)/shard_map/pallas_call | solution.py:213
  91.0 2.6 %collective-permute-start.22 = (bf16[64,2048]{1,0:T(8,128)(2,1)S(1)}, bf16[64,2048]{1,0:T(8,128)(2,1)S(1)}, u32[]{:S(2)}, u32[]{:S(2)}) collective-permute-start(bf16[64,2048]{1,0:T(8,128)(2,1)S(1)} %get-tuple-element.134), channel_id=1, source_target_pairs={{0,192},{64,0},{128,64},{192,128},{1,193},{65,1},{129,65},{193,129... | collective-permute-start | bytes 786440 | tf_op jit(solution)/shard_map/ppermute | solution.py:314
  93.6 2.4 %shard_map.96 = (bf16[2048,512]{1,0:T(8,128)(2,1)S(1)}, bf16[512,512]{1,0:T(8,128)(2,1)S(1)}) custom-call(bf16[2048,128]{1,0:T(8,128)(2,1)S(1)} %get-tuple-element.108.turns_ref, bf16[512,128]{1,0:T(8,128)(2,1)S(1)} %get-tuple-element.109.exponent_ref, bf16[128,4096]{1,0:T(8,128)(2,1)S(1)} %get-tuple-element.110.levels_ref), custom_call_target="tpu_custom_call" | custom-call | flops 31457280 | bytes 2621440 | tf_op jit(solution)/shard_map/pallas_call | solution.py:129
  96.0 2.4 %shard_map.95 = (bf16[2048,512]{1,0:T(8,128)(2,1)S(1)}, bf16[512,512]{1,0:T(8,128)(2,1)S(1)}) custom-call(bf16[2048,128]{1,0:T(8,128)(2,1)S(1)} %get-tuple-element.108.turns_ref, bf16[512,128]{1,0:T(8,128)(2,1)S(1)} %get-tuple-element.109.exponent_ref, bf16[128,4096]{1,0:T(8,128)(2,1)S(1)} %get-tuple-element.110.levels_ref), custom_call_target="tpu_custom_call" | custom-call | flops 31457280 | bytes 2621440 | tf_op jit(solution)/shard_map/pallas_call | solution.py:129
  98.4 2.4 %shard_map.94 = (bf16[2048,512]{1,0:T(8,128)(2,1)S(1)}, bf16[512,512]{1,0:T(8,128)(2,1)S(1)}) custom-call(bf16[2048,128]{1,0:T(8,128)(2,1)S(1)} %get-tuple-element.108.turns_ref, bf16[512,128]{1,0:T(8,128)(2,1)S(1)} %get-tuple-element.109.exponent_ref, bf16[128,4096]{1,0:T(8,128)(2,1)S(1)} %get-tuple-element.110.levels_ref), custom_call_target="tpu_custom_call" | custom-call | flops 31457280 | bytes 2621440 | tf_op jit(solution)/shard_map/pallas_call | solution.py:129
  100.8 2.4 %shard_map.93 = (bf16[2048,512]{1,0:T(8,128)(2,1)S(1)}, bf16[512,512]{1,0:T(8,128)(2,1)S(1)}) custom-call(bf16[2048,128]{1,0:T(8,128)(2,1)S(1)} %get-tuple-element.108.turns_ref, bf16[512,128]{1,0:T(8,128)(2,1)S(1)} %get-tuple-element.109.exponent_ref, bf16[128,4096]{1,0:T(8,128)(2,1)S(1)} %get-tuple-element.110.levels_ref), custom_call_target="tpu_custom_call" | custom-call | flops 31457280 | bytes 2621440 | tf_op jit(solution)/shard_map/pallas_call | solution.py:129
  103.1 3.6 %shard_map.97 = (f32[64,2048]{1,0:T(8,128)S(1)}, bf16[64,2048]{1,0:T(8,128)(2,1)S(1)}, bf16[64,2048]{1,0:T(8,128)(2,1)S(1)}, bf16[64,2048]{1,0:T(8,128)(2,1)S(1)}) custom-call(bf16[256,2048]{1,0:T(8,128)(2,1)S(1)} %shard_map.91.coef_ref, bf16[256,512]{1,0:T(8,128)(2,1)S(1)} %shard_map.92.weight_ref, bf16[2048,512]{1,0:T(8,128)(2,1)S(1)} %get-tuple-element.111.refs_0_, ...), custom_call_target="tpu_custom_call" | custom-call | flops 2684354560 | bytes 10485760 | tf_op jit(solution)/shard_map/pallas_call | solution.py:213
  106.7 0.7 collective-permute-start.17
  107.4 1.9 %collective-permute-start.18 = (bf16[64,2048]{1,0:T(8,128)(2,1)S(1)}, bf16[64,2048]{1,0:T(8,128)(2,1)S(1)}, u32[]{:S(2)}, u32[]{:S(2)}) collective-permute-start(bf16[64,2048]{1,0:T(8,128)(2,1)S(1)} %get-tuple-element.121), channel_id=1, source_target_pairs={{0,128},{64,192},{128,0},{192,64},{1,129},{65,193},{129,1},{193,65... | collective-permute-start | bytes 786440 | tf_op jit(solution)/shard_map/ppermute | solution.py:314
  109.3 2.0 %collective-permute-start.19 = (bf16[64,2048]{1,0:T(8,128)(2,1)S(1)}, bf16[64,2048]{1,0:T(8,128)(2,1)S(1)}, u32[]{:S(2)}, u32[]{:S(2)}) collective-permute-start(bf16[64,2048]{1,0:T(8,128)(2,1)S(1)} %get-tuple-element.122), channel_id=1, source_target_pairs={{0,192},{64,0},{128,64},{192,128},{1,193},{65,1},{129,65},{193,129... | collective-permute-start | bytes 786440 | tf_op jit(solution)/shard_map/ppermute | solution.py:314
  111.4 4.2 %collective-permute-done.17 = bf16[64,2048]{1,0:T(8,128)(2,1)S(1)} collective-permute-done((bf16[64,2048]{1,0:T(8,128)(2,1)S(1)}, bf16[64,2048]{1,0:T(8,128)(2,1)S(1)}, u32[]{:S(2)}, u32[]{:S(2)}) %collective-permute-start.17) | collective-permute-done | bytes 262176 | tf_op jit(solution)/shard_map/ppermute | solution.py:314
  115.6 5.0 %collective-permute-done.18 = bf16[64,2048]{1,0:T(8,128)(2,1)S(1)} collective-permute-done((bf16[64,2048]{1,0:T(8,128)(2,1)S(1)}, bf16[64,2048]{1,0:T(8,128)(2,1)S(1)}, u32[]{:S(2)}, u32[]{:S(2)}) %collective-permute-start.18) | collective-permute-done | bytes 262176 | tf_op jit(solution)/shard_map/ppermute | solution.py:314
  120.7 0.8 collective-permute-done.19
  121.5 1.0 maximum_bitcast_fusion
  (44 shorter events, 1.4 us)
Async XLA Ops:
  0.0 3.8 %collective-permute-start = (bf16[4,2048]{1,0:T(4,128)(2,1)}, bf16[4,2048]{1,0:T(4,128)(2,1)S(1)}, u32[]{:S(2)}, u32[]{:S(2)}) collective-permute-start(bf16[4,2048]{1,0:T(4,128)(2,1)} %param.25), channel_id=1, source_target_pairs={{0,2},{1,3},{2,0},{3,1},{4,6},{5,7},{6,4},{7,5},{8,10},{9,11},{10,... | collective-permute-start | bytes 49160 | tf_op jit(solution)/shard_map/ppermute | solution.py:237
  4.5 4.4 %collective-permute-start.1 = (bf16[8,2048]{1,0:T(8,128)(2,1)S(1)}, bf16[8,2048]{1,0:T(8,128)(2,1)S(1)}, u32[]{:S(2)}, u32[]{:S(2)}) collective-permute-start(bf16[8,2048]{1,0:T(8,128)(2,1)S(1)} %pad_maximum_fusion.4), channel_id=1, source_target_pairs={{0,4},{1,5},{2,6},{3,7},{4,0},{5,1},{6,2},{7,3},{8,12},{9,13},{10,... | collective-permute-start | bytes 98312 | tf_op jit(solution)/shard_map/ppermute | solution.py:237
  8.9 8.1 %collective-permute-start.2 = (bf16[16,2048]{1,0:T(8,128)(2,1)S(1)}, bf16[16,2048]{1,0:T(8,128)(2,1)S(1)}, u32[]{:S(2)}, u32[]{:S(2)}) collective-permute-start(bf16[16,2048]{1,0:T(8,128)(2,1)S(1)} %pad_maximum_fusion.3), channel_id=1, source_target_pairs={{0,8},{1,9},{2,10},{3,11},{4,12},{5,13},{6,14},{7,15},{8,0},{9,1},... | collective-permute-start | bytes 196616 | tf_op jit(solution)/shard_map/ppermute | solution.py:237
  15.6 0.7 collective-permute-start.7
  16.3 4.0 %collective-permute-start.8 = (f32[4,1024]{1,0:T(4,128)S(1)}, f32[4,1024]{1,0:T(4,128)S(1)}, u32[]{:S(2)}, u32[]{:S(2)}) collective-permute-start(f32[4,1024]{1,0:T(4,128)S(1)} %get-tuple-element.104), channel_id=1, source_target_pairs={{128,64},{129,65},{130,66},{131,67},{132,68},{133,69},{134,70},{13... | collective-permute-start | bytes 49160 | tf_op jit(solution)/shard_map/ppermute | solution.py:282
  17.0 31.2 %collective-permute-start.5 = (bf16[32,2048]{1,0:T(8,128)(2,1)S(1)}, bf16[32,2048]{1,0:T(8,128)(2,1)S(1)}, u32[]{:S(2)}, u32[]{:S(2)}) collective-permute-start(bf16[32,2048]{1,0:T(8,128)(2,1)S(1)} %pad_maximum_fusion.1), channel_id=1, source_target_pairs={{0,48},{1,49},{2,50},{3,51},{4,52},{5,53},{6,54},{7,55},{8,56},{9,... | collective-permute-start | bytes 393224 | tf_op jit(solution)/shard_map/ppermute | solution.py:237
  19.6 28.6 %collective-permute-start.4 = (bf16[32,2048]{1,0:T(8,128)(2,1)S(1)}, bf16[32,2048]{1,0:T(8,128)(2,1)S(1)}, u32[]{:S(2)}, u32[]{:S(2)}) collective-permute-start(bf16[32,2048]{1,0:T(8,128)(2,1)S(1)} %pad_maximum_fusion.1), channel_id=1, source_target_pairs={{0,32},{1,33},{2,34},{3,35},{4,36},{5,37},{6,38},{7,39},{8,40},{9,... | collective-permute-start | bytes 393224 | tf_op jit(solution)/shard_map/ppermute | solution.py:237
  20.1 28.1 %collective-permute-start.3 = (bf16[32,2048]{1,0:T(8,128)(2,1)S(1)}, bf16[32,2048]{1,0:T(8,128)(2,1)S(1)}, u32[]{:S(2)}, u32[]{:S(2)}) collective-permute-start(bf16[32,2048]{1,0:T(8,128)(2,1)S(1)} %pad_maximum_fusion.1), channel_id=1, source_target_pairs={{0,16},{1,17},{2,18},{3,19},{4,20},{5,21},{6,22},{7,23},{8,24},{9,... | collective-permute-start | bytes 393224 | tf_op jit(solution)/shard_map/ppermute | solution.py:237
  20.4 54.2 %copy-start.4 = (f32[22]{0:T(128)S(1)}, f32[22]{0:T(128)}, u32[]{:S(2)}) copy-start(f32[22]{0:T(128)} %param.21) | copy-start | bytes 268
  20.4 54.3 %copy-start = (s32[22,4096]{1,0:T(8,128)S(1)}, s32[22,4096]{1,0:T(8,128)}, u32[]{:S(2)}) copy-start(s32[22,4096]{1,0:T(8,128)} %grid_ref.1) | copy-start | bytes 1081348
  20.4 54.3 %copy-start.1 = (f32[22,2048]{1,0:T(8,128)S(1)}, f32[22,2048]{1,0:T(8,128)}, u32[]{:S(2)}) copy-start(f32[22,2048]{1,0:T(8,128)} %freq_ref.1) | copy-start | bytes 540676
  20.4 54.3 %copy-start.2 = (f32[22,512]{1,0:T(8,128)S(1)}, f32[22,512]{1,0:T(8,128)}, u32[]{:S(2)}) copy-start(f32[22,512]{1,0:T(8,128)} %observed_ref.1) | copy-start | bytes 135172
  20.4 54.3 %copy-start.3 = (f32[2048]{0:T(1024)S(1)}, f32[2048]{0:T(1024)}, u32[]{:S(2)}) copy-start(f32[2048]{0:T(1024)} %param.24) | copy-start | bytes 24580
  20.4 20.8 %collective-permute-start.9 = (f32[4,512]{1,0:T(4,128)S(1)}, f32[4,512]{1,0:T(4,128)S(1)}, u32[]{:S(2)}, u32[]{:S(2)}) collective-permute-start(f32[4,512]{1,0:T(4,128)S(1)} %get-tuple-element.107), channel_id=1, source_target_pairs={{64,0},{65,1},{66,2},{67,3},{68,4},{69,5},{70,6},{71,7},{72,8},{73... | collective-permute-start | bytes 24584 | tf_op jit(solution)/shard_map/ppermute | solution.py:282
  44.4 2.5 %collective-permute-start.10 = (bf16[4,512]{1,0:T(4,128)(2,1)S(1)}, bf16[4,512]{1,0:T(4,128)(2,1)S(1)}, u32[]{:S(2)}, u32[]{:S(2)}) collective-permute-start(bf16[4,512]{1,0:T(4,128)(2,1)S(1)} %convert_element_type.43), channel_id=1, source_target_pairs={{0,2},{1,3},{2,0},{3,1},{4,6},{5,7},{6,4},{7,5},{8,10},{9,11},{10,... | collective-permute-start | bytes 12296 | tf_op jit(solution)/shard_map/ppermute | solution.py:237
  46.9 8.9 %collective-permute-start.11 = (bf16[8,512]{1,0:T(8,128)(2,1)S(1)}, bf16[8,512]{1,0:T(8,128)(2,1)S(1)}, u32[]{:S(2)}, u32[]{:S(2)}) collective-permute-start(bf16[8,512]{1,0:T(8,128)(2,1)S(1)} %pad_maximum_fusion.7), channel_id=1, source_target_pairs={{0,4},{1,5},{2,6},{3,7},{4,0},{5,1},{6,2},{7,3},{8,12},{9,13},{10,... | collective-permute-start | bytes 24584 | tf_op jit(solution)/shard_map/ppermute | solution.py:237
  48.3 37.6 %collective-permute-start.6 = (bf16[128,2048]{1,0:T(8,128)(2,1)S(1)}, bf16[128,2048]{1,0:T(8,128)(2,1)S(1)}, u32[]{:S(2)}, u32[]{:S(2)}) collective-permute-start(bf16[128,2048]{1,0:T(8,128)(2,1)S(1)} %pad_maximum_fusion.near_ref), channel_id=1, source_target_pairs={{0,1},{1,0},{2,3},{3,2},{4,5},{5,4},{6,7},{7,6},{8,9},{9,8},{10,11... | collective-permute-start | bytes 1572872 | tf_op jit(solution)/shard_map/ppermute | solution.py:237
  55.8 6.5 %collective-permute-start.12 = (bf16[16,512]{1,0:T(8,128)(2,1)S(1)}, bf16[16,512]{1,0:T(8,128)(2,1)S(1)}, u32[]{:S(2)}, u32[]{:S(2)}) collective-permute-start(bf16[16,512]{1,0:T(8,128)(2,1)S(1)} %pad_maximum_fusion.6), channel_id=1, source_target_pairs={{0,8},{1,9},{2,10},{3,11},{4,12},{5,13},{6,14},{7,15},{8,0},{9,1},... | collective-permute-start | bytes 49160 | tf_op jit(solution)/shard_map/ppermute | solution.py:237
  62.3 4.0 %collective-permute-start.15 = (bf16[32,512]{1,0:T(8,128)(2,1)S(1)}, bf16[32,512]{1,0:T(8,128)(2,1)S(1)}, u32[]{:S(2)}, u32[]{:S(2)}) collective-permute-start(bf16[32,512]{1,0:T(8,128)(2,1)S(1)} %pad_maximum_fusion.5), channel_id=1, source_target_pairs={{0,48},{1,49},{2,50},{3,51},{4,52},{5,53},{6,54},{7,55},{8,56},{9,... | collective-permute-start | bytes 98312 | tf_op jit(solution)/shard_map/ppermute | solution.py:237
  64.8 4.3 %collective-permute-start.14 = (bf16[32,512]{1,0:T(8,128)(2,1)S(1)}, bf16[32,512]{1,0:T(8,128)(2,1)S(1)}, u32[]{:S(2)}, u32[]{:S(2)}) collective-permute-start(bf16[32,512]{1,0:T(8,128)(2,1)S(1)} %pad_maximum_fusion.5), channel_id=1, source_target_pairs={{0,32},{1,33},{2,34},{3,35},{4,36},{5,37},{6,38},{7,39},{8,40},{9,... | collective-permute-start | bytes 98312 | tf_op jit(solution)/shard_map/ppermute | solution.py:237
  65.3 3.8 %collective-permute-start.13 = (bf16[32,512]{1,0:T(8,128)(2,1)S(1)}, bf16[32,512]{1,0:T(8,128)(2,1)S(1)}, u32[]{:S(2)}, u32[]{:S(2)}) collective-permute-start(bf16[32,512]{1,0:T(8,128)(2,1)S(1)} %pad_maximum_fusion.5), channel_id=1, source_target_pairs={{0,16},{1,17},{2,18},{3,19},{4,20},{5,21},{6,22},{7,23},{8,24},{9,... | collective-permute-start | bytes 98312 | tf_op jit(solution)/shard_map/ppermute | solution.py:237
  69.1 15.9 %collective-permute-start.16 = (bf16[128,512]{1,0:T(8,128)(2,1)S(1)}, bf16[128,512]{1,0:T(8,128)(2,1)S(1)}, u32[]{:S(2)}, u32[]{:S(2)}) collective-permute-start(bf16[128,512]{1,0:T(8,128)(2,1)S(1)} %pad_maximum_fusion.2.near_ref), channel_id=1, source_target_pairs={{0,1},{1,0},{2,3},{3,2},{4,5},{5,4},{6,7},{7,6},{8,9},{9,8},{10,11... | collective-permute-start | bytes 393224 | tf_op jit(solution)/shard_map/ppermute | solution.py:237
  90.9 18.4 %collective-permute-start.20 = (bf16[64,2048]{1,0:T(8,128)(2,1)S(1)}, bf16[64,2048]{1,0:T(8,128)(2,1)S(1)}, u32[]{:S(2)}, u32[]{:S(2)}) collective-permute-start(bf16[64,2048]{1,0:T(8,128)(2,1)S(1)} %get-tuple-element.132), channel_id=1, source_target_pairs={{0,64},{64,128},{128,192},{192,0},{1,65},{65,129},{129,193},{193,1... | collective-permute-start | bytes 786440 | tf_op jit(solution)/shard_map/ppermute | solution.py:314
  90.9 20.3 %collective-permute-start.21 = (bf16[64,2048]{1,0:T(8,128)(2,1)S(1)}, bf16[64,2048]{1,0:T(8,128)(2,1)S(1)}, u32[]{:S(2)}, u32[]{:S(2)}) collective-permute-start(bf16[64,2048]{1,0:T(8,128)(2,1)S(1)} %get-tuple-element.133), channel_id=1, source_target_pairs={{0,128},{64,192},{128,0},{192,64},{1,129},{65,193},{129,1},{193,65... | collective-permute-start | bytes 786440 | tf_op jit(solution)/shard_map/ppermute | solution.py:314
  91.0 20.2 %collective-permute-start.22 = (bf16[64,2048]{1,0:T(8,128)(2,1)S(1)}, bf16[64,2048]{1,0:T(8,128)(2,1)S(1)}, u32[]{:S(2)}, u32[]{:S(2)}) collective-permute-start(bf16[64,2048]{1,0:T(8,128)(2,1)S(1)} %get-tuple-element.134), channel_id=1, source_target_pairs={{0,192},{64,0},{128,64},{192,128},{1,193},{65,1},{129,65},{193,129... | collective-permute-start | bytes 786440 | tf_op jit(solution)/shard_map/ppermute | solution.py:314
  106.7 8.9 %collective-permute-start.17 = (bf16[64,2048]{1,0:T(8,128)(2,1)S(1)}, bf16[64,2048]{1,0:T(8,128)(2,1)S(1)}, u32[]{:S(2)}, u32[]{:S(2)}) collective-permute-start(bf16[64,2048]{1,0:T(8,128)(2,1)S(1)} %get-tuple-element.120), channel_id=1, source_target_pairs={{0,64},{64,128},{128,192},{192,0},{1,65},{65,129},{129,193},{193,1... | collective-permute-start | bytes 786440 | tf_op jit(solution)/shard_map/ppermute | solution.py:314
  107.4 13.3 %collective-permute-start.18 = (bf16[64,2048]{1,0:T(8,128)(2,1)S(1)}, bf16[64,2048]{1,0:T(8,128)(2,1)S(1)}, u32[]{:S(2)}, u32[]{:S(2)}) collective-permute-start(bf16[64,2048]{1,0:T(8,128)(2,1)S(1)} %get-tuple-element.121), channel_id=1, source_target_pairs={{0,128},{64,192},{128,0},{192,64},{1,129},{65,193},{129,1},{193,65... | collective-permute-start | bytes 786440 | tf_op jit(solution)/shard_map/ppermute | solution.py:314
  109.3 12.2 %collective-permute-start.19 = (bf16[64,2048]{1,0:T(8,128)(2,1)S(1)}, bf16[64,2048]{1,0:T(8,128)(2,1)S(1)}, u32[]{:S(2)}, u32[]{:S(2)}) collective-permute-start(bf16[64,2048]{1,0:T(8,128)(2,1)S(1)} %get-tuple-element.122), channel_id=1, source_target_pairs={{0,192},{64,0},{128,64},{192,128},{1,193},{65,1},{129,65},{193,129... | collective-permute-start | bytes 786440 | tf_op jit(solution)/shard_map/ppermute | solution.py:314

commit v2 on v1

--- a/solution.py
+++ b/solution.py
@@ -61,7 +61,11 @@
     )
     for start in range(0, wide.shape[1], 512):
         turns_ref[start : start + 512, :] = wide[:, start : start + 512].T.astype(BF16)
-    squares = scale_ref[...] * scale_ref[...]
+    scale = jnp.broadcast_to(scale_ref[...], (DIM, DIM))
+    line = lax.broadcasted_iota(jnp.int32, (DIM, DIM), 0)
+    lane = lax.broadcasted_iota(jnp.int32, (DIM, DIM), 1)
+    scale = jnp.sum(jnp.where(line == lane, scale, 0.0), axis=1, keepdims=True)
+    squares = scale * scale
     observed = observed_ref[...]
     ones = jnp.ones((1, narrow.shape[1]), F32)
     norm = jnp.sum(observed * observed * squares, axis=0, keepdims=True) * (-0.5 * LOG2E)
@@ -99,7 +103,7 @@
         compiler_params=params(),
         cost_estimate=pl.CostEstimate(flops=10**7, transcendentals=0, bytes_accessed=4 * 2**20),
         name="prepare",
-    )(frequencies, phases[None, :], observed, inv_length[:, None], grid_coords)
+    )(frequencies, phases[None, :], observed, inv_length[None, :], grid_coords)
 
 
 def cosine(turns):
@@ -151,55 +155,80 @@
     )(turns, exponent, levels)
 
 
-def order_kernel(place_ref, near_ref, far_ref, out_ref):
-    rows, half = out_ref.shape[0], near_ref.shape[0]
+def choice_kernel(place_ref, out_ref):
+    rows = out_ref.shape[0]
     block = rows // WIDTHS
-    row = lax.broadcasted_iota(jnp.int32, (rows, half), 0)
-    column = lax.broadcasted_iota(jnp.int32, (rows, half), 1)
+    row = lax.broadcasted_iota(jnp.int32, (rows, rows), 0)
+    column = lax.broadcasted_iota(jnp.int32, (rows, rows), 1)
     sample = (row + place_ref[0] * block) & (rows - 1)
     shard = rows // (WIDTHS * DEPTHS * CORES)
-    offset = (sample // shard) ^ place_ref[1]
-    pieces = WIDTHS * DEPTHS
-    source = (offset // CORES + (offset & (CORES - 1)) * pieces) * shard + (sample & (shard - 1))
-    near = (source == column).astype(F32).astype(BF16)
-    far = (source == column + half).astype(F32).astype(BF16)
-    step = 512
-    for start in range(0, out_ref.shape[1], step):
-        cols = slice(start, start + step)
-        out_ref[:, cols] = (
-            jnp.dot(near, near_ref[:, cols], preferred_element_type=F32)
-            + jnp.dot(far, far_ref[:, cols], preferred_element_type=F32)
+    owner, mine = sample // shard, place_ref[1]
+    side = (owner ^ mine) & (CORES - 1)
+    depth = (mine // CORES - owner // CORES) & (DEPTHS - 1)
+    width = (owner ^ mine) // (DEPTHS * CORES)
+    source = ((side * WIDTHS + width) * DEPTHS + depth) * shard + (sample & (shard - 1))
+    out_ref[...] = (source == column).astype(F32).astype(BF16)
+
+
+def choice(place, rows):
+    return pl.pallas_call(
+        choice_kernel,
+        out_shape=jax.ShapeDtypeStruct((rows, rows), BF16),
+        in_specs=[pl.BlockSpec(memory_space=pltpu.SMEM)],
+        out_specs=whole(),
+        compiler_params=params(),
+        cost_estimate=pl.CostEstimate(
+            flops=20 * rows * rows, transcendentals=0, bytes_accessed=2 * rows * rows
+        ),
+        name="choice",
+    )(place)
+
+
+def order_kernel(chosen_ref, *refs):
+    *sets, out_ref = refs
+
+    @pl.loop(0, out_ref.shape[1] // CAND_TILE)
+    def _(tile):
+        cols = pl.ds(pl.multiple_of(tile * CAND_TILE, CAND_TILE), CAND_TILE)
+        lines = jnp.concatenate([held[:, cols] for held in sets], axis=0)
+        out_ref[:, cols] = jnp.dot(
+            chosen_ref[...], lines, preferred_element_type=F32
         ).astype(BF16)
 
 
-def in_order(place, near, far):
+def in_order(chosen, sets):
+    rows, columns = len(sets) * sets[0].shape[0], sets[0].shape[1]
     return pl.pallas_call(
         order_kernel,
-        out_shape=jax.ShapeDtypeStruct((2 * near.shape[0], near.shape[1]), BF16),
-        in_specs=[pl.BlockSpec(memory_space=pltpu.SMEM), whole(), whole()],
+        out_shape=jax.ShapeDtypeStruct((rows, columns), BF16),
+        in_specs=[whole()] * (1 + len(sets)),
         out_specs=whole(),
         compiler_params=params(),
         cost_estimate=pl.CostEstimate(
-            flops=4 * near.shape[0] ** 2 * near.shape[1] * 2,
-            transcendentals=0,
-            bytes_accessed=8 * near.size,
-        ),
-    )(place, near, far)
+            flops=2 * rows * rows * columns, transcendentals=0, bytes_accessed=4 * rows * columns
+        ),
+    )(chosen, *sets)
 
 
 def product_kernel(coef_ref, weight_ref, *refs):
     count = (len(refs) - WIDTHS) // 2
     features, kernels, outs = refs[:count], refs[count : 2 * count], refs[2 * count :]
     block = coef_ref.shape[0] // WIDTHS
+    cands = features[0].shape[1]
     for chunk in range(count):
-        @pl.when(pl.program_id(0) == chunk)
-        def _(chunk=chunk):
-            total = jnp.dot(coef_ref[...], features[chunk][...], preferred_element_type=F32)
+        @pl.loop(0, cands // CAND_TILE)
+        def _(tile, chunk=chunk):
+            cols = pl.ds(pl.multiple_of(tile * CAND_TILE, CAND_TILE), CAND_TILE)
+            total = jnp.dot(coef_ref[...], features[chunk][:, cols], preferred_element_type=F32)
             total = total + jnp.dot(
-                weight_ref[...], kernels[chunk][...], preferred_element_type=F32
+                weight_ref[...], kernels[chunk][:, cols], preferred_element_type=F32
+            )
+            place = pl.ds(
+                pl.multiple_of(chunk * cands + tile * CAND_TILE, CAND_TILE), CAND_TILE
             )
             for target, out in enumerate(outs):
-                out[...] = total[target * block : (target + 1) * block].astype(out.dtype)
+                rows = slice(target * block, (target + 1) * block)
+                out[:, place] = total[rows].astype(out.dtype)
 
 
 def products(coefs, weights, features, kernels):
@@ -213,12 +242,9 @@
     return pl.pallas_call(
         product_kernel,
         out_shape=out_shapes,
-        grid=(count,),
-        in_specs=[whole(), whole()]
-        + [pl.BlockSpec((feats, cands), lambda i: (0, 0))] * count
-        + [pl.BlockSpec((obs, cands), lambda i: (0, 0))] * count,
-        out_specs=tuple(pl.BlockSpec((block, cands), lambda i: (0, i)) for _ in out_shapes),
-        compiler_params=params(40 * 2**20),
+        in_specs=[whole()] * (2 + 2 * count),
+        out_specs=(whole(),) * WIDTHS,
+        compiler_params=params(),
         cost_estimate=pl.CostEstimate(
             flops=2 * coefs.shape[0] * (feats + obs) * count * cands,
             transcendentals=0,
@@ -232,54 +258,165 @@
     return [(i, i ^ mask) for i in range(devices)]
 
 
+def ring_pairs(step):
+    line = DEPTHS * CORES
+    return [
+        (i, i // line * line + (i + step * CORES) % line) for i in range(WIDTHS * line)
+    ]
+
+
+def stack_kernel(*refs):
+    *pieces, out_ref, rows = refs
+    count = pieces[0].shape[0]
+    if count % 16 == 0:
+        for index, piece in enumerate(pieces):
+            out_ref[index * count : (index + 1) * count, :] = piece[...]
+        return
+    for index, piece in enumerate(pieces):
+        rows[index * count : (index + 1) * count, :] = piece[...].astype(F32)
+    out_ref[...] = rows[...].astype(BF16)
+
+
+def stack(pieces):
+    shape = (len(pieces) * pieces[0].shape[0], pieces[0].shape[1])
+    return pl.pallas_call(
+        stack_kernel,
+        out_shape=jax.ShapeDtypeStruct(shape, BF16),
+        in_specs=[whole()] * len(pieces),
+        out_specs=whole(),
+        scratch_shapes=[pltpu.VMEM(shape, F32)],
+        compiler_params=params(),
+        cost_estimate=pl.CostEstimate(
+            flops=0, transcendentals=0, bytes_accessed=4 * shape[0] * shape[1]
+        ),
+    )(*pieces)
+
+
 def spread(piece):
-    def swap(held, mask):
-        return lax.ppermute(held, "cand", exchange_pairs(mask))
-
-    held = piece
-    for hop in (1, 2, 4):
-        other = swap(held, hop * CORES)
-        held = lax.optimization_barrier(jnp.concatenate([held, other], axis=0))
-    others = [swap(held, hop * DEPTHS * CORES) for hop in range(1, WIDTHS)]
-    held = lax.optimization_barrier(jnp.concatenate([held] + others, axis=0))
-    return held, swap(held, 1)
-
-
-def exact_dot(left, right):
-    return jnp.dot(
-        left, right, precision=lax.Precision.HIGHEST, preferred_element_type=jnp.float32
-    )
-
-
-def solve_chain(whitened, factor_rows, diag_inv):
+    def swap(held, pairs):
+        return lax.ppermute(held, "cand", pairs)
+
+    ups, downs = [piece], [piece]
+    for hop in range(1, DEPTHS // 2 + 1):
+        ups.append(swap(ups[-1], ring_pairs(1)))
+        if hop < DEPTHS // 2:
+            downs.append(swap(downs[-1], ring_pairs(-1)))
+    held = stack(ups + downs[:0:-1])
+    others = [swap(held, exchange_pairs(hop * DEPTHS * CORES)) for hop in range(1, WIDTHS)]
+    near = stack([held] + others)
+    return near, swap(near, exchange_pairs(1))
+
+
+def split_kernel(inverse_ref, factor_ref, high_ref, middle_ref, low_ref):
+    first = pl.program_id(0) == 0
+    values = jnp.where(first, inverse_ref[...], factor_ref[...])
+    high, middle, low = three_pieces(values)
+    high_ref[...] = high.astype(BF16)
+    middle_ref[...] = middle.astype(BF16)
+    low_ref[...] = low.astype(BF16)
+
+
+def split(diag_inv, factor_rows, sections):
+    block = diag_inv.shape
+    columns = sections * block[1]
+    return pl.pallas_call(
+        split_kernel,
+        out_shape=(jax.ShapeDtypeStruct((block[0], columns), BF16),) * 3,
+        grid=(sections,),
+        in_specs=[
+            pl.BlockSpec(block, lambda i: (0, 0)),
+            pl.BlockSpec(block, lambda i: (0, jnp.maximum(i - 1, 0))),
+        ],
+        out_specs=(pl.BlockSpec(block, lambda i: (0, i)),) * 3,
+        compiler_params=params(),
+        cost_estimate=pl.CostEstimate(
+            flops=8 * block[0] * columns, transcendentals=0, bytes_accessed=10 * block[0] * columns
+        ),
+        name="split",
+    )(diag_inv, factor_rows)
+
+
+def exact_lines(left, lines):
+    rows = left.shape[0]
+    lines[...] = jnp.zeros_like(lines)
+    for index, piece in enumerate(three_pieces(left)):
+        lines[index * rows : (index + 1) * rows, :] = piece
+    return lines[...].astype(BF16)
+
+
+def exact_dot(lines, rows, pieces, columns):
+    total = None
+    for piece, count in zip(pieces[::-1], (1, 2, 3)):
+        product = jnp.dot(lines, piece[:, columns], preferred_element_type=F32)
+        for index in reversed(range(count)):
+            term = product[index * rows : (index + 1) * rows]
+            total = term if total is None else total + term
+    return total
+
+
+def solve_kernel(
+    section, place_ref, whitened_ref, carried_ref, weights_ref, high_ref, middle_ref, low_ref,
+    *rest,
+):
+    *update_ref, solved_ref, lines = rest
+    pieces = (high_ref, middle_ref, low_ref)
+    count, width = whitened_ref.shape
+    remaining = whitened_ref[...]
+    if carried_ref is not None:
+        remaining = remaining - carried_ref[:, section * width : (section + 1) * width]
+    solved = exact_dot(exact_lines(remaining, lines), count, pieces, slice(0, width))
+    wire = solved.astype(BF16)
+    if weights_ref is not None:
+        wire = jnp.where(place_ref[0] == section, wire.astype(F32), weights_ref[...].astype(F32))
+    solved_ref[...] = wire.astype(BF16)
+    if section > 0:
+        left = exact_lines(solved, lines)
+
+        @pl.loop(0, section)
+        def _(earlier):
+            first = pl.multiple_of(earlier * width, width)
+            later = pl.multiple_of((earlier + 1) * width, width)
+            update = exact_dot(left, count, pieces, pl.ds(later, width))
+            if carried_ref is not None:
+                update = update + carried_ref[:, pl.ds(first, width)]
+            update_ref[0][:, pl.ds(first, width)] = update
+
+
+def solve(section, place, whitened, carried, weights, pieces):
+    count, width = whitened.shape
+    out_shape = [jax.ShapeDtypeStruct((count, width), BF16)]
+    if section > 0:
+        out_shape.insert(0, jax.ShapeDtypeStruct((count, section * width), F32))
+    columns = (section + 1) * width
+
+    def kernel(place_ref, whitened_ref, *refs):
+        if carried is None:
+            refs = (None, None) + refs
+        solve_kernel(section, place_ref, whitened_ref, *refs)
+
+    held = [] if carried is None else [carried, weights]
+    results = pl.pallas_call(
+        kernel,
+        out_shape=out_shape,
+        in_specs=[pl.BlockSpec(memory_space=pltpu.SMEM)] + [whole()] * (1 + len(held) + 3),
+        out_specs=[whole()] * len(out_shape),
+        scratch_shapes=[pltpu.VMEM((16, width), F32)],
+        compiler_params=params(),
+        cost_estimate=pl.CostEstimate(
+            flops=2 * 36 * width * columns, transcendentals=0, bytes_accessed=6 * width * columns
+        ),
+    )(place, whitened, *held, *pieces)
+    return results if section > 0 else (None, results[0])
+
+
+def solve_chain(place, whitened, factor_rows, diag_inv):
     sections = lax.axis_size("rows")
-    position = lax.axis_index("rows")
-    width = diag_inv.shape[1]
-    weights = jnp.zeros_like(whitened)
-    carried = None
+    pieces = split(diag_inv, factor_rows, sections)
+    carried = weights = None
     for section in reversed(range(sections)):
-        earlier = section * width
-
-        def solve_own(carried, weights):
-            remaining = whitened if carried is None else whitened - carried[:, earlier:]
-            solved = exact_dot(remaining, diag_inv)
-            if section == 0:
-                return None, solved
-            update = exact_dot(solved, factor_rows[:, :earlier])
-            if carried is not None:
-                update = carried[:, :earlier] + update
-            return update, solved
-
-        def pass_on(carried, weights):
-            if section == 0:
-                return None, weights
-            shape = (whitened.shape[0], earlier)
-            return (jnp.zeros(shape, jnp.float32) if carried is None else carried[:, :earlier]), weights
-
-        carried, weights = lax.cond(position == section, solve_own, pass_on, carried, weights)
+        carried, weights = solve(section, place, whitened, carried, weights, pieces)
         if section > 0:
-            pairs = [(section, section - 1)]
-            carried = lax.ppermute(carried, "rows", pairs)
+            carried = lax.ppermute(carried, "rows", [(section, section - 1)])
     return weights
 
 
@@ -295,13 +432,14 @@
     prior_coef,
 ):
     place = jnp.stack([lax.axis_index("rows"), lax.axis_index("cand")]).astype(jnp.int32)
-    coef_near, coef_far = spread(prior_coef)
-    weights = solve_chain(whitened, factor_rows, diag_inv).astype(BF16)
-    weight_near, weight_far = spread(weights)
+    chosen = choice(place, whitened.shape[0] * lax.axis_size("cand"))
+    coef_sets = spread(prior_coef)
+    weights = solve_chain(place, whitened, factor_rows, diag_inv)
+    weight_sets = spread(weights)
     turns, exponent, levels = prepare(frequencies, phases, observed, inv_length, grid_coords)
     made = [tiles(turns, exponent, levels, chunk) for chunk in range(CHUNKS)]
-    coefs = in_order(place, coef_near, coef_far)
-    solved = in_order(place, weight_near, weight_far)
+    coefs = in_order(chosen, coef_sets)
+    solved = in_order(chosen, weight_sets)
     rows = lax.axis_size("rows")
     each = CHUNKS // PARTS
     sums = []

time: 123 us -> 139 us (1.13)
  starting transfers between devices: 43.4 us -> 54 us
  Pallas kernels: 29.1 us -> 38.3 us
  waiting for transfers between devices: 43.7 us -> 40.1 us
  local copies, waits for them, and re-layouts: 0.73 us -> 4.15 us
  matrix products: 2.45 us -> 0 us
  other arithmetic: 2.88 us -> 1.34 us
    ppermute x17 -> x25, starting transfers between devices: 36.2 us -> 46.8 us  [the longest x22 44.2 us: swap(): return lax.ppermute(held, 'cand', pairs)]
    pallas_call x4 -> x14, Pallas kernels: 9.47 us -> 18.7 us  [the longest x2 8.29 us: products(): pl.pallas_call(product_kernel, out_shape=out_shapes, in_specs=[whole()] *...]
    unnamed x10 -> x18, local copies, waits for them, and re-layouts: 0.02 us -> 4.15 us
    ppermute x17 -> x25, waiting for transfers between devices: 33.7 us -> 30 us  [the longest x22 20.8 us: swap(): return lax.ppermute(held, 'cand', pairs)]
    dot_general x1 -> x0, matrix products: 2.45 us -> none  [exact_dot(): jnp.dot(left, right, precision=lax.Precision.HIGHEST, preferred_element_t...]
  transfers between devices with their start and end apart: 23 -> 31, of which waited for: 10 -> 17; matrix products, arithmetic and copies ran while one was open for 3% -> 0% of each run, Pallas kernels for 20% -> 24%
where the time goes in v2:
time: 139 us; the launch traced here: 138 us
  starting transfers between devices  54 us (39%)
  waiting for transfers between devices  40.1 us (29%)
  Pallas kernels  38.3 us (28%)
  local copies, waits for them, and re-layouts  4.15 us (3%)
    ppermute x22, starting transfers between devices, swap(): return lax.ppermute(held, 'cand', pairs)  44.2 us
    ppermute x22, waiting for transfers between devices, swap(): return lax.ppermute(held, 'cand', pairs)  20.8 us
    pallas_call x8, Pallas kernels, tiles(): pl.pallas_call(tile_kernel, out_shape=(jax.ShapeDtypeStruct((feats, cands...  19 us
    ppermute x6, waiting for transfers between devices, body(): total = total + lax.ppermute(block, 'rows', pairs).astype(F32)  10.1 us
    ppermute x3, waiting for transfers between devices, solve_chain(): carried = lax.ppermute(carried, 'rows', [(section, section - 1)])  9.22 us
    pallas_call x2, Pallas kernels, products(): pl.pallas_call(product_kernel, out_shape=out_shapes, in_specs=[whole()] *...  8.29 us
    ppermute x6, starting transfers between devices, body(): total = total + lax.ppermute(block, 'rows', pairs).astype(F32)  7.25 us
    pallas_call x4, Pallas kernels, solve(): pl.pallas_call(kernel, out_shape=out_shape, in_specs=[pl.BlockSpec(memory...  5.47 us
  transfers between devices with their start and end apart: 31, of which 17 were waited for; matrix products, arithmetic and copies ran while one was open for 0% of the time, Pallas kernels for 24%

profile of v2, /device:TPU:1, one launch (start us, length us, event | category | flops | bytes accessed | tf_op | source)
XLA Modules:
  0.0 138.2 jit_solution(11968529450353298973)
XLA Ops:
  0.0 2.5 %collective-permute-start = (bf16[4,2048]{1,0:T(4,128)(2,1)}, bf16[4,2048]{1,0:T(4,128)(2,1)S(1)}, u32[]{:S(2)}, u32[]{:S(2)}) collective-permute-start(bf16[4,2048]{1,0:T(4,128)(2,1)} %refs_0_.1), channel_id=1, source_target_pairs={{0,2},{1,3},{2,4},{3,5},{4,6},{5,7},{6,8},{7,9},{8,10},{9,11},{10,... | collective-permute-start | bytes 49160 | tf_op jit(solution)/shard_map/ppermute | solution.py:297
  2.5 3.9 %collective-permute-start.4 = (bf16[4,2048]{1,0:T(4,128)(2,1)}, bf16[4,2048]{1,0:T(4,128)(2,1)S(1)}, u32[]{:S(2)}, u32[]{:S(2)}) collective-permute-start(bf16[4,2048]{1,0:T(4,128)(2,1)} %refs_0_.1), channel_id=1, source_target_pairs={{0,14},{1,15},{2,0},{3,1},{4,2},{5,3},{6,4},{7,5},{8,6},{9,7},{10,... | collective-permute-start | bytes 49160 | tf_op jit(solution)/shard_map/ppermute | solution.py:297
  6.4 1.3 collective-permute-done.refs_1_
  7.7 2.7 %collective-permute-start.5 = (bf16[4,2048]{1,0:T(4,128)(2,1)S(1)}, bf16[4,2048]{1,0:T(4,128)(2,1)S(1)}, u32[]{:S(2)}, u32[]{:S(2)}) collective-permute-start(bf16[4,2048]{1,0:T(4,128)(2,1)S(1)} %collective-permute-done.4.refs_7_), channel_id=1, source_target_pairs={{0,14},{1,15},{2,0},{3,1},{4,2},{5,3},{6,4},{7,5},{8,6},{9,7},{10,... | collective-permute-start | bytes 49160 | tf_op jit(solution)/shard_map/ppermute | solution.py:297
  10.4 1.1 collective-permute-done.1.refs_2_
  11.5 2.7 %collective-permute-start.6 = (bf16[4,2048]{1,0:T(4,128)(2,1)S(1)}, bf16[4,2048]{1,0:T(4,128)(2,1)S(1)}, u32[]{:S(2)}, u32[]{:S(2)}) collective-permute-start(bf16[4,2048]{1,0:T(4,128)(2,1)S(1)} %collective-permute-done.5.refs_6_), channel_id=1, source_target_pairs={{0,14},{1,15},{2,0},{3,1},{4,2},{5,3},{6,4},{7,5},{8,6},{9,7},{10,... | collective-permute-start | bytes 49160 | tf_op jit(solution)/shard_map/ppermute | solution.py:297
  14.2 1.1 collective-permute-done.2.refs_3_
  15.3 3.8 %collective-permute-done.3.refs_4_ = bf16[4,2048]{1,0:T(4,128)(2,1)S(1)} collective-permute-done((bf16[4,2048]{1,0:T(4,128)(2,1)S(1)}, bf16[4,2048]{1,0:T(4,128)(2,1)S(1)}, u32[]{:S(2)}, u32[]{:S(2)}) %collective-permute-start.3) | collective-permute-done | bytes 16416 | tf_op jit(solution)/shard_map/ppermute | solution.py:297
  19.9 1.3 collective-permute-start.7
  21.2 2.5 %collective-permute-start.8 = (bf16[32,2048]{1,0:T(8,128)(2,1)S(1)}, bf16[32,2048]{1,0:T(8,128)(2,1)S(1)}, u32[]{:S(2)}, u32[]{:S(2)}) collective-permute-start(bf16[32,2048]{1,0:T(8,128)(2,1)S(1)} %shard_map.91.refs_0_), channel_id=1, source_target_pairs={{0,32},{1,33},{2,34},{3,35},{4,36},{5,37},{6,38},{7,39},{8,40},{9,... | collective-permute-start | bytes 393224 | tf_op jit(solution)/shard_map/ppermute | solution.py:297
  23.9 3.6 %collective-permute-done.8.refs_2_ = bf16[32,2048]{1,0:T(8,128)(2,1)S(1)} collective-permute-done((bf16[32,2048]{1,0:T(8,128)(2,1)S(1)}, bf16[32,2048]{1,0:T(8,128)(2,1)S(1)}, u32[]{:S(2)}, u32[]{:S(2)}) %collective-permute-start.8) | collective-permute-done | bytes 131104 | tf_op jit(solution)/shard_map/ppermute | solution.py:297
  27.4 1.4 %collective-permute-done.9.refs_3_ = bf16[32,2048]{1,0:T(8,128)(2,1)S(1)} collective-permute-done((bf16[32,2048]{1,0:T(8,128)(2,1)S(1)}, bf16[32,2048]{1,0:T(8,128)(2,1)S(1)}, u32[]{:S(2)}, u32[]{:S(2)}) %collective-permute-start.9) | collective-permute-done | bytes 131104 | tf_op jit(solution)/shard_map/ppermute | solution.py:297
  28.9 6.7 %collective-permute-start.10 = (bf16[128,2048]{1,0:T(8,128)(2,1)S(1)}, bf16[128,2048]{1,0:T(8,128)(2,1)S(1)}, u32[]{:S(2)}, u32[]{:S(2)}) collective-permute-start(bf16[128,2048]{1,0:T(8,128)(2,1)S(1)} %shard_map.92.refs_0_), channel_id=1, source_target_pairs={{0,1},{1,0},{2,3},{3,2},{4,5},{5,4},{6,7},{7,6},{8,9},{9,8},{10,11... | collective-permute-start | bytes 1572872 | tf_op jit(solution)/shard_map/ppermute | solution.py:297
  35.5 2.2 %copy-done = f32[512,2048]{1,0:T(8,128)S(1)} copy-done((f32[512,2048]{1,0:T(8,128)S(1)}, f32[512,2048]{1,0:T(8,128)}, u32[]{:S(2)}) %copy-start) | copy-done | bytes 4194328
  37.7 1.2 copy-done.1
  38.9 2.0 %split.1 = (bf16[512,2048]{1,0:T(8,128)(2,1)S(1)}, bf16[512,2048]{1,0:T(8,128)(2,1)S(1)}, bf16[512,2048]{1,0:T(8,128)(2,1)S(1)}) custom-call(f32[512,512]{1,0:T(8,128)S(1)} %copy-done.1, f32[512,2048]{1,0:T(8,128)S(1)} %copy-done), custom_call_target="tpu_custom_call" | custom-call | flops 8388608 | bytes 10485760 | tf_op jit(solution)/shard_map/split/pallas_call | solution.py:322
  41.0 1.9 %shard_map.94 = (f32[4,1536]{1,0:T(4,128)S(1)}, bf16[4,512]{1,0:T(4,128)(2,1)S(1)}) custom-call(s32[2]{0:T(128)S(1)} %pad_add_fusion.place_ref, f32[4,512]{1,0:T(4,128)S(1)} %copy-done.4, bf16[512,2048]{1,0:T(8,128)(2,1)S(1)} %get-tuple-element.41.refs_0_.refs_2_, bf16[512,2048]{1,0:T(8,128)(2,1)S(1)} %get-tuple-element.42.refs_1_.refs_3_, ...), custom_call_target="tpu_custom_call" | custom-call | flops 75497472 | bytes 6291456 | tf_op jit(solution)/shard_map/pallas_call | solution.py:398
  43.6 1.5 %shard_map.95 = (f32[4,1024]{1,0:T(4,128)S(1)}, bf16[4,512]{1,0:T(4,128)(2,1)S(1)}) custom-call(s32[2]{0:T(128)S(1)} %pad_add_fusion.place_ref, f32[4,512]{1,0:T(4,128)S(1)} %copy-done.4, f32[4,1536]{1,0:T(4,128)S(1)} %collective-permute-done.11.refs_0_, bf16[4,512]{1,0:T(4,128)(2,1)S(1)} %get-tuple-element.45.refs_1_, ...), custom_call_target="tpu_custom_call" | custom-call | flops 56623104 | bytes 4718592 | tf_op jit(solution)/shard_map/pallas_call | solution.py:398
  45.8 1.2 shard_map.96
  47.0 1.3 collective-permute-start.13
  48.3 9.2 %collective-permute-done.13.refs_0_ = f32[4,512]{1,0:T(4,128)S(1)} collective-permute-done((f32[4,512]{1,0:T(4,128)S(1)}, f32[4,512]{1,0:T(4,128)S(1)}, u32[]{:S(2)}, u32[]{:S(2)}) %collective-permute-start.13) | collective-permute-done | bytes 8224 | tf_op jit(solution)/shard_map/ppermute | solution.py:419
  58.5 2.7 %collective-permute-start.18 = (bf16[4,512]{1,0:T(4,128)(2,1)S(1)}, bf16[4,512]{1,0:T(4,128)(2,1)S(1)}, u32[]{:S(2)}, u32[]{:S(2)}) collective-permute-start(bf16[4,512]{1,0:T(4,128)(2,1)S(1)} %shard_map.97.refs_0_), channel_id=1, source_target_pairs={{0,14},{1,15},{2,0},{3,1},{4,2},{5,3},{6,4},{7,5},{8,6},{9,7},{10,... | collective-permute-start | bytes 12296 | tf_op jit(solution)/shard_map/ppermute | solution.py:297
  61.1 1.0 collective-permute-done.14.refs_1_
  62.1 2.7 %collective-permute-start.19 = (bf16[4,512]{1,0:T(4,128)(2,1)S(1)}, bf16[4,512]{1,0:T(4,128)(2,1)S(1)}, u32[]{:S(2)}, u32[]{:S(2)}) collective-permute-start(bf16[4,512]{1,0:T(4,128)(2,1)S(1)} %collective-permute-done.18.refs_7_), channel_id=1, source_target_pairs={{0,14},{1,15},{2,0},{3,1},{4,2},{5,3},{6,4},{7,5},{8,6},{9,7},{10,... | collective-permute-start | bytes 12296 | tf_op jit(solution)/shard_map/ppermute | solution.py:297
  64.8 1.0 collective-permute-done.15.refs_2_
  65.8 3.0 %collective-permute-start.20 = (bf16[4,512]{1,0:T(4,128)(2,1)S(1)}, bf16[4,512]{1,0:T(4,128)(2,1)S(1)}, u32[]{:S(2)}, u32[]{:S(2)}) collective-permute-start(bf16[4,512]{1,0:T(4,128)(2,1)S(1)} %collective-permute-done.19.refs_6_), channel_id=1, source_target_pairs={{0,14},{1,15},{2,0},{3,1},{4,2},{5,3},{6,4},{7,5},{8,6},{9,7},{10,... | collective-permute-start | bytes 12296 | tf_op jit(solution)/shard_map/ppermute | solution.py:297
  69.5 3.6 %collective-permute-done.17.refs_4_ = bf16[4,512]{1,0:T(4,128)(2,1)S(1)} collective-permute-done((bf16[4,512]{1,0:T(4,128)(2,1)S(1)}, bf16[4,512]{1,0:T(4,128)(2,1)S(1)}, u32[]{:S(2)}, u32[]{:S(2)}) %collective-permute-start.17) | collective-permute-done | bytes 4128 | tf_op jit(solution)/shard_map/ppermute | solution.py:297
  73.3 2.0 %collective-permute-start.22 = (bf16[32,512]{1,0:T(8,128)(2,1)S(1)}, bf16[32,512]{1,0:T(8,128)(2,1)S(1)}, u32[]{:S(2)}, u32[]{:S(2)}) collective-permute-start(bf16[32,512]{1,0:T(8,128)(2,1)S(1)} %shard_map.98.refs_0_), channel_id=1, source_target_pairs={{0,32},{1,33},{2,34},{3,35},{4,36},{5,37},{6,38},{7,39},{8,40},{9,... | collective-permute-start | bytes 98312 | tf_op jit(solution)/shard_map/ppermute | solution.py:297
  75.2 1.9 %collective-permute-start.23 = (bf16[32,512]{1,0:T(8,128)(2,1)S(1)}, bf16[32,512]{1,0:T(8,128)(2,1)S(1)}, u32[]{:S(2)}, u32[]{:S(2)}) collective-permute-start(bf16[32,512]{1,0:T(8,128)(2,1)S(1)} %shard_map.98.refs_0_), channel_id=1, source_target_pairs={{0,48},{1,49},{2,50},{3,51},{4,52},{5,53},{6,54},{7,55},{8,56},{9,... | collective-permute-start | bytes 98312 | tf_op jit(solution)/shard_map/ppermute | solution.py:297
  77.6 1.6 %collective-permute-done.23.refs_3_ = bf16[32,512]{1,0:T(8,128)(2,1)S(1)} collective-permute-done((bf16[32,512]{1,0:T(8,128)(2,1)S(1)}, bf16[32,512]{1,0:T(8,128)(2,1)S(1)}, u32[]{:S(2)}, u32[]{:S(2)}) %collective-permute-start.23) | collective-permute-done | bytes 32800 | tf_op jit(solution)/shard_map/ppermute | solution.py:297
  79.2 9.5 %collective-permute-start.24 = (bf16[128,512]{1,0:T(8,128)(2,1)S(1)}, bf16[128,512]{1,0:T(8,128)(2,1)S(1)}, u32[]{:S(2)}, u32[]{:S(2)}) collective-permute-start(bf16[128,512]{1,0:T(8,128)(2,1)S(1)} %shard_map.99.refs_0_), channel_id=1, source_target_pairs={{0,1},{1,0},{2,3},{3,2},{4,5},{5,4},{6,7},{7,6},{8,9},{9,8},{10,11... | collective-permute-start | bytes 393224 | tf_op jit(solution)/shard_map/ppermute | solution.py:297
  90.2 2.4 %shard_map.101 = (bf16[2048,512]{1,0:T(8,128)(2,1)S(1)}, bf16[512,512]{1,0:T(8,128)(2,1)S(1)}) custom-call(bf16[2048,128]{1,0:T(8,128)(2,1)S(1)} %get-tuple-element.50.turns_ref, bf16[512,128]{1,0:T(8,128)(2,1)S(1)} %get-tuple-element.51.exponent_ref, bf16[128,4096]{1,0:T(8,128)(2,1)S(1)} %get-tuple-element.52.levels_ref), custom_call_target="tpu_custom_call" | custom-call | flops 31457280 | bytes 2621440 | tf_op jit(solution)/shard_map/pallas_call | solution.py:133
  92.6 2.4 %shard_map.102 = (bf16[2048,512]{1,0:T(8,128)(2,1)S(1)}, bf16[512,512]{1,0:T(8,128)(2,1)S(1)}) custom-call(bf16[2048,128]{1,0:T(8,128)(2,1)S(1)} %get-tuple-element.50.turns_ref, bf16[512,128]{1,0:T(8,128)(2,1)S(1)} %get-tuple-element.51.exponent_ref, bf16[128,4096]{1,0:T(8,128)(2,1)S(1)} %get-tuple-element.52.levels_ref), custom_call_target="tpu_custom_call" | custom-call | flops 31457280 | bytes 2621440 | tf_op jit(solution)/shard_map/pallas_call | solution.py:133
  95.0 2.4 %shard_map.103 = (bf16[2048,512]{1,0:T(8,128)(2,1)S(1)}, bf16[512,512]{1,0:T(8,128)(2,1)S(1)}) custom-call(bf16[2048,128]{1,0:T(8,128)(2,1)S(1)} %get-tuple-element.50.turns_ref, bf16[512,128]{1,0:T(8,128)(2,1)S(1)} %get-tuple-element.51.exponent_ref, bf16[128,4096]{1,0:T(8,128)(2,1)S(1)} %get-tuple-element.52.levels_ref), custom_call_target="tpu_custom_call" | custom-call | flops 31457280 | bytes 2621440 | tf_op jit(solution)/shard_map/pallas_call | solution.py:133
  97.4 2.4 %shard_map.104 = (bf16[2048,512]{1,0:T(8,128)(2,1)S(1)}, bf16[512,512]{1,0:T(8,128)(2,1)S(1)}) custom-call(bf16[2048,128]{1,0:T(8,128)(2,1)S(1)} %get-tuple-element.50.turns_ref, bf16[512,128]{1,0:T(8,128)(2,1)S(1)} %get-tuple-element.51.exponent_ref, bf16[128,4096]{1,0:T(8,128)(2,1)S(1)} %get-tuple-element.52.levels_ref), custom_call_target="tpu_custom_call" | custom-call | flops 31457280 | bytes 2621440 | tf_op jit(solution)/shard_map/pallas_call | solution.py:133
  100.2 1.6 %shard_map.93.coef_ref = bf16[256,2048]{1,0:T(8,128)(2,1)S(1)} custom-call(bf16[256,256]{1,0:T(8,128)(2,1)S(1)} %choice.1.chosen_ref, bf16[128,2048]{1,0:T(8,128)(2,1)S(1)} %shard_map.92.refs_0_, bf16[128,2048]{1,0:T(8,128)(2,1)S(1)} %collective-permute-done.10.refs_1_), custom_call_target="tpu_custom_call" | custom-call | flops 268435456 | bytes 2097152 | tf_op jit(solution)/shard_map/pallas_call | solution.py:201
  101.7 4.1 %shard_map.105 = (f32[64,2048]{1,0:T(8,128)S(1)}, bf16[64,2048]{1,0:T(8,128)(2,1)S(1)}, bf16[64,2048]{1,0:T(8,128)(2,1)S(1)}, bf16[64,2048]{1,0:T(8,128)(2,1)S(1)}) custom-call(bf16[256,2048]{1,0:T(8,128)(2,1)S(1)} %shard_map.93.coef_ref, bf16[256,512]{1,0:T(8,128)(2,1)S(1)} %shard_map.100.weight_ref, bf16[2048,512]{1,0:T(8,128)(2,1)S(1)} %get-tuple-element.53.refs_0_, ...), custom_call_target="tpu_custom_call" | custom-call | flops 2684354560 | bytes 10485760 | tf_op jit(solution)/shard_map/pallas_call | solution.py:242
  106.1 2.6 %collective-permute-start.27 = (bf16[64,2048]{1,0:T(8,128)(2,1)S(1)}, bf16[64,2048]{1,0:T(8,128)(2,1)S(1)}, u32[]{:S(2)}, u32[]{:S(2)}) collective-permute-start(bf16[64,2048]{1,0:T(8,128)(2,1)S(1)} %get-tuple-element.64), channel_id=1, source_target_pairs={{0,192},{64,0},{128,64},{192,128},{1,193},{65,1},{129,65},{193,129... | collective-permute-start | bytes 786440 | tf_op jit(solution)/shard_map/ppermute | solution.py:452
  108.7 2.4 %shard_map.106 = (bf16[2048,512]{1,0:T(8,128)(2,1)S(1)}, bf16[512,512]{1,0:T(8,128)(2,1)S(1)}) custom-call(bf16[2048,128]{1,0:T(8,128)(2,1)S(1)} %get-tuple-element.50.turns_ref, bf16[512,128]{1,0:T(8,128)(2,1)S(1)} %get-tuple-element.51.exponent_ref, bf16[128,4096]{1,0:T(8,128)(2,1)S(1)} %get-tuple-element.52.levels_ref), custom_call_target="tpu_custom_call" | custom-call | flops 31457280 | bytes 2621440 | tf_op jit(solution)/shard_map/pallas_call | solution.py:133
  111.0 2.4 %shard_map.107 = (bf16[2048,512]{1,0:T(8,128)(2,1)S(1)}, bf16[512,512]{1,0:T(8,128)(2,1)S(1)}) custom-call(bf16[2048,128]{1,0:T(8,128)(2,1)S(1)} %get-tuple-element.50.turns_ref, bf16[512,128]{1,0:T(8,128)(2,1)S(1)} %get-tuple-element.51.exponent_ref, bf16[128,4096]{1,0:T(8,128)(2,1)S(1)} %get-tuple-element.52.levels_ref), custom_call_target="tpu_custom_call" | custom-call | flops 31457280 | bytes 2621440 | tf_op jit(solution)/shard_map/pallas_call | solution.py:133
  113.4 2.4 %shard_map.108 = (bf16[2048,512]{1,0:T(8,128)(2,1)S(1)}, bf16[512,512]{1,0:T(8,128)(2,1)S(1)}) custom-call(bf16[2048,128]{1,0:T(8,128)(2,1)S(1)} %get-tuple-element.50.turns_ref, bf16[512,128]{1,0:T(8,128)(2,1)S(1)} %get-tuple-element.51.exponent_ref, bf16[128,4096]{1,0:T(8,128)(2,1)S(1)} %get-tuple-element.52.levels_ref), custom_call_target="tpu_custom_call" | custom-call | flops 31457280 | bytes 2621440 | tf_op jit(solution)/shard_map/pallas_call | solution.py:133
  115.8 2.4 %shard_map.109 = (bf16[2048,512]{1,0:T(8,128)(2,1)S(1)}, bf16[512,512]{1,0:T(8,128)(2,1)S(1)}) custom-call(bf16[2048,128]{1,0:T(8,128)(2,1)S(1)} %get-tuple-element.50.turns_ref, bf16[512,128]{1,0:T(8,128)(2,1)S(1)} %get-tuple-element.51.exponent_ref, bf16[128,4096]{1,0:T(8,128)(2,1)S(1)} %get-tuple-element.52.levels_ref), custom_call_target="tpu_custom_call" | custom-call | flops 31457280 | bytes 2621440 | tf_op jit(solution)/shard_map/pallas_call | solution.py:133
  118.2 4.1 %shard_map.110 = (f32[64,2048]{1,0:T(8,128)S(1)}, bf16[64,2048]{1,0:T(8,128)(2,1)S(1)}, bf16[64,2048]{1,0:T(8,128)(2,1)S(1)}, bf16[64,2048]{1,0:T(8,128)(2,1)S(1)}) custom-call(bf16[256,2048]{1,0:T(8,128)(2,1)S(1)} %shard_map.93.coef_ref, bf16[256,512]{1,0:T(8,128)(2,1)S(1)} %shard_map.100.weight_ref, bf16[2048,512]{1,0:T(8,128)(2,1)S(1)} %get-tuple-element.65.refs_0_, ...), custom_call_target="tpu_custom_call" | custom-call | flops 2684354560 | bytes 10485760 | tf_op jit(solution)/shard_map/pallas_call | solution.py:242
  123.0 1.9 %collective-permute-start.29 = (bf16[64,2048]{1,0:T(8,128)(2,1)S(1)}, bf16[64,2048]{1,0:T(8,128)(2,1)S(1)}, u32[]{:S(2)}, u32[]{:S(2)}) collective-permute-start(bf16[64,2048]{1,0:T(8,128)(2,1)S(1)} %get-tuple-element.75), channel_id=1, source_target_pairs={{0,128},{64,192},{128,0},{192,64},{1,129},{65,193},{129,1},{193,65... | collective-permute-start | bytes 786440 | tf_op jit(solution)/shard_map/ppermute | solution.py:452
  124.9 2.0 %collective-permute-start.30 = (bf16[64,2048]{1,0:T(8,128)(2,1)S(1)}, bf16[64,2048]{1,0:T(8,128)(2,1)S(1)}, u32[]{:S(2)}, u32[]{:S(2)}) collective-permute-start(bf16[64,2048]{1,0:T(8,128)(2,1)S(1)} %get-tuple-element.76), channel_id=1, source_target_pairs={{0,192},{64,0},{128,64},{192,128},{1,193},{65,1},{129,65},{193,129... | collective-permute-start | bytes 786440 | tf_op jit(solution)/shard_map/ppermute | solution.py:452
  127.0 4.2 %collective-permute-done.28 = bf16[64,2048]{1,0:T(8,128)(2,1)S(1)} collective-permute-done((bf16[64,2048]{1,0:T(8,128)(2,1)S(1)}, bf16[64,2048]{1,0:T(8,128)(2,1)S(1)}, u32[]{:S(2)}, u32[]{:S(2)}) %collective-permute-start.28) | collective-permute-done | bytes 262176 | tf_op jit(solution)/shard_map/ppermute | solution.py:452
  131.2 5.1 %collective-permute-done.29 = bf16[64,2048]{1,0:T(8,128)(2,1)S(1)} collective-permute-done((bf16[64,2048]{1,0:T(8,128)(2,1)S(1)}, bf16[64,2048]{1,0:T(8,128)(2,1)S(1)}, u32[]{:S(2)}, u32[]{:S(2)}) %collective-permute-start.29) | collective-permute-done | bytes 262176 | tf_op jit(solution)/shard_map/ppermute | solution.py:452
  137.2 1.0 maximum_bitcast_fusion
  (59 shorter events, 8.4 us)
Async XLA Ops:
  0.0 7.7 %collective-permute-start = (bf16[4,2048]{1,0:T(4,128)(2,1)}, bf16[4,2048]{1,0:T(4,128)(2,1)S(1)}, u32[]{:S(2)}, u32[]{:S(2)}) collective-permute-start(bf16[4,2048]{1,0:T(4,128)(2,1)} %refs_0_.1), channel_id=1, source_target_pairs={{0,2},{1,3},{2,4},{3,5},{4,6},{5,7},{6,8},{7,9},{8,10},{9,11},{10,... | collective-permute-start | bytes 49160 | tf_op jit(solution)/shard_map/ppermute | solution.py:297
  2.5 5.3 %collective-permute-start.4 = (bf16[4,2048]{1,0:T(4,128)(2,1)}, bf16[4,2048]{1,0:T(4,128)(2,1)S(1)}, u32[]{:S(2)}, u32[]{:S(2)}) collective-permute-start(bf16[4,2048]{1,0:T(4,128)(2,1)} %refs_0_.1), channel_id=1, source_target_pairs={{0,14},{1,15},{2,0},{3,1},{4,2},{5,3},{6,4},{7,5},{8,6},{9,7},{10,... | collective-permute-start | bytes 49160 | tf_op jit(solution)/shard_map/ppermute | solution.py:297
  7.7 3.8 %collective-permute-start.1 = (bf16[4,2048]{1,0:T(4,128)(2,1)S(1)}, bf16[4,2048]{1,0:T(4,128)(2,1)S(1)}, u32[]{:S(2)}, u32[]{:S(2)}) collective-permute-start(bf16[4,2048]{1,0:T(4,128)(2,1)S(1)} %collective-permute-done.refs_1_), channel_id=1, source_target_pairs={{0,2},{1,3},{2,4},{3,5},{4,6},{5,7},{6,8},{7,9},{8,10},{9,11},{10,... | collective-permute-start | bytes 49160 | tf_op jit(solution)/shard_map/ppermute | solution.py:297
  7.7 3.8 %collective-permute-start.5 = (bf16[4,2048]{1,0:T(4,128)(2,1)S(1)}, bf16[4,2048]{1,0:T(4,128)(2,1)S(1)}, u32[]{:S(2)}, u32[]{:S(2)}) collective-permute-start(bf16[4,2048]{1,0:T(4,128)(2,1)S(1)} %collective-permute-done.4.refs_7_), channel_id=1, source_target_pairs={{0,14},{1,15},{2,0},{3,1},{4,2},{5,3},{6,4},{7,5},{8,6},{9,7},{10,... | collective-permute-start | bytes 49160 | tf_op jit(solution)/shard_map/ppermute | solution.py:297
  11.5 3.8 %collective-permute-start.2 = (bf16[4,2048]{1,0:T(4,128)(2,1)S(1)}, bf16[4,2048]{1,0:T(4,128)(2,1)S(1)}, u32[]{:S(2)}, u32[]{:S(2)}) collective-permute-start(bf16[4,2048]{1,0:T(4,128)(2,1)S(1)} %collective-permute-done.1.refs_2_), channel_id=1, source_target_pairs={{0,2},{1,3},{2,4},{3,5},{4,6},{5,7},{6,8},{7,9},{8,10},{9,11},{10,... | collective-permute-start | bytes 49160 | tf_op jit(solution)/shard_map/ppermute | solution.py:297
  11.5 3.8 %collective-permute-start.6 = (bf16[4,2048]{1,0:T(4,128)(2,1)S(1)}, bf16[4,2048]{1,0:T(4,128)(2,1)S(1)}, u32[]{:S(2)}, u32[]{:S(2)}) collective-permute-start(bf16[4,2048]{1,0:T(4,128)(2,1)S(1)} %collective-permute-done.5.refs_6_), channel_id=1, source_target_pairs={{0,14},{1,15},{2,0},{3,1},{4,2},{5,3},{6,4},{7,5},{8,6},{9,7},{10,... | collective-permute-start | bytes 49160 | tf_op jit(solution)/shard_map/ppermute | solution.py:297
  15.3 3.8 %collective-permute-start.3 = (bf16[4,2048]{1,0:T(4,128)(2,1)S(1)}, bf16[4,2048]{1,0:T(4,128)(2,1)S(1)}, u32[]{:S(2)}, u32[]{:S(2)}) collective-permute-start(bf16[4,2048]{1,0:T(4,128)(2,1)S(1)} %collective-permute-done.2.refs_3_), channel_id=1, source_target_pairs={{0,2},{1,3},{2,4},{3,5},{4,6},{5,7},{6,8},{7,9},{8,10},{9,11},{10,... | collective-permute-start | bytes 49160 | tf_op jit(solution)/shard_map/ppermute | solution.py:297
  19.1 0.7 copy-start.6
  19.9 3.9 %collective-permute-start.7 = (bf16[32,2048]{1,0:T(8,128)(2,1)S(1)}, bf16[32,2048]{1,0:T(8,128)(2,1)S(1)}, u32[]{:S(2)}, u32[]{:S(2)}) collective-permute-start(bf16[32,2048]{1,0:T(8,128)(2,1)S(1)} %shard_map.91.refs_0_), channel_id=1, source_target_pairs={{0,16},{1,17},{2,18},{3,19},{4,20},{5,21},{6,22},{7,23},{8,24},{9,... | collective-permute-start | bytes 393224 | tf_op jit(solution)/shard_map/ppermute | solution.py:297
  21.2 6.2 %collective-permute-start.8 = (bf16[32,2048]{1,0:T(8,128)(2,1)S(1)}, bf16[32,2048]{1,0:T(8,128)(2,1)S(1)}, u32[]{:S(2)}, u32[]{:S(2)}) collective-permute-start(bf16[32,2048]{1,0:T(8,128)(2,1)S(1)} %shard_map.91.refs_0_), channel_id=1, source_target_pairs={{0,32},{1,33},{2,34},{3,35},{4,36},{5,37},{6,38},{7,39},{8,40},{9,... | collective-permute-start | bytes 393224 | tf_op jit(solution)/shard_map/ppermute | solution.py:297
  23.7 5.2 %collective-permute-start.9 = (bf16[32,2048]{1,0:T(8,128)(2,1)S(1)}, bf16[32,2048]{1,0:T(8,128)(2,1)S(1)}, u32[]{:S(2)}, u32[]{:S(2)}) collective-permute-start(bf16[32,2048]{1,0:T(8,128)(2,1)S(1)} %shard_map.91.refs_0_), channel_id=1, source_target_pairs={{0,48},{1,49},{2,50},{3,51},{4,52},{5,53},{6,54},{7,55},{8,56},{9,... | collective-permute-start | bytes 393224 | tf_op jit(solution)/shard_map/ppermute | solution.py:297
  28.9 71.3 %collective-permute-start.10 = (bf16[128,2048]{1,0:T(8,128)(2,1)S(1)}, bf16[128,2048]{1,0:T(8,128)(2,1)S(1)}, u32[]{:S(2)}, u32[]{:S(2)}) collective-permute-start(bf16[128,2048]{1,0:T(8,128)(2,1)S(1)} %shard_map.92.refs_0_), channel_id=1, source_target_pairs={{0,1},{1,0},{2,3},{3,2},{4,5},{5,4},{6,7},{7,6},{8,9},{9,8},{10,11... | collective-permute-start | bytes 1572872 | tf_op jit(solution)/shard_map/ppermute | solution.py:297
  35.5 2.2 %copy-start = (f32[512,2048]{1,0:T(8,128)S(1)}, f32[512,2048]{1,0:T(8,128)}, u32[]{:S(2)}) copy-start(f32[512,2048]{1,0:T(8,128)} %factor_ref.1) | copy-start | bytes 12582916
  37.7 1.2 copy-start.1
  38.9 2.1 %copy-start.4 = (f32[4,512]{1,0:T(4,128)S(1)}, f32[4,512]{1,0:T(4,128)}, u32[]{:S(2)}) copy-start(f32[4,512]{1,0:T(4,128)} %whitened_ref.7) | copy-start | bytes 24580
  42.9 0.7 collective-permute-start.11
  45.1 0.7 collective-permute-start.12
  47.0 10.5 %collective-permute-start.13 = (f32[4,512]{1,0:T(4,128)S(1)}, f32[4,512]{1,0:T(4,128)S(1)}, u32[]{:S(2)}, u32[]{:S(2)}) collective-permute-start(f32[4,512]{1,0:T(4,128)S(1)} %get-tuple-element.48), channel_id=1, source_target_pairs={{64,0},{65,1},{66,2},{67,3},{68,4},{69,5},{70,6},{71,7},{72,8},{73... | collective-permute-start | bytes 24584 | tf_op jit(solution)/shard_map/ppermute | solution.py:419
  57.5 32.1 %copy-start.2 = (s32[22,4096]{1,0:T(8,128)S(1)}, s32[22,4096]{1,0:T(8,128)}, u32[]{:S(2)}) copy-start(s32[22,4096]{1,0:T(8,128)} %grid_ref.1) | copy-start | bytes 1081348
  57.5 32.1 %copy-start.3 = (f32[22,2048]{1,0:T(8,128)S(1)}, f32[22,2048]{1,0:T(8,128)}, u32[]{:S(2)}) copy-start(f32[22,2048]{1,0:T(8,128)} %freq_ref.1) | copy-start | bytes 540676
  57.5 32.1 %copy-start.5 = (f32[22,512]{1,0:T(8,128)S(1)}, f32[22,512]{1,0:T(8,128)}, u32[]{:S(2)}) copy-start(f32[22,512]{1,0:T(8,128)} %observed_ref.1) | copy-start | bytes 135172
  57.5 32.1 %copy-start.7 = (f32[2048]{0:T(1024)S(1)}, f32[2048]{0:T(1024)}, u32[]{:S(2)}) copy-start(f32[2048]{0:T(1024)} %param.16) | copy-start | bytes 24580
  57.5 32.1 %copy-start.8 = (f32[22]{0:T(128)S(1)}, f32[22]{0:T(128)}, u32[]{:S(2)}) copy-start(f32[22]{0:T(128)} %param.13) | copy-start | bytes 268
  58.4 3.7 %collective-permute-start.14 = (bf16[4,512]{1,0:T(4,128)(2,1)S(1)}, bf16[4,512]{1,0:T(4,128)(2,1)S(1)}, u32[]{:S(2)}, u32[]{:S(2)}) collective-permute-start(bf16[4,512]{1,0:T(4,128)(2,1)S(1)} %shard_map.97.refs_0_), channel_id=1, source_target_pairs={{0,2},{1,3},{2,4},{3,5},{4,6},{5,7},{6,8},{7,9},{8,10},{9,11},{10,... | collective-permute-start | bytes 12296 | tf_op jit(solution)/shard_map/ppermute | solution.py:297
  58.5 3.7 %collective-permute-start.18 = (bf16[4,512]{1,0:T(4,128)(2,1)S(1)}, bf16[4,512]{1,0:T(4,128)(2,1)S(1)}, u32[]{:S(2)}, u32[]{:S(2)}) collective-permute-start(bf16[4,512]{1,0:T(4,128)(2,1)S(1)} %shard_map.97.refs_0_), channel_id=1, source_target_pairs={{0,14},{1,15},{2,0},{3,1},{4,2},{5,3},{6,4},{7,5},{8,6},{9,7},{10,... | collective-permute-start | bytes 12296 | tf_op jit(solution)/shard_map/ppermute | solution.py:297
  62.1 3.7 %collective-permute-start.15 = (bf16[4,512]{1,0:T(4,128)(2,1)S(1)}, bf16[4,512]{1,0:T(4,128)(2,1)S(1)}, u32[]{:S(2)}, u32[]{:S(2)}) collective-permute-start(bf16[4,512]{1,0:T(4,128)(2,1)S(1)} %collective-permute-done.14.refs_1_), channel_id=1, source_target_pairs={{0,2},{1,3},{2,4},{3,5},{4,6},{5,7},{6,8},{7,9},{8,10},{9,11},{10,... | collective-permute-start | bytes 12296 | tf_op jit(solution)/shard_map/ppermute | solution.py:297
  62.1 3.7 %collective-permute-start.19 = (bf16[4,512]{1,0:T(4,128)(2,1)S(1)}, bf16[4,512]{1,0:T(4,128)(2,1)S(1)}, u32[]{:S(2)}, u32[]{:S(2)}) collective-permute-start(bf16[4,512]{1,0:T(4,128)(2,1)S(1)} %collective-permute-done.18.refs_7_), channel_id=1, source_target_pairs={{0,14},{1,15},{2,0},{3,1},{4,2},{5,3},{6,4},{7,5},{8,6},{9,7},{10,... | collective-permute-start | bytes 12296 | tf_op jit(solution)/shard_map/ppermute | solution.py:297
  65.8 3.7 %collective-permute-start.16 = (bf16[4,512]{1,0:T(4,128)(2,1)S(1)}, bf16[4,512]{1,0:T(4,128)(2,1)S(1)}, u32[]{:S(2)}, u32[]{:S(2)}) collective-permute-start(bf16[4,512]{1,0:T(4,128)(2,1)S(1)} %collective-permute-done.15.refs_2_), channel_id=1, source_target_pairs={{0,2},{1,3},{2,4},{3,5},{4,6},{5,7},{6,8},{7,9},{8,10},{9,11},{10,... | collective-permute-start | bytes 12296 | tf_op jit(solution)/shard_map/ppermute | solution.py:297
  65.8 3.7 %collective-permute-start.20 = (bf16[4,512]{1,0:T(4,128)(2,1)S(1)}, bf16[4,512]{1,0:T(4,128)(2,1)S(1)}, u32[]{:S(2)}, u32[]{:S(2)}) collective-permute-start(bf16[4,512]{1,0:T(4,128)(2,1)S(1)} %collective-permute-done.19.refs_6_), channel_id=1, source_target_pairs={{0,14},{1,15},{2,0},{3,1},{4,2},{5,3},{6,4},{7,5},{8,6},{9,7},{10,... | collective-permute-start | bytes 12296 | tf_op jit(solution)/shard_map/ppermute | solution.py:297
  69.5 3.7 %collective-permute-start.17 = (bf16[4,512]{1,0:T(4,128)(2,1)S(1)}, bf16[4,512]{1,0:T(4,128)(2,1)S(1)}, u32[]{:S(2)}, u32[]{:S(2)}) collective-permute-start(bf16[4,512]{1,0:T(4,128)(2,1)S(1)} %collective-permute-done.16.refs_3_), channel_id=1, source_target_pairs={{0,2},{1,3},{2,4},{3,5},{4,6},{5,7},{6,8},{7,9},{8,10},{9,11},{10,... | collective-permute-start | bytes 12296 | tf_op jit(solution)/shard_map/ppermute | solution.py:297
  73.2 3.9 %collective-permute-start.21 = (bf16[32,512]{1,0:T(8,128)(2,1)S(1)}, bf16[32,512]{1,0:T(8,128)(2,1)S(1)}, u32[]{:S(2)}, u32[]{:S(2)}) collective-permute-start(bf16[32,512]{1,0:T(8,128)(2,1)S(1)} %shard_map.98.refs_0_), channel_id=1, source_target_pairs={{0,16},{1,17},{2,18},{3,19},{4,20},{5,21},{6,22},{7,23},{8,24},{9,... | collective-permute-start | bytes 98312 | tf_op jit(solution)/shard_map/ppermute | solution.py:297
  73.3 4.4 %collective-permute-start.22 = (bf16[32,512]{1,0:T(8,128)(2,1)S(1)}, bf16[32,512]{1,0:T(8,128)(2,1)S(1)}, u32[]{:S(2)}, u32[]{:S(2)}) collective-permute-start(bf16[32,512]{1,0:T(8,128)(2,1)S(1)} %shard_map.98.refs_0_), channel_id=1, source_target_pairs={{0,32},{1,33},{2,34},{3,35},{4,36},{5,37},{6,38},{7,39},{8,40},{9,... | collective-permute-start | bytes 98312 | tf_op jit(solution)/shard_map/ppermute | solution.py:297
  75.2 4.0 %collective-permute-start.23 = (bf16[32,512]{1,0:T(8,128)(2,1)S(1)}, bf16[32,512]{1,0:T(8,128)(2,1)S(1)}, u32[]{:S(2)}, u32[]{:S(2)}) collective-permute-start(bf16[32,512]{1,0:T(8,128)(2,1)S(1)} %shard_map.98.refs_0_), channel_id=1, source_target_pairs={{0,48},{1,49},{2,50},{3,51},{4,52},{5,53},{6,54},{7,55},{8,56},{9,... | collective-permute-start | bytes 98312 | tf_op jit(solution)/shard_map/ppermute | solution.py:297
  79.2 20.6 %collective-permute-start.24 = (bf16[128,512]{1,0:T(8,128)(2,1)S(1)}, bf16[128,512]{1,0:T(8,128)(2,1)S(1)}, u32[]{:S(2)}, u32[]{:S(2)}) collective-permute-start(bf16[128,512]{1,0:T(8,128)(2,1)S(1)} %shard_map.99.refs_0_), channel_id=1, source_target_pairs={{0,1},{1,0},{2,3},{3,2},{4,5},{5,4},{6,7},{7,6},{8,9},{9,8},{10,11... | collective-permute-start | bytes 393224 | tf_op jit(solution)/shard_map/ppermute | solution.py:297
  105.9 19.0 %collective-permute-start.25 = (bf16[64,2048]{1,0:T(8,128)(2,1)S(1)}, bf16[64,2048]{1,0:T(8,128)(2,1)S(1)}, u32[]{:S(2)}, u32[]{:S(2)}) collective-permute-start(bf16[64,2048]{1,0:T(8,128)(2,1)S(1)} %get-tuple-element.62), channel_id=1, source_target_pairs={{0,64},{64,128},{128,192},{192,0},{1,65},{65,129},{129,193},{193,1... | collective-permute-start | bytes 786440 | tf_op jit(solution)/shard_map/ppermute | solution.py:452
  106.0 20.9 %collective-permute-start.26 = (bf16[64,2048]{1,0:T(8,128)(2,1)S(1)}, bf16[64,2048]{1,0:T(8,128)(2,1)S(1)}, u32[]{:S(2)}, u32[]{:S(2)}) collective-permute-start(bf16[64,2048]{1,0:T(8,128)(2,1)S(1)} %get-tuple-element.63), channel_id=1, source_target_pairs={{0,128},{64,192},{128,0},{192,64},{1,129},{65,193},{129,1},{193,65... | collective-permute-start | bytes 786440 | tf_op jit(solution)/shard_map/ppermute | solution.py:452
  106.1 20.8 %collective-permute-start.27 = (bf16[64,2048]{1,0:T(8,128)(2,1)S(1)}, bf16[64,2048]{1,0:T(8,128)(2,1)S(1)}, u32[]{:S(2)}, u32[]{:S(2)}) collective-permute-start(bf16[64,2048]{1,0:T(8,128)(2,1)S(1)} %get-tuple-element.64), channel_id=1, source_target_pairs={{0,192},{64,0},{128,64},{192,128},{1,193},{65,1},{129,65},{193,129... | collective-permute-start | bytes 786440 | tf_op jit(solution)/shard_map/ppermute | solution.py:452
  122.4 8.9 %collective-permute-start.28 = (bf16[64,2048]{1,0:T(8,128)(2,1)S(1)}, bf16[64,2048]{1,0:T(8,128)(2,1)S(1)}, u32[]{:S(2)}, u32[]{:S(2)}) collective-permute-start(bf16[64,2048]{1,0:T(8,128)(2,1)S(1)} %get-tuple-element.74), channel_id=1, source_target_pairs={{0,64},{64,128},{128,192},{192,0},{1,65},{65,129},{129,193},{193,1... | collective-permute-start | bytes 786440 | tf_op jit(solution)/shard_map/ppermute | solution.py:452
  123.0 13.3 %collective-permute-start.29 = (bf16[64,2048]{1,0:T(8,128)(2,1)S(1)}, bf16[64,2048]{1,0:T(8,128)(2,1)S(1)}, u32[]{:S(2)}, u32[]{:S(2)}) collective-permute-start(bf16[64,2048]{1,0:T(8,128)(2,1)S(1)} %get-tuple-element.75), channel_id=1, source_target_pairs={{0,128},{64,192},{128,0},{192,64},{1,129},{65,193},{129,1},{193,65... | collective-permute-start | bytes 786440 | tf_op jit(solution)/shard_map/ppermute | solution.py:452
  124.9 12.2 %collective-permute-start.30 = (bf16[64,2048]{1,0:T(8,128)(2,1)S(1)}, bf16[64,2048]{1,0:T(8,128)(2,1)S(1)}, u32[]{:S(2)}, u32[]{:S(2)}) collective-permute-start(bf16[64,2048]{1,0:T(8,128)(2,1)S(1)} %get-tuple-element.76), channel_id=1, source_target_pairs={{0,192},{64,0},{128,64},{192,128},{1,193},{65,1},{129,65},{193,129... | collective-permute-start | bytes 786440 | tf_op jit(solution)/shard_map/ppermute | solution.py:452

commit v3 on v2

v3 whole, which is shorter than its diff:
```python
import jax
import jax.numpy as jnp
from jax import lax
from jax.experimental import pallas as pl
from jax.experimental.pallas import tpu as pltpu
from jax.sharding import PartitionSpec as P

F32 = jnp.float32
BF16 = jnp.bfloat16
GRID = 21
DIM = 22
CORES = 2
DEPTHS = 8
WIDTHS = 4
LANES = 128
STRIPE = 24
ROW_CHUNK = 256
CAND_TILE = 256
CHUNKS = 8
PARTS = 2
VMEM_BYTES = 16 * 2**20
LOG2E = 1.4426950408889634
INV_TURN = 0.15915494309189535
SINE = (0.55535848, -0.91343016, 0.4493464, -0.09804192)


def params(limit=VMEM_BYTES):
    return pltpu.CompilerParams(vmem_limit_bytes=limit)


def whole():
    return pl.BlockSpec(memory_space=pltpu.VMEM)


def three_pieces(values):
    high = values.astype(BF16).astype(F32)
    rest = values - high
    middle = rest.astype(BF16).astype(F32)
    return high, middle, (rest - middle).astype(BF16).astype(F32)


def stack_pieces(scratch, values, tail):
    scratch[...] = jnp.zeros_like(scratch)
    for piece, part in enumerate(values):
        scratch[piece * STRIPE : piece * STRIPE + DIM, :] = part
    row = lax.broadcasted_iota(jnp.int32, (8, scratch.shape[1]), 0)
    block = jnp.zeros((8, scratch.shape[1]), F32)
    for index, line in enumerate(tail):
        block = jnp.where(row == index, line, block)
    scratch[3 * STRIPE : 3 * STRIPE + 8, :] = block


def prepare_kernel(*refs):
    sources, refs = refs[:7], refs[7:]
    (turns_ref, exponent_ref, levels_ref, inverse_ref, factor_ref), refs = refs[:5], refs[5:]
    (freq_ref, phase_ref, observed_ref, scale_ref, grid_ref), refs = refs[:5], refs[5:]
    wide, narrow, tall, sems = refs
    targets = (freq_ref, phase_ref, observed_ref, scale_ref, grid_ref, inverse_ref, factor_ref)
    copies = [
        pltpu.make_async_copy(
            source.at[:, : target.shape[1]], target, sems.at[index]
        )
        for index, (source, target) in enumerate(zip(sources, targets))
    ]
    for copy in copies:
        copy.start()
    for copy in copies[:5]:
        copy.wait()
    stack_pieces(
        wide,
        three_pieces(freq_ref[...] * (INV_TURN / (GRID - 1))),
        three_pieces(phase_ref[...] * INV_TURN),
    )
    for start in range(0, wide.shape[1], 512):
        turns_ref[start : start + 512, :] = wide[:, start : start + 512].T.astype(BF16)
    scale = jnp.broadcast_to(scale_ref[...], (DIM, DIM))
    line = lax.broadcasted_iota(jnp.int32, (DIM, DIM), 0)
    lane = lax.broadcasted_iota(jnp.int32, (DIM, DIM), 1)
    scale = jnp.sum(jnp.where(line == lane, scale, 0.0), axis=1, keepdims=True)
    squares = scale * scale
    observed = observed_ref[...]
    ones = jnp.ones((1, narrow.shape[1]), F32)
    norm = jnp.sum(observed * observed * squares, axis=0, keepdims=True) * (-0.5 * LOG2E)
    stack_pieces(
        narrow,
        three_pieces(observed * squares * (LOG2E / (GRID - 1))),
        three_pieces(norm) + (ones, ones, ones),
    )
    exponent_ref[...] = narrow[...].T.astype(BF16)
    levels = grid_ref[...].astype(F32)
    ones = jnp.ones((1, tall.shape[1]), F32)
    norm = jnp.sum(levels * levels * squares, axis=0, keepdims=True) * (
        -0.5 * LOG2E / (GRID - 1) ** 2
    )
    stack_pieces(tall, (levels, levels, levels), (ones, ones, ones) + three_pieces(norm))
    levels_ref[...] = tall[...].astype(BF16)
    for copy in copies[5:]:
        copy.wait()


def prepare(frequencies, phases, observed, inv_length, grid_coords, diag_inv, factor_rows):
    feats, obs, cands = frequencies.shape[1], observed.shape[1], grid_coords.shape[1]
    arrays = (frequencies, phases[None, :], observed, inv_length[None, :], grid_coords)
    earlier = factor_rows.shape[1] - diag_inv.shape[1]
    return pl.pallas_call(
        prepare_kernel,
        out_shape=(
            jax.ShapeDtypeStruct((feats, LANES), BF16),
            jax.ShapeDtypeStruct((obs, LANES), BF16),
            jax.ShapeDtypeStruct((LANES, cands), BF16),
            jax.ShapeDtypeStruct(diag_inv.shape, F32),
            jax.ShapeDtypeStruct((factor_rows.shape[0], earlier), F32),
        ),
        in_specs=[pl.BlockSpec(memory_space=pl.ANY)] * 7,
        out_specs=(whole(),) * 5,
        scratch_shapes=[pltpu.VMEM(array.shape, array.dtype) for array in arrays]
        + [
            pltpu.VMEM((LANES, feats), F32),
            pltpu.VMEM((LANES, obs), F32),
            pltpu.VMEM((LANES, cands), F32),
            pltpu.SemaphoreType.DMA((7,)),
        ],
        compiler_params=params(44 * 2**20),
        cost_estimate=pl.CostEstimate(flops=10**7, transcendentals=0, bytes_accessed=8 * 2**20),
        name="prepare",
    )(*arrays, diag_inv, factor_rows)


def cosine(turns):
    near = turns - jnp.round(turns)
    square = near * near
    poly = ((SINE[3] * square + SINE[2]) * square + SINE[1]) * square + SINE[0]
    sine = near * poly
    return (0.015625 - sine * sine).astype(BF16)


def tile_kernel(turns_ref, exponent_ref, levels_ref, features_ref, kernel_ref):
    levels = levels_ref[...]
    for start in range(0, turns_ref.shape[0], ROW_CHUNK):
        rows = slice(start, start + ROW_CHUNK)
        turns = jnp.dot(turns_ref[rows, :], levels, preferred_element_type=F32)
        features_ref[rows, :] = cosine(turns)
    for start in range(0, exponent_ref.shape[0], ROW_CHUNK):
        rows = slice(start, start + ROW_CHUNK)
        exponent = jnp.dot(exponent_ref[rows, :], levels, preferred_element_type=F32)
        kernel_ref[rows, :] = jnp.exp2(exponent).astype(BF16)


def tiles(turns, exponent, levels, chunk):
    feats, obs = turns.shape[0], exponent.shape[0]
    cands = levels.shape[1] // CHUNKS
    steps = cands // CAND_TILE
    return pl.pallas_call(
        tile_kernel,
        out_shape=(
            jax.ShapeDtypeStruct((feats, cands), BF16),
            jax.ShapeDtypeStruct((obs, cands), BF16),
        ),
        grid=(steps,),
        in_specs=[
            whole(),
            whole(),
            pl.BlockSpec((LANES, CAND_TILE), lambda i: (0, i + chunk * steps)),
        ],
        out_specs=(
            pl.BlockSpec((feats, CAND_TILE), lambda i: (0, i)),
            pl.BlockSpec((obs, CAND_TILE), lambda i: (0, i)),
        ),
        compiler_params=params(),
        cost_estimate=pl.CostEstimate(
            flops=24 * (feats + obs) * cands,
            transcendentals=obs * cands,
            bytes_accessed=2 * (feats + obs) * cands,
        ),
    )(turns, exponent, levels)


def order_kernel(near_ref, far_ref, out_ref):
    rows, half = out_ref.shape[0], near_ref.shape[0] // WIDTHS
    block = rows // WIDTHS
    shard = rows // (WIDTHS * DEPTHS * CORES)
    across, mine = lax.axis_index("rows"), lax.axis_index("cand")
    row = lax.broadcasted_iota(jnp.int32, (block, block), 0)
    column = lax.broadcasted_iota(jnp.int32, (block, block), 1)
    offset = (row // shard) ^ (mine & (DEPTHS * CORES - 1))
    source = ((offset & (CORES - 1)) * DEPTHS + offset // CORES) * shard + (row & (shard - 1))
    chosen = (source == column).astype(F32).astype(BF16)
    for target in range(WIDTHS):
        width = ((across + target) & (WIDTHS - 1)) ^ (mine // (DEPTHS * CORES))
        held = pl.ds(pl.multiple_of(width * half, half), half)
        lines = jnp.concatenate([near_ref[held, :], far_ref[held, :]], axis=0)
        out_ref[target * block : (target + 1) * block, :] = jnp.dot(
            chosen, lines, preferred_element_type=F32
        ).astype(BF16)


def in_order(near, far):
    rows, columns = 2 * near.shape[0], near.shape[1]
    return pl.pallas_call(
        order_kernel,
        out_shape=jax.ShapeDtypeStruct((rows, columns), BF16),
        in_specs=[whole(), whole()],
        out_specs=whole(),
        compiler_params=params(),
        cost_estimate=pl.CostEstimate(
            flops=2 * rows * rows * columns, transcendentals=0, bytes_accessed=4 * rows * columns
        ),
    )(near, far)


def prior_kernel(coef_ref, *refs):
    *features, out_ref = refs
    cands = features[0].shape[1]
    for chunk, feature_ref in enumerate(features):
        out_ref[:, chunk * cands : (chunk + 1) * cands] = jnp.dot(
            coef_ref[...], feature_ref[...], preferred_element_type=F32
        )


def cross_kernel(weight_ref, prior_ref, *refs):
    kernels, outs = refs[:-WIDTHS], refs[-WIDTHS:]
    block = weight_ref.shape[0] // WIDTHS
    cands = kernels[0].shape[1]
    for chunk, kernel_ref in enumerate(kernels):
        cols = slice(chunk * cands, (chunk + 1) * cands)
        total = prior_ref[:, cols] + jnp.dot(
            weight_ref[...], kernel_ref[...], preferred_element_type=F32
        )
        for target, out in enumerate(outs):
            rows = slice(target * block, (target + 1) * block)
            out[:, cols] = total[rows].astype(out.dtype)


def prior_product(coefs, features):
    rows, cands = coefs.shape[0], len(features) * features[0].shape[1]
    feats = coefs.shape[1]
    return pl.pallas_call(
        prior_kernel,
        out_shape=jax.ShapeDtypeStruct((rows, cands), F32),
        in_specs=[whole()] * (1 + len(features)),
        out_specs=whole(),
        compiler_params=params(),
        cost_estimate=pl.CostEstimate(
            flops=2 * rows * feats * cands, transcendentals=0, bytes_accessed=2 * feats * cands
        ),
    )(coefs, *features)


def cross_product(weights, prior, kernels):
    rows, cands = prior.shape
    obs = weights.shape[1]
    shape = (rows // WIDTHS, cands)
    out_shapes = (jax.ShapeDtypeStruct(shape, F32),) + (jax.ShapeDtypeStruct(shape, BF16),) * (
        WIDTHS - 1
    )
    return pl.pallas_call(
        cross_kernel,
        out_shape=out_shapes,
        in_specs=[whole()] * (2 + len(kernels)),
        out_specs=(whole(),) * WIDTHS,
        compiler_params=params(),
        cost_estimate=pl.CostEstimate(
            flops=2 * rows * obs * cands, transcendentals=0, bytes_accessed=8 * rows * cands
        ),
    )(weights, prior, *kernels)


def total_kernel(*refs):
    *parts, out_ref = refs
    cands = parts[0].shape[1]
    for part in range(len(parts) // WIDTHS):
        own, *others = parts[part * WIDTHS : (part + 1) * WIDTHS]
        total = own[...]
        for other in others:
            total = total + other[...].astype(F32)
        out_ref[:, part * cands : (part + 1) * cands] = total


def total(parts):
    flat = [block for part in parts for block in part]
    shape = (flat[0].shape[0], len(parts) * flat[0].shape[1])
    return pl.pallas_call(
        total_kernel,
        out_shape=jax.ShapeDtypeStruct(shape, F32),
        in_specs=[whole()] * len(flat),
        out_specs=whole(),
        compiler_params=params(),
        cost_estimate=pl.CostEstimate(
            flops=3 * shape[0] * shape[1], transcendentals=0, bytes_accessed=14 * shape[0] * shape[1]
        ),
        name="total",
    )(*flat)


def exchange_pairs(mask):
    devices = WIDTHS * DEPTHS * CORES
    return [(i, i ^ mask) for i in range(devices)]


def stack_kernel(*refs):
    *pieces, out_ref, rows = refs
    count = pieces[0].shape[0]
    if count % 16 == 0:
        for index, piece in enumerate(pieces):
            out_ref[index * count : (index + 1) * count, :] = piece[...]
        return
    for index, piece in enumerate(pieces):
        rows[index * count : (index + 1) * count, :] = piece[...].astype(F32)
    out_ref[...] = rows[...].astype(BF16)


def stack(pieces):
    shape = (len(pieces) * pieces[0].shape[0], pieces[0].shape[1])
    return pl.pallas_call(
        stack_kernel,
        out_shape=jax.ShapeDtypeStruct(shape, BF16),
        in_specs=[whole()] * len(pieces),
        out_specs=whole(),
        scratch_shapes=[pltpu.VMEM(shape, F32)],
        compiler_params=params(),
        cost_estimate=pl.CostEstimate(
            flops=0, transcendentals=0, bytes_accessed=4 * shape[0] * shape[1]
        ),
    )(*pieces)


def spread(piece, at_once):
    def swap(held, pairs):
        return lax.ppermute(held, "cand", pairs)

    held = piece
    for hop in (1, 2, 4):
        other = swap(held, exchange_pairs(hop * CORES))
        held = stack([held, other])
    step = DEPTHS * CORES
    if at_once:
        others = [swap(held, exchange_pairs(hop * step)) for hop in range(1, WIDTHS)]
        near = stack([held] + others)
    else:
        near = stack([held, swap(held, exchange_pairs(step))])
        near = stack([near, swap(near, exchange_pairs(2 * step))])
    return near, swap(near, exchange_pairs(1))


def exact_lines(left, lines):
    rows = left.shape[0]
    lines[...] = jnp.zeros_like(lines)
    for index, piece in enumerate(three_pieces(left)):
        lines[index * rows : (index + 1) * rows, :] = piece
    return lines[...].astype(BF16)


def exact_dot(lines, rows, right):
    total = None
    for piece, count in zip(three_pieces(right)[::-1], (1, 2, 3)):
        product = jnp.dot(lines, piece.astype(BF16), preferred_element_type=F32)
        for index in reversed(range(count)):
            term = product[index * rows : (index + 1) * rows]
            total = term if total is None else total + term
    return total


def solve_kernel(
    section, whitened_ref, inverse_ref, factor_ref, carried_ref, weights_ref, *rest
):
    *update_ref, solved_ref, lines = rest
    count, width = whitened_ref.shape
    active = lax.axis_index("rows") == section

    @pl.when(active)
    def _():
        remaining = whitened_ref[...]
        if carried_ref is not None:
            remaining = remaining - carried_ref[:, section * width : (section + 1) * width]
        solved = exact_dot(exact_lines(remaining, lines), count, inverse_ref[...])
        solved_ref[...] = solved.astype(BF16)
        if section > 0:
            left = exact_lines(solved, lines)

            @pl.loop(0, section)
            def _(earlier):
                cols = pl.ds(pl.multiple_of(earlier * width, width), width)
                update = exact_dot(left, count, factor_ref[:, cols])
                if carried_ref is not None:
                    update = update + carried_ref[:, cols]
                update_ref[0][:, cols] = update

    if weights_ref is not None:
        @pl.when(jnp.logical_not(active))
        def _():
            solved_ref[...] = weights_ref[...]


def solve(section, whitened, carried, weights, diag_inv, factor_rows):
    count, width = whitened.shape
    out_shape = [jax.ShapeDtypeStruct((count, width), BF16)]
    if section > 0:
        out_shape.insert(0, jax.ShapeDtypeStruct((count, section * width), F32))
    first = carried is None

    def kernel(whitened_ref, inverse_ref, factor_ref, *refs):
        if first:
            refs = (None, None) + refs
        solve_kernel(section, whitened_ref, inverse_ref, factor_ref, *refs)

    held = [] if first else [carried, weights]
    columns = (section + 1) * width
    results = pl.pallas_call(
        kernel,
        out_shape=out_shape,
        in_specs=[whole()] * (3 + len(held)),
        out_specs=[whole()] * len(out_shape),
        scratch_shapes=[pltpu.VMEM((16, width), F32)],
        compiler_params=params(),
        cost_estimate=pl.CostEstimate(
            flops=2 * 36 * width * columns, transcendentals=0, bytes_accessed=4 * width * columns
        ),
    )(whitened, diag_inv, factor_rows, *held)
    return results if section > 0 else (None, results[0])


def solve_chain(whitened, factor_rows, diag_inv):
    sections = lax.axis_size("rows")
    carried = weights = None
    for section in reversed(range(sections)):
        carried, weights = solve(section, whitened, carried, weights, diag_inv, factor_rows)
        if section > 0:
            carried = lax.ppermute(carried, "rows", [(section, section - 1)])
    return weights


def body(
    whitened,
    factor_rows,
    diag_inv,
    observed,
    inv_length,
    grid_coords,
    frequencies,
    phases,
    prior_coef,
):
    turns, exponent, levels, inverse, factor = prepare(
        frequencies, phases, observed, inv_length, grid_coords, diag_inv, factor_rows
    )
    coef_near, coef_far = spread(prior_coef, False)
    weights = solve_chain(whitened, factor, inverse)
    weight_near, weight_far = spread(weights, True)
    made = [tiles(turns, exponent, levels, chunk) for chunk in range(CHUNKS)]
    coefs = in_order(coef_near, coef_far)
    solved = in_order(weight_near, weight_far)
    rows = lax.axis_size("rows")
    each = CHUNKS // PARTS
    parts = []
    for part in range(PARTS):
        mine = made[part * each : (part + 1) * each]
        prior = prior_product(coefs, [m[0] for m in mine])
        own, *away = cross_product(solved, prior, [m[1] for m in mine])
        arrived = []
        for shift, block in enumerate(away, 1):
            pairs = [(i, (i + shift) % rows) for i in range(rows)]
            arrived.append(lax.ppermute(block, "rows", pairs))
        parts.append([own] + arrived)
    return total(parts).T


def solution(mesh):
    in_specs = (
        P("cand", "rows"),
        P("rows", None),
        P("rows", None),
        P(None, "rows"),
        P(),
        P(None, "cand"),
        P(None, "rows"),
        P("rows"),
        P("cand", "rows"),
    )
    out_specs = P("cand", "rows")

    return jax.shard_map(body, mesh=mesh, in_specs=in_specs, out_specs=out_specs, check_vma=False)
```

time: 139 us -> 133 us (0.957)
  Pallas kernels: 38.3 us -> 30.1 us
  waiting for transfers between devices: 40.1 us -> 47.9 us
  starting transfers between devices: 54 us -> 52 us
    pallas_call x8 -> x9, Pallas kernels: 16.6 us -> 7.79 us  [the longest x2 4.68 us: prior_product(): pl.pallas_call(prior_kernel, out_shape=jax.ShapeDtypeStruct((rows, cands)...]
    ppermute x6, waiting for transfers between devices: 10.1 us -> 16 us  [body(): arrived.append(lax.ppermute(block, 'rows', pairs))]
    ppermute x22 -> x13, starting transfers between devices: 44.2 us -> 41.8 us  [swap(): return lax.ppermute(held, 'cand', pairs)]
    pallas_call x1, Pallas kernels: 0.56 us -> 2.51 us  [prepare(): pl.pallas_call(prepare_kernel, out_shape=(jax.ShapeDtypeStruct((feats, LA...]
    unnamed x18 -> x16, local copies, waits for them, and re-layouts: 4.15 us -> 2.88 us
    ppermute x22 -> x13, waiting for transfers between devices: 20.8 us -> 21.3 us  [swap(): return lax.ppermute(held, 'cand', pairs)]
  transfers between devices with their start and end apart: 31 -> 22, of which waited for: 17 -> 14; matrix products, arithmetic and copies ran while one was open for 0% -> 0% of each run, Pallas kernels for 24% -> 19%
where the time goes in v3:
time: 133 us
  starting transfers between devices  52 us (39%)
  waiting for transfers between devices  47.9 us (36%)
  Pallas kernels  30.1 us (23%)
  local copies, waits for them, and re-layouts  2.88 us (2%)
    ppermute x13, starting transfers between devices, swap(): return lax.ppermute(held, 'cand', pairs)  41.8 us
    ppermute x13, waiting for transfers between devices, swap(): return lax.ppermute(held, 'cand', pairs)  21.3 us
    pallas_call x8, Pallas kernels, tiles(): pl.pallas_call(tile_kernel, out_shape=(jax.ShapeDtypeStruct((feats, cands...  19 us
    ppermute x6, waiting for transfers between devices, body(): arrived.append(lax.ppermute(block, 'rows', pairs))  16 us
    ppermute x3, waiting for transfers between devices, solve_chain(): carried = lax.ppermute(carried, 'rows', [(section, section - 1)])  10.5 us
    ppermute x6, starting transfers between devices, body(): arrived.append(lax.ppermute(block, 'rows', pairs))  7.54 us
    pallas_call x2, Pallas kernels, prior_product(): pl.pallas_call(prior_kernel, out_shape=jax.ShapeDtypeStruct((rows, cands)...  4.68 us
    unnamed x16, local copies, waits for them, and re-layouts  2.88 us
  transfers between devices with their start and end apart: 22, of which 14 were waited for; matrix products, arithmetic and copies ran while one was open for 0% of the time, Pallas kernels for 19%

profile of v3, /device:TPU:1, one launch (start us, length us, event | category | flops | bytes accessed | tf_op | source)
XLA Modules:
  0.0 133.2 jit_solution(14487217832256579282)
XLA Ops:
  0.0 2.5 %collective-permute-start.10 = (bf16[4,2048]{1,0:T(4,128)(2,1)}, bf16[4,2048]{1,0:T(4,128)(2,1)S(1)}, u32[]{:S(2)}, u32[]{:S(2)}) collective-permute-start(bf16[4,2048]{1,0:T(4,128)(2,1)} %refs_0_.3), channel_id=1, source_target_pairs={{0,2},{1,3},{2,0},{3,1},{4,6},{5,7},{6,4},{7,5},{8,10},{9,11},{10,... | collective-permute-start | bytes 49160 | tf_op jit(solution)/shard_map/ppermute | solution.py:329
  2.6 1.3 %collective-permute-done.10.refs_1_ = bf16[4,2048]{1,0:T(4,128)(2,1)S(1)} collective-permute-done((bf16[4,2048]{1,0:T(4,128)(2,1)}, bf16[4,2048]{1,0:T(4,128)(2,1)S(1)}, u32[]{:S(2)}, u32[]{:S(2)}) %collective-permute-start.10) | collective-permute-done | bytes 16416 | tf_op jit(solution)/shard_map/ppermute | solution.py:329
  3.9 0.7 copy-done.5
  4.6 3.1 %collective-permute-start.11 = (bf16[8,2048]{1,0:T(8,128)(2,1)S(1)}, bf16[8,2048]{1,0:T(8,128)(2,1)S(1)}, u32[]{:S(2)}, u32[]{:S(2)}) collective-permute-start(bf16[8,2048]{1,0:T(8,128)(2,1)S(1)} %shard_map.100.refs_0_), channel_id=1, source_target_pairs={{0,4},{1,5},{2,6},{3,7},{4,0},{5,1},{6,2},{7,3},{8,12},{9,13},{10,... | collective-permute-start | bytes 98312 | tf_op jit(solution)/shard_map/ppermute | solution.py:329
  7.7 1.3 collective-permute-done.11.refs_1_
  9.0 6.1 %collective-permute-start.12 = (bf16[16,2048]{1,0:T(8,128)(2,1)S(1)}, bf16[16,2048]{1,0:T(8,128)(2,1)S(1)}, u32[]{:S(2)}, u32[]{:S(2)}) collective-permute-start(bf16[16,2048]{1,0:T(8,128)(2,1)S(1)} %shard_map.101.refs_0_), channel_id=1, source_target_pairs={{0,8},{1,9},{2,10},{3,11},{4,12},{5,13},{6,14},{7,15},{8,0},{9,1},... | collective-permute-start | bytes 196616 | tf_op jit(solution)/shard_map/ppermute | solution.py:329
  15.1 1.8 %collective-permute-done.12.refs_1_ = bf16[16,2048]{1,0:T(8,128)(2,1)S(1)} collective-permute-done((bf16[16,2048]{1,0:T(8,128)(2,1)S(1)}, bf16[16,2048]{1,0:T(8,128)(2,1)S(1)}, u32[]{:S(2)}, u32[]{:S(2)}) %collective-permute-start.12) | collective-permute-done | bytes 65568 | tf_op jit(solution)/shard_map/ppermute | solution.py:329
  16.9 1.3 collective-permute-start.13
  18.2 2.9 %collective-permute-done.13.refs_1_ = bf16[32,2048]{1,0:T(8,128)(2,1)S(1)} collective-permute-done((bf16[32,2048]{1,0:T(8,128)(2,1)S(1)}, bf16[32,2048]{1,0:T(8,128)(2,1)S(1)}, u32[]{:S(2)}, u32[]{:S(2)}) %collective-permute-start.13) | collective-permute-done | bytes 131104 | tf_op jit(solution)/shard_map/ppermute | solution.py:329
  21.2 2.5 %collective-permute-start.14 = (bf16[64,2048]{1,0:T(8,128)(2,1)S(1)}, bf16[64,2048]{1,0:T(8,128)(2,1)S(1)}, u32[]{:S(2)}, u32[]{:S(2)}) collective-permute-start(bf16[64,2048]{1,0:T(8,128)(2,1)S(1)} %shard_map.103.refs_0_), channel_id=1, source_target_pairs={{0,32},{1,33},{2,34},{3,35},{4,36},{5,37},{6,38},{7,39},{8,40},{9,... | collective-permute-start | bytes 786440 | tf_op jit(solution)/shard_map/ppermute | solution.py:329
  23.7 5.7 %collective-permute-done.14.refs_1_ = bf16[64,2048]{1,0:T(8,128)(2,1)S(1)} collective-permute-done((bf16[64,2048]{1,0:T(8,128)(2,1)S(1)}, bf16[64,2048]{1,0:T(8,128)(2,1)S(1)}, u32[]{:S(2)}, u32[]{:S(2)}) %collective-permute-start.14) | collective-permute-done | bytes 262176 | tf_op jit(solution)/shard_map/ppermute | solution.py:329
  29.4 7.2 %collective-permute-start.15 = (bf16[128,2048]{1,0:T(8,128)(2,1)S(1)}, bf16[128,2048]{1,0:T(8,128)(2,1)S(1)}, u32[]{:S(2)}, u32[]{:S(2)}) collective-permute-start(bf16[128,2048]{1,0:T(8,128)(2,1)S(1)} %shard_map.104.near_ref), channel_id=1, source_target_pairs={{0,1},{1,0},{2,3},{3,2},{4,5},{5,4},{6,7},{7,6},{8,9},{9,8},{10,11... | collective-permute-start | bytes 1572872 | tf_op jit(solution)/shard_map/ppermute | solution.py:329
  36.6 0.8 copy-done.4
  37.4 0.7 copy-done.6
  38.1 0.7 copy-done.7
  38.8 2.5 %prepare.1 = (bf16[2048,128]{1,0:T(8,128)(2,1)S(1)}, bf16[512,128]{1,0:T(8,128)(2,1)S(1)}, bf16[128,4096]{1,0:T(8,128)(2,1)S(1)}, f32[512,512]{1,0:T(8,128)S(1)}, f32[512,1536]{1,0:T(8,128)S(1)}) custom-call(f32[22,2048]{1,0:T(8,128)S(1)} %copy-done.2, f32[1,2048]{1,0:T(1,128)S(1)} %bitcast.3, f32[22,512]{1,0:T(8,128)S(1)} %copy-done.4, ...), custom_call_target="tpu_custom_call" | custom-call | flops 10000000 | bytes 8388608 | tf_op jit(solution)/shard_map/prepare/pallas_call | solution.py:105
  41.3 0.7 collective-permute-start
  42.0 0.7 collective-permute-start.1
  42.7 1.3 collective-permute-start.2
  44.0 10.5 %collective-permute-done.2.refs_0_ = f32[4,512]{1,0:T(4,128)S(1)} collective-permute-done((f32[4,512]{1,0:T(4,128)S(1)}, f32[4,512]{1,0:T(4,128)S(1)}, u32[]{:S(2)}, u32[]{:S(2)}) %collective-permute-start.2) | collective-permute-done | bytes 8224 | tf_op jit(solution)/shard_map/ppermute | solution.py:428
  55.3 2.3 %collective-permute-done.3.refs_1_ = bf16[4,512]{1,0:T(4,128)(2,1)S(1)} collective-permute-done((bf16[4,512]{1,0:T(4,128)(2,1)S(1)}, bf16[4,512]{1,0:T(4,128)(2,1)S(1)}, u32[]{:S(2)}, u32[]{:S(2)}) %collective-permute-start.3) | collective-permute-done | bytes 4128 | tf_op jit(solution)/shard_map/ppermute | solution.py:329
  57.6 2.2 %collective-permute-start.4 = (bf16[8,512]{1,0:T(8,128)(2,1)S(1)}, bf16[8,512]{1,0:T(8,128)(2,1)S(1)}, u32[]{:S(2)}, u32[]{:S(2)}) collective-permute-start(bf16[8,512]{1,0:T(8,128)(2,1)S(1)} %shard_map.95.refs_0_), channel_id=1, source_target_pairs={{0,4},{1,5},{2,6},{3,7},{4,0},{5,1},{6,2},{7,3},{8,12},{9,13},{10,... | collective-permute-start | bytes 24584 | tf_op jit(solution)/shard_map/ppermute | solution.py:329
  59.8 1.2 collective-permute-done.4.refs_1_
  61.0 5.9 %collective-permute-start.5 = (bf16[16,512]{1,0:T(8,128)(2,1)S(1)}, bf16[16,512]{1,0:T(8,128)(2,1)S(1)}, u32[]{:S(2)}, u32[]{:S(2)}) collective-permute-start(bf16[16,512]{1,0:T(8,128)(2,1)S(1)} %shard_map.96.refs_0_), channel_id=1, source_target_pairs={{0,8},{1,9},{2,10},{3,11},{4,12},{5,13},{6,14},{7,15},{8,0},{9,1},... | collective-permute-start | bytes 49160 | tf_op jit(solution)/shard_map/ppermute | solution.py:329
  66.8 1.1 collective-permute-done.5.refs_1_
  68.0 3.1 %collective-permute-start.8 = (bf16[32,512]{1,0:T(8,128)(2,1)S(1)}, bf16[32,512]{1,0:T(8,128)(2,1)S(1)}, u32[]{:S(2)}, u32[]{:S(2)}) collective-permute-start(bf16[32,512]{1,0:T(8,128)(2,1)S(1)} %shard_map.97.refs_0_), channel_id=1, source_target_pairs={{0,48},{1,49},{2,50},{3,51},{4,52},{5,53},{6,54},{7,55},{8,56},{9,... | collective-permute-start | bytes 98312 | tf_op jit(solution)/shard_map/ppermute | solution.py:329
  71.6 1.0 collective-permute-done.8.refs_3_
  72.6 2.7 %collective-permute-done.7.refs_2_ = bf16[32,512]{1,0:T(8,128)(2,1)S(1)} collective-permute-done((bf16[32,512]{1,0:T(8,128)(2,1)S(1)}, bf16[32,512]{1,0:T(8,128)(2,1)S(1)}, u32[]{:S(2)}, u32[]{:S(2)}) %collective-permute-start.7) | collective-permute-done | bytes 32800 | tf_op jit(solution)/shard_map/ppermute | solution.py:329
  75.3 7.1 %collective-permute-start.9 = (bf16[128,512]{1,0:T(8,128)(2,1)S(1)}, bf16[128,512]{1,0:T(8,128)(2,1)S(1)}, u32[]{:S(2)}, u32[]{:S(2)}) collective-permute-start(bf16[128,512]{1,0:T(8,128)(2,1)S(1)} %shard_map.98.near_ref), channel_id=1, source_target_pairs={{0,1},{1,0},{2,3},{3,2},{4,5},{5,4},{6,7},{7,6},{8,9},{9,8},{10,11... | collective-permute-start | bytes 393224 | tf_op jit(solution)/shard_map/ppermute | solution.py:329
  82.5 2.4 %shard_map.115 = (bf16[2048,512]{1,0:T(8,128)(2,1)S(1)}, bf16[512,512]{1,0:T(8,128)(2,1)S(1)}) custom-call(bf16[2048,128]{1,0:T(8,128)(2,1)S(1)} %get-tuple-element.48.turns_ref, bf16[512,128]{1,0:T(8,128)(2,1)S(1)} %get-tuple-element.49.exponent_ref, bf16[128,4096]{1,0:T(8,128)(2,1)S(1)} %get-tuple-element.50.levels_ref), custom_call_target="tpu_custom_call" | custom-call | flops 31457280 | bytes 2621440 | tf_op jit(solution)/shard_map/pallas_call | solution.py:153
  84.8 2.4 %shard_map.114 = (bf16[2048,512]{1,0:T(8,128)(2,1)S(1)}, bf16[512,512]{1,0:T(8,128)(2,1)S(1)}) custom-call(bf16[2048,128]{1,0:T(8,128)(2,1)S(1)} %get-tuple-element.48.turns_ref, bf16[512,128]{1,0:T(8,128)(2,1)S(1)} %get-tuple-element.49.exponent_ref, bf16[128,4096]{1,0:T(8,128)(2,1)S(1)} %get-tuple-element.50.levels_ref), custom_call_target="tpu_custom_call" | custom-call | flops 31457280 | bytes 2621440 | tf_op jit(solution)/shard_map/pallas_call | solution.py:153
  87.2 2.4 %shard_map.113 = (bf16[2048,512]{1,0:T(8,128)(2,1)S(1)}, bf16[512,512]{1,0:T(8,128)(2,1)S(1)}) custom-call(bf16[2048,128]{1,0:T(8,128)(2,1)S(1)} %get-tuple-element.48.turns_ref, bf16[512,128]{1,0:T(8,128)(2,1)S(1)} %get-tuple-element.49.exponent_ref, bf16[128,4096]{1,0:T(8,128)(2,1)S(1)} %get-tuple-element.50.levels_ref), custom_call_target="tpu_custom_call" | custom-call | flops 31457280 | bytes 2621440 | tf_op jit(solution)/shard_map/pallas_call | solution.py:153
  89.6 2.4 %shard_map.112 = (bf16[2048,512]{1,0:T(8,128)(2,1)S(1)}, bf16[512,512]{1,0:T(8,128)(2,1)S(1)}) custom-call(bf16[2048,128]{1,0:T(8,128)(2,1)S(1)} %get-tuple-element.48.turns_ref, bf16[512,128]{1,0:T(8,128)(2,1)S(1)} %get-tuple-element.49.exponent_ref, bf16[128,4096]{1,0:T(8,128)(2,1)S(1)} %get-tuple-element.50.levels_ref), custom_call_target="tpu_custom_call" | custom-call | flops 31457280 | bytes 2621440 | tf_op jit(solution)/shard_map/pallas_call | solution.py:153
  92.7 2.4 %shard_map.116.prior_ref = f32[256,2048]{1,0:T(8,128)S(1)} custom-call(bf16[256,2048]{1,0:T(8,128)(2,1)S(1)} %shard_map.105.coef_ref, bf16[2048,512]{1,0:T(8,128)(2,1)S(1)} %get-tuple-element.63.refs_0_, bf16[2048,512]{1,0:T(8,128)(2,1)S(1)} %get-tuple-element.64.refs_1_, bf16[2048,512]{1,0:T(8,128)(2,1)S(1)} %get-tuple-element.65.refs_2_, ...), custom_call_target="tpu_custom_call" | custom-call | flops 2147483648 | bytes 8388608 | tf_op jit(solution)/shard_map/pallas_call | solution.py:237
  95.1 0.7 shard_map.117
  96.1 2.4 %shard_map.109 = (bf16[2048,512]{1,0:T(8,128)(2,1)S(1)}, bf16[512,512]{1,0:T(8,128)(2,1)S(1)}) custom-call(bf16[2048,128]{1,0:T(8,128)(2,1)S(1)} %get-tuple-element.48.turns_ref, bf16[512,128]{1,0:T(8,128)(2,1)S(1)} %get-tuple-element.49.exponent_ref, bf16[128,4096]{1,0:T(8,128)(2,1)S(1)} %get-tuple-element.50.levels_ref), custom_call_target="tpu_custom_call" | custom-call | flops 31457280 | bytes 2621440 | tf_op jit(solution)/shard_map/pallas_call | solution.py:153
  98.5 2.4 %shard_map.108 = (bf16[2048,512]{1,0:T(8,128)(2,1)S(1)}, bf16[512,512]{1,0:T(8,128)(2,1)S(1)}) custom-call(bf16[2048,128]{1,0:T(8,128)(2,1)S(1)} %get-tuple-element.48.turns_ref, bf16[512,128]{1,0:T(8,128)(2,1)S(1)} %get-tuple-element.49.exponent_ref, bf16[128,4096]{1,0:T(8,128)(2,1)S(1)} %get-tuple-element.50.levels_ref), custom_call_target="tpu_custom_call" | custom-call | flops 31457280 | bytes 2621440 | tf_op jit(solution)/shard_map/pallas_call | solution.py:153
  100.9 2.4 %shard_map.107 = (bf16[2048,512]{1,0:T(8,128)(2,1)S(1)}, bf16[512,512]{1,0:T(8,128)(2,1)S(1)}) custom-call(bf16[2048,128]{1,0:T(8,128)(2,1)S(1)} %get-tuple-element.48.turns_ref, bf16[512,128]{1,0:T(8,128)(2,1)S(1)} %get-tuple-element.49.exponent_ref, bf16[128,4096]{1,0:T(8,128)(2,1)S(1)} %get-tuple-element.50.levels_ref), custom_call_target="tpu_custom_call" | custom-call | flops 31457280 | bytes 2621440 | tf_op jit(solution)/shard_map/pallas_call | solution.py:153
  103.3 2.4 %shard_map.106 = (bf16[2048,512]{1,0:T(8,128)(2,1)S(1)}, bf16[512,512]{1,0:T(8,128)(2,1)S(1)}) custom-call(bf16[2048,128]{1,0:T(8,128)(2,1)S(1)} %get-tuple-element.48.turns_ref, bf16[512,128]{1,0:T(8,128)(2,1)S(1)} %get-tuple-element.49.exponent_ref, bf16[128,4096]{1,0:T(8,128)(2,1)S(1)} %get-tuple-element.50.levels_ref), custom_call_target="tpu_custom_call" | custom-call | flops 31457280 | bytes 2621440 | tf_op jit(solution)/shard_map/pallas_call | solution.py:153
  105.8 2.7 %collective-permute-start.21 = (bf16[64,2048]{1,0:T(8,128)(2,1)S(1)}, bf16[64,2048]{1,0:T(8,128)(2,1)S(1)}, u32[]{:S(2)}, u32[]{:S(2)}) collective-permute-start(bf16[64,2048]{1,0:T(8,128)(2,1)S(1)} %get-tuple-element.74), channel_id=1, source_target_pairs={{0,192},{64,0},{128,64},{192,128},{1,193},{65,1},{129,65},{193,129... | collective-permute-start | bytes 786440 | tf_op jit(solution)/shard_map/ppermute | solution.py:462
  108.5 2.3 %shard_map.110.prior_ref = f32[256,2048]{1,0:T(8,128)S(1)} custom-call(bf16[256,2048]{1,0:T(8,128)(2,1)S(1)} %shard_map.105.coef_ref, bf16[2048,512]{1,0:T(8,128)(2,1)S(1)} %get-tuple-element.51.refs_0_, bf16[2048,512]{1,0:T(8,128)(2,1)S(1)} %get-tuple-element.52.refs_1_, bf16[2048,512]{1,0:T(8,128)(2,1)S(1)} %get-tuple-element.53.refs_2_, ...), custom_call_target="tpu_custom_call" | custom-call | flops 2147483648 | bytes 8388608 | tf_op jit(solution)/shard_map/pallas_call | solution.py:237
  110.8 0.7 shard_map.111
  112.1 1.9 %collective-permute-start.17 = (bf16[64,2048]{1,0:T(8,128)(2,1)S(1)}, bf16[64,2048]{1,0:T(8,128)(2,1)S(1)}, u32[]{:S(2)}, u32[]{:S(2)}) collective-permute-start(bf16[64,2048]{1,0:T(8,128)(2,1)S(1)} %get-tuple-element.61), channel_id=1, source_target_pairs={{0,128},{64,192},{128,0},{192,64},{1,129},{65,193},{129,1},{193,65... | collective-permute-start | bytes 786440 | tf_op jit(solution)/shard_map/ppermute | solution.py:462
  114.0 2.0 %collective-permute-start.18 = (bf16[64,2048]{1,0:T(8,128)(2,1)S(1)}, bf16[64,2048]{1,0:T(8,128)(2,1)S(1)}, u32[]{:S(2)}, u32[]{:S(2)}) collective-permute-start(bf16[64,2048]{1,0:T(8,128)(2,1)S(1)} %get-tuple-element.62), channel_id=1, source_target_pairs={{0,192},{64,0},{128,64},{192,128},{1,193},{65,1},{129,65},{193,129... | collective-permute-start | bytes 786440 | tf_op jit(solution)/shard_map/ppermute | solution.py:462
  116.0 4.8 %collective-permute-done.21.refs_7_ = bf16[64,2048]{1,0:T(8,128)(2,1)S(1)} collective-permute-done((bf16[64,2048]{1,0:T(8,128)(2,1)S(1)}, bf16[64,2048]{1,0:T(8,128)(2,1)S(1)}, u32[]{:S(2)}, u32[]{:S(2)}) %collective-permute-start.21) | collective-permute-done | bytes 262176 | tf_op jit(solution)/shard_map/ppermute | solution.py:462
  120.7 5.5 %collective-permute-done.17.refs_2_ = bf16[64,2048]{1,0:T(8,128)(2,1)S(1)} collective-permute-done((bf16[64,2048]{1,0:T(8,128)(2,1)S(1)}, bf16[64,2048]{1,0:T(8,128)(2,1)S(1)}, u32[]{:S(2)}, u32[]{:S(2)}) %collective-permute-start.17) | collective-permute-done | bytes 262176 | tf_op jit(solution)/shard_map/ppermute | solution.py:462
  126.3 5.7 %collective-permute-done.18.refs_3_ = bf16[64,2048]{1,0:T(8,128)(2,1)S(1)} collective-permute-done((bf16[64,2048]{1,0:T(8,128)(2,1)S(1)}, bf16[64,2048]{1,0:T(8,128)(2,1)S(1)}, u32[]{:S(2)}, u32[]{:S(2)}) %collective-permute-start.18) | collective-permute-done | bytes 262176 | tf_op jit(solution)/shard_map/ppermute | solution.py:462
  132.0 1.2 total.1
  (41 shorter events, 3.1 us)
Async XLA Ops:
  0.0 36.6 %copy-start.2 = (f32[22,2048]{1,0:T(8,128)S(1)}, f32[22,2048]{1,0:T(8,128)}, u32[]{:S(2)}) copy-start(f32[22,2048]{1,0:T(8,128)} %refs_0_.2) | copy-start | bytes 540676
  0.0 36.6 %copy-start.1 = (s32[22,4096]{1,0:T(8,128)S(1)}, s32[22,4096]{1,0:T(8,128)}, u32[]{:S(2)}) copy-start(s32[22,4096]{1,0:T(8,128)} %refs_4_.1) | copy-start | bytes 1081348
  0.0 36.6 %copy-start = (f32[512,512]{1,0:T(8,128)S(1)}, f32[512,512]{1,0:T(8,128)}, u32[]{:S(2)}) copy-start(f32[512,512]{1,0:T(8,128)} %refs_5_.1) | copy-start | bytes 3145732
  0.0 3.9 %collective-permute-start.10 = (bf16[4,2048]{1,0:T(4,128)(2,1)}, bf16[4,2048]{1,0:T(4,128)(2,1)S(1)}, u32[]{:S(2)}, u32[]{:S(2)}) collective-permute-start(bf16[4,2048]{1,0:T(4,128)(2,1)} %refs_0_.3), channel_id=1, source_target_pairs={{0,2},{1,3},{2,0},{3,1},{4,6},{5,7},{6,4},{7,5},{8,10},{9,11},{10,... | collective-permute-start | bytes 49160 | tf_op jit(solution)/shard_map/ppermute | solution.py:329
  3.9 0.7 copy-start.5
  4.6 4.4 %collective-permute-start.11 = (bf16[8,2048]{1,0:T(8,128)(2,1)S(1)}, bf16[8,2048]{1,0:T(8,128)(2,1)S(1)}, u32[]{:S(2)}, u32[]{:S(2)}) collective-permute-start(bf16[8,2048]{1,0:T(8,128)(2,1)S(1)} %shard_map.100.refs_0_), channel_id=1, source_target_pairs={{0,4},{1,5},{2,6},{3,7},{4,0},{5,1},{6,2},{7,3},{8,12},{9,13},{10,... | collective-permute-start | bytes 98312 | tf_op jit(solution)/shard_map/ppermute | solution.py:329
  9.0 7.9 %collective-permute-start.12 = (bf16[16,2048]{1,0:T(8,128)(2,1)S(1)}, bf16[16,2048]{1,0:T(8,128)(2,1)S(1)}, u32[]{:S(2)}, u32[]{:S(2)}) collective-permute-start(bf16[16,2048]{1,0:T(8,128)(2,1)S(1)} %shard_map.101.refs_0_), channel_id=1, source_target_pairs={{0,8},{1,9},{2,10},{3,11},{4,12},{5,13},{6,14},{7,15},{8,0},{9,1},... | collective-permute-start | bytes 196616 | tf_op jit(solution)/shard_map/ppermute | solution.py:329
  16.9 4.2 %collective-permute-start.13 = (bf16[32,2048]{1,0:T(8,128)(2,1)S(1)}, bf16[32,2048]{1,0:T(8,128)(2,1)S(1)}, u32[]{:S(2)}, u32[]{:S(2)}) collective-permute-start(bf16[32,2048]{1,0:T(8,128)(2,1)S(1)} %shard_map.102.refs_0_), channel_id=1, source_target_pairs={{0,16},{1,17},{2,18},{3,19},{4,20},{5,21},{6,22},{7,23},{8,24},{9,... | collective-permute-start | bytes 393224 | tf_op jit(solution)/shard_map/ppermute | solution.py:329
  21.2 8.2 %collective-permute-start.14 = (bf16[64,2048]{1,0:T(8,128)(2,1)S(1)}, bf16[64,2048]{1,0:T(8,128)(2,1)S(1)}, u32[]{:S(2)}, u32[]{:S(2)}) collective-permute-start(bf16[64,2048]{1,0:T(8,128)(2,1)S(1)} %shard_map.103.refs_0_), channel_id=1, source_target_pairs={{0,32},{1,33},{2,34},{3,35},{4,36},{5,37},{6,38},{7,39},{8,40},{9,... | collective-permute-start | bytes 786440 | tf_op jit(solution)/shard_map/ppermute | solution.py:329
  29.4 62.8 %collective-permute-start.15 = (bf16[128,2048]{1,0:T(8,128)(2,1)S(1)}, bf16[128,2048]{1,0:T(8,128)(2,1)S(1)}, u32[]{:S(2)}, u32[]{:S(2)}) collective-permute-start(bf16[128,2048]{1,0:T(8,128)(2,1)S(1)} %shard_map.104.near_ref), channel_id=1, source_target_pairs={{0,1},{1,0},{2,3},{3,2},{4,5},{5,4},{6,7},{7,6},{8,9},{9,8},{10,11... | collective-permute-start | bytes 1572872 | tf_op jit(solution)/shard_map/ppermute | solution.py:329
  36.6 0.8 copy-start.4
  37.4 0.7 copy-start.6
  38.1 0.7 copy-start.7
  38.8 2.5 %copy-start.3 = (f32[4,512]{1,0:T(4,128)S(1)}, f32[4,512]{1,0:T(4,128)}, u32[]{:S(2)}) copy-start(f32[4,512]{1,0:T(4,128)} %whitened_ref.7) | copy-start | bytes 24580
  41.3 0.7 collective-permute-start
  42.0 0.7 collective-permute-start.1
  42.7 11.8 %collective-permute-start.2 = (f32[4,512]{1,0:T(4,128)S(1)}, f32[4,512]{1,0:T(4,128)S(1)}, u32[]{:S(2)}, u32[]{:S(2)}) collective-permute-start(f32[4,512]{1,0:T(4,128)S(1)} %get-tuple-element.46), channel_id=1, source_target_pairs={{64,0},{65,1},{66,2},{67,3},{68,4},{69,5},{70,6},{71,7},{72,8},{73... | collective-permute-start | bytes 24584 | tf_op jit(solution)/shard_map/ppermute | solution.py:428
  55.0 2.5 %collective-permute-start.3 = (bf16[4,512]{1,0:T(4,128)(2,1)S(1)}, bf16[4,512]{1,0:T(4,128)(2,1)S(1)}, u32[]{:S(2)}, u32[]{:S(2)}) collective-permute-start(bf16[4,512]{1,0:T(4,128)(2,1)S(1)} %shard_map.94.refs_0_), channel_id=1, source_target_pairs={{0,2},{1,3},{2,0},{3,1},{4,6},{5,7},{6,4},{7,5},{8,10},{9,11},{10,... | collective-permute-start | bytes 12296 | tf_op jit(solution)/shard_map/ppermute | solution.py:329
  57.6 3.4 %collective-permute-start.4 = (bf16[8,512]{1,0:T(8,128)(2,1)S(1)}, bf16[8,512]{1,0:T(8,128)(2,1)S(1)}, u32[]{:S(2)}, u32[]{:S(2)}) collective-permute-start(bf16[8,512]{1,0:T(8,128)(2,1)S(1)} %shard_map.95.refs_0_), channel_id=1, source_target_pairs={{0,4},{1,5},{2,6},{3,7},{4,0},{5,1},{6,2},{7,3},{8,12},{9,13},{10,... | collective-permute-start | bytes 24584 | tf_op jit(solution)/shard_map/ppermute | solution.py:329
  61.0 7.0 %collective-permute-start.5 = (bf16[16,512]{1,0:T(8,128)(2,1)S(1)}, bf16[16,512]{1,0:T(8,128)(2,1)S(1)}, u32[]{:S(2)}, u32[]{:S(2)}) collective-permute-start(bf16[16,512]{1,0:T(8,128)(2,1)S(1)} %shard_map.96.refs_0_), channel_id=1, source_target_pairs={{0,8},{1,9},{2,10},{3,11},{4,12},{5,13},{6,14},{7,15},{8,0},{9,1},... | collective-permute-start | bytes 49160 | tf_op jit(solution)/shard_map/ppermute | solution.py:329
  68.0 4.7 %collective-permute-start.8 = (bf16[32,512]{1,0:T(8,128)(2,1)S(1)}, bf16[32,512]{1,0:T(8,128)(2,1)S(1)}, u32[]{:S(2)}, u32[]{:S(2)}) collective-permute-start(bf16[32,512]{1,0:T(8,128)(2,1)S(1)} %shard_map.97.refs_0_), channel_id=1, source_target_pairs={{0,48},{1,49},{2,50},{3,51},{4,52},{5,53},{6,54},{7,55},{8,56},{9,... | collective-permute-start | bytes 98312 | tf_op jit(solution)/shard_map/ppermute | solution.py:329
  71.1 4.3 %collective-permute-start.7 = (bf16[32,512]{1,0:T(8,128)(2,1)S(1)}, bf16[32,512]{1,0:T(8,128)(2,1)S(1)}, u32[]{:S(2)}, u32[]{:S(2)}) collective-permute-start(bf16[32,512]{1,0:T(8,128)(2,1)S(1)} %shard_map.97.refs_0_), channel_id=1, source_target_pairs={{0,32},{1,33},{2,34},{3,35},{4,36},{5,37},{6,38},{7,39},{8,40},{9,... | collective-permute-start | bytes 98312 | tf_op jit(solution)/shard_map/ppermute | solution.py:329
  71.2 4.1 %collective-permute-start.6 = (bf16[32,512]{1,0:T(8,128)(2,1)S(1)}, bf16[32,512]{1,0:T(8,128)(2,1)S(1)}, u32[]{:S(2)}, u32[]{:S(2)}) collective-permute-start(bf16[32,512]{1,0:T(8,128)(2,1)S(1)} %shard_map.97.refs_0_), channel_id=1, source_target_pairs={{0,16},{1,17},{2,18},{3,19},{4,20},{5,21},{6,22},{7,23},{8,24},{9,... | collective-permute-start | bytes 98312 | tf_op jit(solution)/shard_map/ppermute | solution.py:329
  75.3 16.7 %collective-permute-start.9 = (bf16[128,512]{1,0:T(8,128)(2,1)S(1)}, bf16[128,512]{1,0:T(8,128)(2,1)S(1)}, u32[]{:S(2)}, u32[]{:S(2)}) collective-permute-start(bf16[128,512]{1,0:T(8,128)(2,1)S(1)} %shard_map.98.near_ref), channel_id=1, source_target_pairs={{0,1},{1,0},{2,3},{3,2},{4,5},{5,4},{6,7},{7,6},{8,9},{9,8},{10,11... | collective-permute-start | bytes 393224 | tf_op jit(solution)/shard_map/ppermute | solution.py:329
  95.8 18.2 %collective-permute-start.19 = (bf16[64,2048]{1,0:T(8,128)(2,1)S(1)}, bf16[64,2048]{1,0:T(8,128)(2,1)S(1)}, u32[]{:S(2)}, u32[]{:S(2)}) collective-permute-start(bf16[64,2048]{1,0:T(8,128)(2,1)S(1)} %get-tuple-element.72), channel_id=1, source_target_pairs={{0,64},{64,128},{128,192},{192,0},{1,65},{65,129},{129,193},{193,1... | collective-permute-start | bytes 786440 | tf_op jit(solution)/shard_map/ppermute | solution.py:462
  105.7 10.3 %collective-permute-start.20 = (bf16[64,2048]{1,0:T(8,128)(2,1)S(1)}, bf16[64,2048]{1,0:T(8,128)(2,1)S(1)}, u32[]{:S(2)}, u32[]{:S(2)}) collective-permute-start(bf16[64,2048]{1,0:T(8,128)(2,1)S(1)} %get-tuple-element.73), channel_id=1, source_target_pairs={{0,128},{64,192},{128,0},{192,64},{1,129},{65,193},{129,1},{193,65... | collective-permute-start | bytes 786440 | tf_op jit(solution)/shard_map/ppermute | solution.py:462
  105.8 15.0 %collective-permute-start.21 = (bf16[64,2048]{1,0:T(8,128)(2,1)S(1)}, bf16[64,2048]{1,0:T(8,128)(2,1)S(1)}, u32[]{:S(2)}, u32[]{:S(2)}) collective-permute-start(bf16[64,2048]{1,0:T(8,128)(2,1)S(1)} %get-tuple-element.74), channel_id=1, source_target_pairs={{0,192},{64,0},{128,64},{192,128},{1,193},{65,1},{129,65},{193,129... | collective-permute-start | bytes 786440 | tf_op jit(solution)/shard_map/ppermute | solution.py:462
  111.5 9.2 %collective-permute-start.16 = (bf16[64,2048]{1,0:T(8,128)(2,1)S(1)}, bf16[64,2048]{1,0:T(8,128)(2,1)S(1)}, u32[]{:S(2)}, u32[]{:S(2)}) collective-permute-start(bf16[64,2048]{1,0:T(8,128)(2,1)S(1)} %get-tuple-element.60), channel_id=1, source_target_pairs={{0,64},{64,128},{128,192},{192,0},{1,65},{65,129},{129,193},{193,1... | collective-permute-start | bytes 786440 | tf_op jit(solution)/shard_map/ppermute | solution.py:462
  112.1 14.2 %collective-permute-start.17 = (bf16[64,2048]{1,0:T(8,128)(2,1)S(1)}, bf16[64,2048]{1,0:T(8,128)(2,1)S(1)}, u32[]{:S(2)}, u32[]{:S(2)}) collective-permute-start(bf16[64,2048]{1,0:T(8,128)(2,1)S(1)} %get-tuple-element.61), channel_id=1, source_target_pairs={{0,128},{64,192},{128,0},{192,64},{1,129},{65,193},{129,1},{193,65... | collective-permute-start | bytes 786440 | tf_op jit(solution)/shard_map/ppermute | solution.py:462
  114.0 18.0 %collective-permute-start.18 = (bf16[64,2048]{1,0:T(8,128)(2,1)S(1)}, bf16[64,2048]{1,0:T(8,128)(2,1)S(1)}, u32[]{:S(2)}, u32[]{:S(2)}) collective-permute-start(bf16[64,2048]{1,0:T(8,128)(2,1)S(1)} %get-tuple-element.62), channel_id=1, source_target_pairs={{0,192},{64,0},{128,64},{192,128},{1,193},{65,1},{129,65},{193,129... | collective-permute-start | bytes 786440 | tf_op jit(solution)/shard_map/ppermute | solution.py:462

commit v4 on v3

--- a/solution.py
+++ b/solution.py
@@ -120,10 +120,15 @@
             pltpu.VMEM((LANES, cands), F32),
             pltpu.SemaphoreType.DMA((7,)),
         ],
-        compiler_params=params(44 * 2**20),
+        compiler_params=params(),
         cost_estimate=pl.CostEstimate(flops=10**7, transcendentals=0, bytes_accessed=8 * 2**20),
         name="prepare",
-    )(*arrays, diag_inv, factor_rows)
+    )(
+        *(
+            pltpu.with_memory_space_constraint(array, pltpu.HBM)
+            for array in (*arrays, diag_inv, factor_rows)
+        )
+    )
 
 
 def cosine(turns):
@@ -183,10 +188,13 @@
     row = lax.broadcasted_iota(jnp.int32, (block, block), 0)
     column = lax.broadcasted_iota(jnp.int32, (block, block), 1)
     offset = (row // shard) ^ (mine & (DEPTHS * CORES - 1))
-    source = ((offset & (CORES - 1)) * DEPTHS + offset // CORES) * shard + (row & (shard - 1))
+    depth = offset // CORES
+    depth = jnp.where(depth < DEPTHS // 2, depth, depth ^ (DEPTHS // 2 - 1))
+    source = ((offset & (CORES - 1)) * DEPTHS + depth) * shard + (row & (shard - 1))
     chosen = (source == column).astype(F32).astype(BF16)
     for target in range(WIDTHS):
         width = ((across + target) & (WIDTHS - 1)) ^ (mine // (DEPTHS * CORES))
+        width = width ^ (width // 2)
         held = pl.ds(pl.multiple_of(width * half, half), half)
         lines = jnp.concatenate([near_ref[held, :], far_ref[held, :]], axis=0)
         out_ref[target * block : (target + 1) * block, :] = jnp.dot(
@@ -329,16 +337,16 @@
         return lax.ppermute(held, "cand", pairs)
 
     held = piece
-    for hop in (1, 2, 4):
+    for hop in (1, 2, 7):
         other = swap(held, exchange_pairs(hop * CORES))
         held = stack([held, other])
     step = DEPTHS * CORES
     if at_once:
-        others = [swap(held, exchange_pairs(hop * step)) for hop in range(1, WIDTHS)]
+        others = [swap(held, exchange_pairs(hop * step)) for hop in (1, 3, 2)]
         near = stack([held] + others)
     else:
         near = stack([held, swap(held, exchange_pairs(step))])
-        near = stack([near, swap(near, exchange_pairs(2 * step))])
+        near = stack([near, swap(near, exchange_pairs(3 * step))])
     return near, swap(near, exchange_pairs(1))
 
 

time: 133 us -> 126 us (0.947); the launches traced: 133 us -> 125 us
  starting transfers between devices: 52 us -> 46.7 us
  local copies, waits for them, and re-layouts: 2.88 us -> 0.72 us
    ppermute x13, starting transfers between devices: 41.8 us -> 36.5 us  [swap(): return lax.ppermute(held, 'cand', pairs)]
    ppermute x13, waiting for transfers between devices: 21.3 us -> 18.3 us  [swap(): return lax.ppermute(held, 'cand', pairs)]
    unnamed x16 -> x4, local copies, waits for them, and re-layouts: 2.88 us -> 0.72 us
    ppermute x3, waiting for transfers between devices: 10.5 us -> 12.4 us  [solve_chain(): carried = lax.ppermute(carried, 'rows', [(section, section - 1)])]
  transfers between devices with their start and end apart: 22 -> 22, of which waited for: 14 -> 14; matrix products, arithmetic and copies ran while one was open for 0% -> 0% of each run, Pallas kernels for 19% -> 20%
where the time goes in v4:
time: 126 us; the launch traced here: 125 us
  starting transfers between devices  46.7 us (37%)
  waiting for transfers between devices  46.7 us (37%)
  Pallas kernels  30.2 us (24%)
    ppermute x13, starting transfers between devices, swap(): return lax.ppermute(held, 'cand', pairs)  36.5 us
    pallas_call x8, Pallas kernels, tiles(): pl.pallas_call(tile_kernel, out_shape=(jax.ShapeDtypeStruct((feats, cands...  19 us
    ppermute x13, waiting for transfers between devices, swap(): return lax.ppermute(held, 'cand', pairs)  18.3 us
    ppermute x6, waiting for transfers between devices, body(): arrived.append(lax.ppermute(block, 'rows', pairs))  16 us
    ppermute x3, waiting for transfers between devices, solve_chain(): carried = lax.ppermute(carried, 'rows', [(section, section - 1)])  12.4 us
    ppermute x6, starting transfers between devices, body(): arrived.append(lax.ppermute(block, 'rows', pairs))  7.55 us
    pallas_call x2, Pallas kernels, prior_product(): pl.pallas_call(prior_kernel, out_shape=jax.ShapeDtypeStruct((rows, cands)...  4.64 us
    ppermute x3, starting transfers between devices, solve_chain(): carried = lax.ppermute(carried, 'rows', [(section, section - 1)])  2.62 us
  transfers between devices with their start and end apart: 22, of which 14 were waited for; matrix products, arithmetic and copies ran while one was open for 0% of the time, Pallas kernels for 20%

profile of v4, /device:TPU:1, one launch (start us, length us, event | category | flops | bytes accessed | tf_op | source)
XLA Modules:
  0.0 124.6 jit_solution(5923185821899602119)
XLA Ops:
  0.0 2.5 %collective-permute-start.10 = (bf16[4,2048]{1,0:T(4,128)(2,1)}, bf16[4,2048]{1,0:T(4,128)(2,1)S(1)}, u32[]{:S(2)}, u32[]{:S(2)}) collective-permute-start(bf16[4,2048]{1,0:T(4,128)(2,1)} %refs_0_.3), channel_id=1, source_target_pairs={{0,2},{1,3},{2,0},{3,1},{4,6},{5,7},{6,4},{7,5},{8,10},{9,11},{10,... | collective-permute-start | bytes 49160 | tf_op jit(solution)/shard_map/ppermute | solution.py:337
  2.5 1.3 %collective-permute-done.10.refs_1_ = bf16[4,2048]{1,0:T(4,128)(2,1)S(1)} collective-permute-done((bf16[4,2048]{1,0:T(4,128)(2,1)}, bf16[4,2048]{1,0:T(4,128)(2,1)S(1)}, u32[]{:S(2)}, u32[]{:S(2)}) %collective-permute-start.10) | collective-permute-done | bytes 16416 | tf_op jit(solution)/shard_map/ppermute | solution.py:337
  3.8 0.7 copy-done.1
  4.5 3.1 %collective-permute-start.11 = (bf16[8,2048]{1,0:T(8,128)(2,1)S(1)}, bf16[8,2048]{1,0:T(8,128)(2,1)S(1)}, u32[]{:S(2)}, u32[]{:S(2)}) collective-permute-start(bf16[8,2048]{1,0:T(8,128)(2,1)S(1)} %shard_map.100.refs_0_), channel_id=1, source_target_pairs={{0,4},{1,5},{2,6},{3,7},{4,0},{5,1},{6,2},{7,3},{8,12},{9,13},{10,... | collective-permute-start | bytes 98312 | tf_op jit(solution)/shard_map/ppermute | solution.py:337
  7.6 1.3 %collective-permute-done.11.refs_1_ = bf16[8,2048]{1,0:T(8,128)(2,1)S(1)} collective-permute-done((bf16[8,2048]{1,0:T(8,128)(2,1)S(1)}, bf16[8,2048]{1,0:T(8,128)(2,1)S(1)}, u32[]{:S(2)}, u32[]{:S(2)}) %collective-permute-start.11) | collective-permute-done | bytes 32800 | tf_op jit(solution)/shard_map/ppermute | solution.py:337
  8.9 4.8 %collective-permute-start.12 = (bf16[16,2048]{1,0:T(8,128)(2,1)S(1)}, bf16[16,2048]{1,0:T(8,128)(2,1)S(1)}, u32[]{:S(2)}, u32[]{:S(2)}) collective-permute-start(bf16[16,2048]{1,0:T(8,128)(2,1)S(1)} %shard_map.101.refs_0_), channel_id=1, source_target_pairs={{0,14},{1,15},{2,12},{3,13},{4,10},{5,11},{6,8},{7,9},{8,6},{9,7},... | collective-permute-start | bytes 196616 | tf_op jit(solution)/shard_map/ppermute | solution.py:337
  13.7 2.0 %collective-permute-done.12.refs_1_ = bf16[16,2048]{1,0:T(8,128)(2,1)S(1)} collective-permute-done((bf16[16,2048]{1,0:T(8,128)(2,1)S(1)}, bf16[16,2048]{1,0:T(8,128)(2,1)S(1)}, u32[]{:S(2)}, u32[]{:S(2)}) %collective-permute-start.12) | collective-permute-done | bytes 65568 | tf_op jit(solution)/shard_map/ppermute | solution.py:337
  15.7 1.3 %collective-permute-start.13 = (bf16[32,2048]{1,0:T(8,128)(2,1)S(1)}, bf16[32,2048]{1,0:T(8,128)(2,1)S(1)}, u32[]{:S(2)}, u32[]{:S(2)}) collective-permute-start(bf16[32,2048]{1,0:T(8,128)(2,1)S(1)} %shard_map.102.refs_0_), channel_id=1, source_target_pairs={{0,16},{1,17},{2,18},{3,19},{4,20},{5,21},{6,22},{7,23},{8,24},{9,... | collective-permute-start | bytes 393224 | tf_op jit(solution)/shard_map/ppermute | solution.py:337
  17.0 2.6 %collective-permute-done.13.refs_1_ = bf16[32,2048]{1,0:T(8,128)(2,1)S(1)} collective-permute-done((bf16[32,2048]{1,0:T(8,128)(2,1)S(1)}, bf16[32,2048]{1,0:T(8,128)(2,1)S(1)}, u32[]{:S(2)}, u32[]{:S(2)}) %collective-permute-start.13) | collective-permute-done | bytes 131104 | tf_op jit(solution)/shard_map/ppermute | solution.py:337
  19.6 2.6 %collective-permute-start.14 = (bf16[64,2048]{1,0:T(8,128)(2,1)S(1)}, bf16[64,2048]{1,0:T(8,128)(2,1)S(1)}, u32[]{:S(2)}, u32[]{:S(2)}) collective-permute-start(bf16[64,2048]{1,0:T(8,128)(2,1)S(1)} %shard_map.103.refs_0_), channel_id=1, source_target_pairs={{0,48},{1,49},{2,50},{3,51},{4,52},{5,53},{6,54},{7,55},{8,56},{9,... | collective-permute-start | bytes 786440 | tf_op jit(solution)/shard_map/ppermute | solution.py:337
  22.2 4.0 %collective-permute-done.14.refs_1_ = bf16[64,2048]{1,0:T(8,128)(2,1)S(1)} collective-permute-done((bf16[64,2048]{1,0:T(8,128)(2,1)S(1)}, bf16[64,2048]{1,0:T(8,128)(2,1)S(1)}, u32[]{:S(2)}, u32[]{:S(2)}) %collective-permute-start.14) | collective-permute-done | bytes 262176 | tf_op jit(solution)/shard_map/ppermute | solution.py:337
  26.2 6.7 %collective-permute-start.15 = (bf16[128,2048]{1,0:T(8,128)(2,1)S(1)}, bf16[128,2048]{1,0:T(8,128)(2,1)S(1)}, u32[]{:S(2)}, u32[]{:S(2)}) collective-permute-start(bf16[128,2048]{1,0:T(8,128)(2,1)S(1)} %shard_map.104.near_ref), channel_id=1, source_target_pairs={{0,1},{1,0},{2,3},{3,2},{4,5},{5,4},{6,7},{7,6},{8,9},{9,8},{10,11... | collective-permute-start | bytes 1572872 | tf_op jit(solution)/shard_map/ppermute | solution.py:337
  32.9 2.6 %prepare.1 = (bf16[2048,128]{1,0:T(8,128)(2,1)S(1)}, bf16[512,128]{1,0:T(8,128)(2,1)S(1)}, bf16[128,4096]{1,0:T(8,128)(2,1)S(1)}, f32[512,512]{1,0:T(8,128)S(1)}, f32[512,1536]{1,0:T(8,128)S(1)}) custom-call(f32[22,2048]{1,0:T(8,128)} %refs_0_.2, f32[1,2048]{1,0:T(1,128)} %bitcast.3, f32[22,512]{1,0:T(8,128)} %refs_2_.1, f32[1,22]{1,0:T(1,128)} %bitcast.4, ...), custom_call_target="tpu_custom_call" | custom-call | flops 10000000 | bytes 8388608 | tf_op jit(solution)/shard_map/prepare/pallas_call | solution.py:105
  35.5 0.7 collective-permute-start
  36.2 0.7 collective-permute-start.1
  36.9 1.3 %collective-permute-start.2 = (f32[4,512]{1,0:T(4,128)S(1)}, f32[4,512]{1,0:T(4,128)S(1)}, u32[]{:S(2)}, u32[]{:S(2)}) collective-permute-start(f32[4,512]{1,0:T(4,128)S(1)} %get-tuple-element.46), channel_id=1, source_target_pairs={{64,0},{65,1},{66,2},{67,3},{68,4},{69,5},{70,6},{71,7},{72,8},{73... | collective-permute-start | bytes 24584 | tf_op jit(solution)/shard_map/ppermute | solution.py:436
  38.2 12.4 %collective-permute-done.2.refs_0_ = f32[4,512]{1,0:T(4,128)S(1)} collective-permute-done((f32[4,512]{1,0:T(4,128)S(1)}, f32[4,512]{1,0:T(4,128)S(1)}, u32[]{:S(2)}, u32[]{:S(2)}) %collective-permute-start.2) | collective-permute-done | bytes 8224 | tf_op jit(solution)/shard_map/ppermute | solution.py:436
  51.1 1.0 collective-permute-start.3
  52.1 1.5 %collective-permute-done.3.refs_1_ = bf16[4,512]{1,0:T(4,128)(2,1)S(1)} collective-permute-done((bf16[4,512]{1,0:T(4,128)(2,1)S(1)}, bf16[4,512]{1,0:T(4,128)(2,1)S(1)}, u32[]{:S(2)}, u32[]{:S(2)}) %collective-permute-start.3) | collective-permute-done | bytes 4128 | tf_op jit(solution)/shard_map/ppermute | solution.py:337
  53.6 1.5 %collective-permute-start.4 = (bf16[8,512]{1,0:T(8,128)(2,1)S(1)}, bf16[8,512]{1,0:T(8,128)(2,1)S(1)}, u32[]{:S(2)}, u32[]{:S(2)}) collective-permute-start(bf16[8,512]{1,0:T(8,128)(2,1)S(1)} %shard_map.95.refs_0_), channel_id=1, source_target_pairs={{0,4},{1,5},{2,6},{3,7},{4,0},{5,1},{6,2},{7,3},{8,12},{9,13},{10,... | collective-permute-start | bytes 24584 | tf_op jit(solution)/shard_map/ppermute | solution.py:337
  55.1 1.9 %collective-permute-done.4.refs_1_ = bf16[8,512]{1,0:T(8,128)(2,1)S(1)} collective-permute-done((bf16[8,512]{1,0:T(8,128)(2,1)S(1)}, bf16[8,512]{1,0:T(8,128)(2,1)S(1)}, u32[]{:S(2)}, u32[]{:S(2)}) %collective-permute-start.4) | collective-permute-done | bytes 8224 | tf_op jit(solution)/shard_map/ppermute | solution.py:337
  57.1 3.2 %collective-permute-start.5 = (bf16[16,512]{1,0:T(8,128)(2,1)S(1)}, bf16[16,512]{1,0:T(8,128)(2,1)S(1)}, u32[]{:S(2)}, u32[]{:S(2)}) collective-permute-start(bf16[16,512]{1,0:T(8,128)(2,1)S(1)} %shard_map.96.refs_0_), channel_id=1, source_target_pairs={{0,14},{1,15},{2,12},{3,13},{4,10},{5,11},{6,8},{7,9},{8,6},{9,7},... | collective-permute-start | bytes 49160 | tf_op jit(solution)/shard_map/ppermute | solution.py:337
  60.3 1.1 collective-permute-done.5.refs_1_
  61.4 1.5 %collective-permute-start.8 = (bf16[32,512]{1,0:T(8,128)(2,1)S(1)}, bf16[32,512]{1,0:T(8,128)(2,1)S(1)}, u32[]{:S(2)}, u32[]{:S(2)}) collective-permute-start(bf16[32,512]{1,0:T(8,128)(2,1)S(1)} %shard_map.97.refs_0_), channel_id=1, source_target_pairs={{0,32},{1,33},{2,34},{3,35},{4,36},{5,37},{6,38},{7,39},{8,40},{9,... | collective-permute-start | bytes 98312 | tf_op jit(solution)/shard_map/ppermute | solution.py:337
  62.9 0.9 collective-permute-start.7
  63.9 0.6 collective-permute-start.6
  64.5 1.2 collective-permute-done.8.refs_3_
  65.7 1.2 collective-permute-done.7.refs_2_
  66.9 6.9 %collective-permute-start.9 = (bf16[128,512]{1,0:T(8,128)(2,1)S(1)}, bf16[128,512]{1,0:T(8,128)(2,1)S(1)}, u32[]{:S(2)}, u32[]{:S(2)}) collective-permute-start(bf16[128,512]{1,0:T(8,128)(2,1)S(1)} %shard_map.98.near_ref), channel_id=1, source_target_pairs={{0,1},{1,0},{2,3},{3,2},{4,5},{5,4},{6,7},{7,6},{8,9},{9,8},{10,11... | collective-permute-start | bytes 393224 | tf_op jit(solution)/shard_map/ppermute | solution.py:337
  73.9 2.4 %shard_map.115 = (bf16[2048,512]{1,0:T(8,128)(2,1)S(1)}, bf16[512,512]{1,0:T(8,128)(2,1)S(1)}) custom-call(bf16[2048,128]{1,0:T(8,128)(2,1)S(1)} %get-tuple-element.48.turns_ref, bf16[512,128]{1,0:T(8,128)(2,1)S(1)} %get-tuple-element.49.exponent_ref, bf16[128,4096]{1,0:T(8,128)(2,1)S(1)} %get-tuple-element.50.levels_ref), custom_call_target="tpu_custom_call" | custom-call | flops 31457280 | bytes 2621440 | tf_op jit(solution)/shard_map/pallas_call | solution.py:158
  76.2 2.4 %shard_map.114 = (bf16[2048,512]{1,0:T(8,128)(2,1)S(1)}, bf16[512,512]{1,0:T(8,128)(2,1)S(1)}) custom-call(bf16[2048,128]{1,0:T(8,128)(2,1)S(1)} %get-tuple-element.48.turns_ref, bf16[512,128]{1,0:T(8,128)(2,1)S(1)} %get-tuple-element.49.exponent_ref, bf16[128,4096]{1,0:T(8,128)(2,1)S(1)} %get-tuple-element.50.levels_ref), custom_call_target="tpu_custom_call" | custom-call | flops 31457280 | bytes 2621440 | tf_op jit(solution)/shard_map/pallas_call | solution.py:158
  78.6 2.4 %shard_map.113 = (bf16[2048,512]{1,0:T(8,128)(2,1)S(1)}, bf16[512,512]{1,0:T(8,128)(2,1)S(1)}) custom-call(bf16[2048,128]{1,0:T(8,128)(2,1)S(1)} %get-tuple-element.48.turns_ref, bf16[512,128]{1,0:T(8,128)(2,1)S(1)} %get-tuple-element.49.exponent_ref, bf16[128,4096]{1,0:T(8,128)(2,1)S(1)} %get-tuple-element.50.levels_ref), custom_call_target="tpu_custom_call" | custom-call | flops 31457280 | bytes 2621440 | tf_op jit(solution)/shard_map/pallas_call | solution.py:158
  81.0 2.4 %shard_map.112 = (bf16[2048,512]{1,0:T(8,128)(2,1)S(1)}, bf16[512,512]{1,0:T(8,128)(2,1)S(1)}) custom-call(bf16[2048,128]{1,0:T(8,128)(2,1)S(1)} %get-tuple-element.48.turns_ref, bf16[512,128]{1,0:T(8,128)(2,1)S(1)} %get-tuple-element.49.exponent_ref, bf16[128,4096]{1,0:T(8,128)(2,1)S(1)} %get-tuple-element.50.levels_ref), custom_call_target="tpu_custom_call" | custom-call | flops 31457280 | bytes 2621440 | tf_op jit(solution)/shard_map/pallas_call | solution.py:158
  84.1 2.3 %shard_map.116.prior_ref = f32[256,2048]{1,0:T(8,128)S(1)} custom-call(bf16[256,2048]{1,0:T(8,128)(2,1)S(1)} %shard_map.105.coef_ref, bf16[2048,512]{1,0:T(8,128)(2,1)S(1)} %get-tuple-element.63.refs_0_, bf16[2048,512]{1,0:T(8,128)(2,1)S(1)} %get-tuple-element.64.refs_1_, bf16[2048,512]{1,0:T(8,128)(2,1)S(1)} %get-tuple-element.65.refs_2_, ...), custom_call_target="tpu_custom_call" | custom-call | flops 2147483648 | bytes 8388608 | tf_op jit(solution)/shard_map/pallas_call | solution.py:245
  86.4 0.7 shard_map.117
  87.5 2.4 %shard_map.109 = (bf16[2048,512]{1,0:T(8,128)(2,1)S(1)}, bf16[512,512]{1,0:T(8,128)(2,1)S(1)}) custom-call(bf16[2048,128]{1,0:T(8,128)(2,1)S(1)} %get-tuple-element.48.turns_ref, bf16[512,128]{1,0:T(8,128)(2,1)S(1)} %get-tuple-element.49.exponent_ref, bf16[128,4096]{1,0:T(8,128)(2,1)S(1)} %get-tuple-element.50.levels_ref), custom_call_target="tpu_custom_call" | custom-call | flops 31457280 | bytes 2621440 | tf_op jit(solution)/shard_map/pallas_call | solution.py:158
  89.9 2.4 %shard_map.108 = (bf16[2048,512]{1,0:T(8,128)(2,1)S(1)}, bf16[512,512]{1,0:T(8,128)(2,1)S(1)}) custom-call(bf16[2048,128]{1,0:T(8,128)(2,1)S(1)} %get-tuple-element.48.turns_ref, bf16[512,128]{1,0:T(8,128)(2,1)S(1)} %get-tuple-element.49.exponent_ref, bf16[128,4096]{1,0:T(8,128)(2,1)S(1)} %get-tuple-element.50.levels_ref), custom_call_target="tpu_custom_call" | custom-call | flops 31457280 | bytes 2621440 | tf_op jit(solution)/shard_map/pallas_call | solution.py:158
  92.3 2.4 %shard_map.107 = (bf16[2048,512]{1,0:T(8,128)(2,1)S(1)}, bf16[512,512]{1,0:T(8,128)(2,1)S(1)}) custom-call(bf16[2048,128]{1,0:T(8,128)(2,1)S(1)} %get-tuple-element.48.turns_ref, bf16[512,128]{1,0:T(8,128)(2,1)S(1)} %get-tuple-element.49.exponent_ref, bf16[128,4096]{1,0:T(8,128)(2,1)S(1)} %get-tuple-element.50.levels_ref), custom_call_target="tpu_custom_call" | custom-call | flops 31457280 | bytes 2621440 | tf_op jit(solution)/shard_map/pallas_call | solution.py:158
  94.6 2.4 %shard_map.106 = (bf16[2048,512]{1,0:T(8,128)(2,1)S(1)}, bf16[512,512]{1,0:T(8,128)(2,1)S(1)}) custom-call(bf16[2048,128]{1,0:T(8,128)(2,1)S(1)} %get-tuple-element.48.turns_ref, bf16[512,128]{1,0:T(8,128)(2,1)S(1)} %get-tuple-element.49.exponent_ref, bf16[128,4096]{1,0:T(8,128)(2,1)S(1)} %get-tuple-element.50.levels_ref), custom_call_target="tpu_custom_call" | custom-call | flops 31457280 | bytes 2621440 | tf_op jit(solution)/shard_map/pallas_call | solution.py:158
  97.1 2.7 %collective-permute-start.21 = (bf16[64,2048]{1,0:T(8,128)(2,1)S(1)}, bf16[64,2048]{1,0:T(8,128)(2,1)S(1)}, u32[]{:S(2)}, u32[]{:S(2)}) collective-permute-start(bf16[64,2048]{1,0:T(8,128)(2,1)S(1)} %get-tuple-element.74), channel_id=1, source_target_pairs={{0,192},{64,0},{128,64},{192,128},{1,193},{65,1},{129,65},{193,129... | collective-permute-start | bytes 786440 | tf_op jit(solution)/shard_map/ppermute | solution.py:470
  99.9 2.3 %shard_map.110.prior_ref = f32[256,2048]{1,0:T(8,128)S(1)} custom-call(bf16[256,2048]{1,0:T(8,128)(2,1)S(1)} %shard_map.105.coef_ref, bf16[2048,512]{1,0:T(8,128)(2,1)S(1)} %get-tuple-element.51.refs_0_, bf16[2048,512]{1,0:T(8,128)(2,1)S(1)} %get-tuple-element.52.refs_1_, bf16[2048,512]{1,0:T(8,128)(2,1)S(1)} %get-tuple-element.53.refs_2_, ...), custom_call_target="tpu_custom_call" | custom-call | flops 2147483648 | bytes 8388608 | tf_op jit(solution)/shard_map/pallas_call | solution.py:245
  102.2 0.7 shard_map.111
  103.5 1.9 %collective-permute-start.17 = (bf16[64,2048]{1,0:T(8,128)(2,1)S(1)}, bf16[64,2048]{1,0:T(8,128)(2,1)S(1)}, u32[]{:S(2)}, u32[]{:S(2)}) collective-permute-start(bf16[64,2048]{1,0:T(8,128)(2,1)S(1)} %get-tuple-element.61), channel_id=1, source_target_pairs={{0,128},{64,192},{128,0},{192,64},{1,129},{65,193},{129,1},{193,65... | collective-permute-start | bytes 786440 | tf_op jit(solution)/shard_map/ppermute | solution.py:470
  105.4 2.0 %collective-permute-start.18 = (bf16[64,2048]{1,0:T(8,128)(2,1)S(1)}, bf16[64,2048]{1,0:T(8,128)(2,1)S(1)}, u32[]{:S(2)}, u32[]{:S(2)}) collective-permute-start(bf16[64,2048]{1,0:T(8,128)(2,1)S(1)} %get-tuple-element.62), channel_id=1, source_target_pairs={{0,192},{64,0},{128,64},{192,128},{1,193},{65,1},{129,65},{193,129... | collective-permute-start | bytes 786440 | tf_op jit(solution)/shard_map/ppermute | solution.py:470
  107.3 4.8 %collective-permute-done.21.refs_7_ = bf16[64,2048]{1,0:T(8,128)(2,1)S(1)} collective-permute-done((bf16[64,2048]{1,0:T(8,128)(2,1)S(1)}, bf16[64,2048]{1,0:T(8,128)(2,1)S(1)}, u32[]{:S(2)}, u32[]{:S(2)}) %collective-permute-start.21) | collective-permute-done | bytes 262176 | tf_op jit(solution)/shard_map/ppermute | solution.py:470
  112.1 5.5 %collective-permute-done.17.refs_2_ = bf16[64,2048]{1,0:T(8,128)(2,1)S(1)} collective-permute-done((bf16[64,2048]{1,0:T(8,128)(2,1)S(1)}, bf16[64,2048]{1,0:T(8,128)(2,1)S(1)}, u32[]{:S(2)}, u32[]{:S(2)}) %collective-permute-start.17) | collective-permute-done | bytes 262176 | tf_op jit(solution)/shard_map/ppermute | solution.py:470
  117.6 5.8 %collective-permute-done.18.refs_3_ = bf16[64,2048]{1,0:T(8,128)(2,1)S(1)} collective-permute-done((bf16[64,2048]{1,0:T(8,128)(2,1)S(1)}, bf16[64,2048]{1,0:T(8,128)(2,1)S(1)}, u32[]{:S(2)}, u32[]{:S(2)}) %collective-permute-start.18) | collective-permute-done | bytes 262176 | tf_op jit(solution)/shard_map/ppermute | solution.py:470
  123.4 1.2 total.1
  (29 shorter events, 2.3 us)
Async XLA Ops:
  0.0 3.8 %collective-permute-start.10 = (bf16[4,2048]{1,0:T(4,128)(2,1)}, bf16[4,2048]{1,0:T(4,128)(2,1)S(1)}, u32[]{:S(2)}, u32[]{:S(2)}) collective-permute-start(bf16[4,2048]{1,0:T(4,128)(2,1)} %refs_0_.3), channel_id=1, source_target_pairs={{0,2},{1,3},{2,0},{3,1},{4,6},{5,7},{6,4},{7,5},{8,10},{9,11},{10,... | collective-permute-start | bytes 49160 | tf_op jit(solution)/shard_map/ppermute | solution.py:337
  3.8 0.7 copy-start.1
  4.5 4.4 %collective-permute-start.11 = (bf16[8,2048]{1,0:T(8,128)(2,1)S(1)}, bf16[8,2048]{1,0:T(8,128)(2,1)S(1)}, u32[]{:S(2)}, u32[]{:S(2)}) collective-permute-start(bf16[8,2048]{1,0:T(8,128)(2,1)S(1)} %shard_map.100.refs_0_), channel_id=1, source_target_pairs={{0,4},{1,5},{2,6},{3,7},{4,0},{5,1},{6,2},{7,3},{8,12},{9,13},{10,... | collective-permute-start | bytes 98312 | tf_op jit(solution)/shard_map/ppermute | solution.py:337
  8.9 6.8 %collective-permute-start.12 = (bf16[16,2048]{1,0:T(8,128)(2,1)S(1)}, bf16[16,2048]{1,0:T(8,128)(2,1)S(1)}, u32[]{:S(2)}, u32[]{:S(2)}) collective-permute-start(bf16[16,2048]{1,0:T(8,128)(2,1)S(1)} %shard_map.101.refs_0_), channel_id=1, source_target_pairs={{0,14},{1,15},{2,12},{3,13},{4,10},{5,11},{6,8},{7,9},{8,6},{9,7},... | collective-permute-start | bytes 196616 | tf_op jit(solution)/shard_map/ppermute | solution.py:337
  15.7 3.9 %collective-permute-start.13 = (bf16[32,2048]{1,0:T(8,128)(2,1)S(1)}, bf16[32,2048]{1,0:T(8,128)(2,1)S(1)}, u32[]{:S(2)}, u32[]{:S(2)}) collective-permute-start(bf16[32,2048]{1,0:T(8,128)(2,1)S(1)} %shard_map.102.refs_0_), channel_id=1, source_target_pairs={{0,16},{1,17},{2,18},{3,19},{4,20},{5,21},{6,22},{7,23},{8,24},{9,... | collective-permute-start | bytes 393224 | tf_op jit(solution)/shard_map/ppermute | solution.py:337
  19.6 6.5 %collective-permute-start.14 = (bf16[64,2048]{1,0:T(8,128)(2,1)S(1)}, bf16[64,2048]{1,0:T(8,128)(2,1)S(1)}, u32[]{:S(2)}, u32[]{:S(2)}) collective-permute-start(bf16[64,2048]{1,0:T(8,128)(2,1)S(1)} %shard_map.103.refs_0_), channel_id=1, source_target_pairs={{0,48},{1,49},{2,50},{3,51},{4,52},{5,53},{6,54},{7,55},{8,56},{9,... | collective-permute-start | bytes 786440 | tf_op jit(solution)/shard_map/ppermute | solution.py:337
  26.2 57.5 %collective-permute-start.15 = (bf16[128,2048]{1,0:T(8,128)(2,1)S(1)}, bf16[128,2048]{1,0:T(8,128)(2,1)S(1)}, u32[]{:S(2)}, u32[]{:S(2)}) collective-permute-start(bf16[128,2048]{1,0:T(8,128)(2,1)S(1)} %shard_map.104.near_ref), channel_id=1, source_target_pairs={{0,1},{1,0},{2,3},{3,2},{4,5},{5,4},{6,7},{7,6},{8,9},{9,8},{10,11... | collective-permute-start | bytes 1572872 | tf_op jit(solution)/shard_map/ppermute | solution.py:337
  32.9 2.6 %copy-start = (f32[4,512]{1,0:T(4,128)S(1)}, f32[4,512]{1,0:T(4,128)}, u32[]{:S(2)}) copy-start(f32[4,512]{1,0:T(4,128)} %whitened_ref.7) | copy-start | bytes 24580
  35.5 0.7 collective-permute-start
  36.2 0.7 collective-permute-start.1
  36.9 13.7 %collective-permute-start.2 = (f32[4,512]{1,0:T(4,128)S(1)}, f32[4,512]{1,0:T(4,128)S(1)}, u32[]{:S(2)}, u32[]{:S(2)}) collective-permute-start(f32[4,512]{1,0:T(4,128)S(1)} %get-tuple-element.46), channel_id=1, source_target_pairs={{64,0},{65,1},{66,2},{67,3},{68,4},{69,5},{70,6},{71,7},{72,8},{73... | collective-permute-start | bytes 24584 | tf_op jit(solution)/shard_map/ppermute | solution.py:436
  51.1 2.5 %collective-permute-start.3 = (bf16[4,512]{1,0:T(4,128)(2,1)S(1)}, bf16[4,512]{1,0:T(4,128)(2,1)S(1)}, u32[]{:S(2)}, u32[]{:S(2)}) collective-permute-start(bf16[4,512]{1,0:T(4,128)(2,1)S(1)} %shard_map.94.refs_0_), channel_id=1, source_target_pairs={{0,2},{1,3},{2,0},{3,1},{4,6},{5,7},{6,4},{7,5},{8,10},{9,11},{10,... | collective-permute-start | bytes 12296 | tf_op jit(solution)/shard_map/ppermute | solution.py:337
  53.6 3.4 %collective-permute-start.4 = (bf16[8,512]{1,0:T(8,128)(2,1)S(1)}, bf16[8,512]{1,0:T(8,128)(2,1)S(1)}, u32[]{:S(2)}, u32[]{:S(2)}) collective-permute-start(bf16[8,512]{1,0:T(8,128)(2,1)S(1)} %shard_map.95.refs_0_), channel_id=1, source_target_pairs={{0,4},{1,5},{2,6},{3,7},{4,0},{5,1},{6,2},{7,3},{8,12},{9,13},{10,... | collective-permute-start | bytes 24584 | tf_op jit(solution)/shard_map/ppermute | solution.py:337
  57.1 4.3 %collective-permute-start.5 = (bf16[16,512]{1,0:T(8,128)(2,1)S(1)}, bf16[16,512]{1,0:T(8,128)(2,1)S(1)}, u32[]{:S(2)}, u32[]{:S(2)}) collective-permute-start(bf16[16,512]{1,0:T(8,128)(2,1)S(1)} %shard_map.96.refs_0_), channel_id=1, source_target_pairs={{0,14},{1,15},{2,12},{3,13},{4,10},{5,11},{6,8},{7,9},{8,6},{9,7},... | collective-permute-start | bytes 49160 | tf_op jit(solution)/shard_map/ppermute | solution.py:337
  61.4 4.3 %collective-permute-start.8 = (bf16[32,512]{1,0:T(8,128)(2,1)S(1)}, bf16[32,512]{1,0:T(8,128)(2,1)S(1)}, u32[]{:S(2)}, u32[]{:S(2)}) collective-permute-start(bf16[32,512]{1,0:T(8,128)(2,1)S(1)} %shard_map.97.refs_0_), channel_id=1, source_target_pairs={{0,32},{1,33},{2,34},{3,35},{4,36},{5,37},{6,38},{7,39},{8,40},{9,... | collective-permute-start | bytes 98312 | tf_op jit(solution)/shard_map/ppermute | solution.py:337
  62.9 4.0 %collective-permute-start.7 = (bf16[32,512]{1,0:T(8,128)(2,1)S(1)}, bf16[32,512]{1,0:T(8,128)(2,1)S(1)}, u32[]{:S(2)}, u32[]{:S(2)}) collective-permute-start(bf16[32,512]{1,0:T(8,128)(2,1)S(1)} %shard_map.97.refs_0_), channel_id=1, source_target_pairs={{0,48},{1,49},{2,50},{3,51},{4,52},{5,53},{6,54},{7,55},{8,56},{9,... | collective-permute-start | bytes 98312 | tf_op jit(solution)/shard_map/ppermute | solution.py:337
  63.9 3.0 %collective-permute-start.6 = (bf16[32,512]{1,0:T(8,128)(2,1)S(1)}, bf16[32,512]{1,0:T(8,128)(2,1)S(1)}, u32[]{:S(2)}, u32[]{:S(2)}) collective-permute-start(bf16[32,512]{1,0:T(8,128)(2,1)S(1)} %shard_map.97.refs_0_), channel_id=1, source_target_pairs={{0,16},{1,17},{2,18},{3,19},{4,20},{5,21},{6,22},{7,23},{8,24},{9,... | collective-permute-start | bytes 98312 | tf_op jit(solution)/shard_map/ppermute | solution.py:337
  66.9 16.5 %collective-permute-start.9 = (bf16[128,512]{1,0:T(8,128)(2,1)S(1)}, bf16[128,512]{1,0:T(8,128)(2,1)S(1)}, u32[]{:S(2)}, u32[]{:S(2)}) collective-permute-start(bf16[128,512]{1,0:T(8,128)(2,1)S(1)} %shard_map.98.near_ref), channel_id=1, source_target_pairs={{0,1},{1,0},{2,3},{3,2},{4,5},{5,4},{6,7},{7,6},{8,9},{9,8},{10,11... | collective-permute-start | bytes 393224 | tf_op jit(solution)/shard_map/ppermute | solution.py:337
  87.2 18.2 %collective-permute-start.19 = (bf16[64,2048]{1,0:T(8,128)(2,1)S(1)}, bf16[64,2048]{1,0:T(8,128)(2,1)S(1)}, u32[]{:S(2)}, u32[]{:S(2)}) collective-permute-start(bf16[64,2048]{1,0:T(8,128)(2,1)S(1)} %get-tuple-element.72), channel_id=1, source_target_pairs={{0,64},{64,128},{128,192},{192,0},{1,65},{65,129},{129,193},{193,1... | collective-permute-start | bytes 786440 | tf_op jit(solution)/shard_map/ppermute | solution.py:470
  97.0 10.3 %collective-permute-start.20 = (bf16[64,2048]{1,0:T(8,128)(2,1)S(1)}, bf16[64,2048]{1,0:T(8,128)(2,1)S(1)}, u32[]{:S(2)}, u32[]{:S(2)}) collective-permute-start(bf16[64,2048]{1,0:T(8,128)(2,1)S(1)} %get-tuple-element.73), channel_id=1, source_target_pairs={{0,128},{64,192},{128,0},{192,64},{1,129},{65,193},{129,1},{193,65... | collective-permute-start | bytes 786440 | tf_op jit(solution)/shard_map/ppermute | solution.py:470
  97.1 15.0 %collective-permute-start.21 = (bf16[64,2048]{1,0:T(8,128)(2,1)S(1)}, bf16[64,2048]{1,0:T(8,128)(2,1)S(1)}, u32[]{:S(2)}, u32[]{:S(2)}) collective-permute-start(bf16[64,2048]{1,0:T(8,128)(2,1)S(1)} %get-tuple-element.74), channel_id=1, source_target_pairs={{0,192},{64,0},{128,64},{192,128},{1,193},{65,1},{129,65},{193,129... | collective-permute-start | bytes 786440 | tf_op jit(solution)/shard_map/ppermute | solution.py:470
  102.9 9.2 %collective-permute-start.16 = (bf16[64,2048]{1,0:T(8,128)(2,1)S(1)}, bf16[64,2048]{1,0:T(8,128)(2,1)S(1)}, u32[]{:S(2)}, u32[]{:S(2)}) collective-permute-start(bf16[64,2048]{1,0:T(8,128)(2,1)S(1)} %get-tuple-element.60), channel_id=1, source_target_pairs={{0,64},{64,128},{128,192},{192,0},{1,65},{65,129},{129,193},{193,1... | collective-permute-start | bytes 786440 | tf_op jit(solution)/shard_map/ppermute | solution.py:470
  103.5 14.2 %collective-permute-start.17 = (bf16[64,2048]{1,0:T(8,128)(2,1)S(1)}, bf16[64,2048]{1,0:T(8,128)(2,1)S(1)}, u32[]{:S(2)}, u32[]{:S(2)}) collective-permute-start(bf16[64,2048]{1,0:T(8,128)(2,1)S(1)} %get-tuple-element.61), channel_id=1, source_target_pairs={{0,128},{64,192},{128,0},{192,64},{1,129},{65,193},{129,1},{193,65... | collective-permute-start | bytes 786440 | tf_op jit(solution)/shard_map/ppermute | solution.py:470
  105.4 18.0 %collective-permute-start.18 = (bf16[64,2048]{1,0:T(8,128)(2,1)S(1)}, bf16[64,2048]{1,0:T(8,128)(2,1)S(1)}, u32[]{:S(2)}, u32[]{:S(2)}) collective-permute-start(bf16[64,2048]{1,0:T(8,128)(2,1)S(1)} %get-tuple-element.62), channel_id=1, source_target_pairs={{0,192},{64,0},{128,64},{192,128},{1,193},{65,1},{129,65},{193,129... | collective-permute-start | bytes 786440 | tf_op jit(solution)/shard_map/ppermute | solution.py:470

commit v5 on v4

--- a/solution.py
+++ b/solution.py
@@ -1,3 +1,5 @@
+import functools
+
 import jax
 import jax.numpy as jnp
 from jax import lax
@@ -17,7 +19,7 @@
 ROW_CHUNK = 256
 CAND_TILE = 256
 CHUNKS = 8
-PARTS = 2
+PARTS = ((0, 6), (6, 8))
 VMEM_BYTES = 16 * 2**20
 LOG2E = 1.4426950408889634
 INV_TURN = 0.15915494309189535
@@ -273,31 +275,32 @@
     )(weights, prior, *kernels)
 
 
-def total_kernel(*refs):
-    *parts, out_ref = refs
-    cands = parts[0].shape[1]
-    for part in range(len(parts) // WIDTHS):
-        own, *others = parts[part * WIDTHS : (part + 1) * WIDTHS]
-        total = own[...]
-        for other in others:
-            total = total + other[...].astype(F32)
-        out_ref[:, part * cands : (part + 1) * cands] = total
-
-
-def total(parts):
-    flat = [block for part in parts for block in part]
-    shape = (flat[0].shape[0], len(parts) * flat[0].shape[1])
-    return pl.pallas_call(
-        total_kernel,
-        out_shape=jax.ShapeDtypeStruct(shape, F32),
-        in_specs=[whole()] * len(flat),
-        out_specs=whole(),
-        compiler_params=params(),
-        cost_estimate=pl.CostEstimate(
-            flops=3 * shape[0] * shape[1], transcendentals=0, bytes_accessed=14 * shape[0] * shape[1]
-        ),
-        name="total",
-    )(*flat)
+def total_kernel(first, *refs):
+    *parts, out_ref, sums, sem = refs
+    total = parts[0][...]
+    for part in parts[1:WIDTHS]:
+        total = total + part[...].astype(F32)
+    sums[...] = total
+    copy = pltpu.make_async_copy(sums, out_ref.at[:, first : first + total.shape[1]], sem)
+    copy.start()
+    copy.wait()
+
+
+def total(parts, first, cands, held):
+    rows, columns = parts[0].shape
+    extra = [] if held is None else [held]
+    return pl.pallas_call(
+        functools.partial(total_kernel, first),
+        out_shape=jax.ShapeDtypeStruct((rows, cands), F32),
+        in_specs=[whole()] * len(parts) + [pl.BlockSpec(memory_space=pl.ANY)] * len(extra),
+        out_specs=pl.BlockSpec(memory_space=pl.ANY),
+        scratch_shapes=[pltpu.VMEM((rows, columns), F32), pltpu.SemaphoreType.DMA(())],
+        input_output_aliases={len(parts): 0} if extra else {},
+        compiler_params=params(),
+        cost_estimate=pl.CostEstimate(
+            flops=3 * rows * columns, transcendentals=0, bytes_accessed=14 * rows * columns
+        ),
+    )(*parts, *extra)
 
 
 def exchange_pairs(mask):
@@ -458,18 +461,19 @@
     coefs = in_order(coef_near, coef_far)
     solved = in_order(weight_near, weight_far)
     rows = lax.axis_size("rows")
-    each = CHUNKS // PARTS
-    parts = []
-    for part in range(PARTS):
-        mine = made[part * each : (part + 1) * each]
+    result = None
+    for first, last in PARTS:
+        mine = made[first:last]
         prior = prior_product(coefs, [m[0] for m in mine])
         own, *away = cross_product(solved, prior, [m[1] for m in mine])
         arrived = []
         for shift, block in enumerate(away, 1):
             pairs = [(i, (i + shift) % rows) for i in range(rows)]
             arrived.append(lax.ppermute(block, "rows", pairs))
-        parts.append([own] + arrived)
-    return total(parts).T
+        cands = grid_coords.shape[1]
+        start = first * (cands // CHUNKS)
+        result = total([own] + arrived, start, cands, result)
+    return result.T
 
 
 def solution(mesh):

time: 126 us -> 125 us (level)
  starting transfers between devices: 46.7 us -> 45 us
    ppermute x6, starting transfers between devices: 7.55 us -> 5.28 us  [body(): arrived.append(lax.ppermute(block, 'rows', pairs))]
    ppermute x6, waiting for transfers between devices: 16 us -> 14.2 us  [body(): arrived.append(lax.ppermute(block, 'rows', pairs))]
where the time goes in v5:
time: 125 us; the launch traced here: 122 us
  waiting for transfers between devices  45.5 us (36%)
  starting transfers between devices  45 us (36%)
  Pallas kernels  30.8 us (25%)
    ppermute x13, starting transfers between devices, swap(): return lax.ppermute(held, 'cand', pairs)  37.1 us
    pallas_call x8, Pallas kernels, tiles(): pl.pallas_call(tile_kernel, out_shape=(jax.ShapeDtypeStruct((feats, cands...  19 us
    ppermute x13, waiting for transfers between devices, swap(): return lax.ppermute(held, 'cand', pairs)  18.9 us
    ppermute x6, waiting for transfers between devices, body(): arrived.append(lax.ppermute(block, 'rows', pairs))  14.2 us
    ppermute x3, waiting for transfers between devices, solve_chain(): carried = lax.ppermute(carried, 'rows', [(section, section - 1)])  12.4 us
    ppermute x6, starting transfers between devices, body(): arrived.append(lax.ppermute(block, 'rows', pairs))  5.28 us
    pallas_call x2, Pallas kernels, prior_product(): pl.pallas_call(prior_kernel, out_shape=jax.ShapeDtypeStruct((rows, cands)...  4.64 us
    ppermute x3, starting transfers between devices, solve_chain(): carried = lax.ppermute(carried, 'rows', [(section, section - 1)])  2.62 us
  transfers between devices with their start and end apart: 22, of which 14 were waited for; matrix products, arithmetic and copies ran while one was open for 0% of the time, Pallas kernels for 20%

profile of v5, /device:TPU:1, one launch (start us, length us, event | category | flops | bytes accessed | tf_op | source)
XLA Modules:
  0.0 122.4 jit_solution(15414594933585621381)
XLA Ops:
  0.0 2.5 %collective-permute-start.10 = (bf16[4,2048]{1,0:T(4,128)(2,1)}, bf16[4,2048]{1,0:T(4,128)(2,1)S(1)}, u32[]{:S(2)}, u32[]{:S(2)}) collective-permute-start(bf16[4,2048]{1,0:T(4,128)(2,1)} %refs_0_.3), channel_id=1, source_target_pairs={{0,2},{1,3},{2,0},{3,1},{4,6},{5,7},{6,4},{7,5},{8,10},{9,11},{10,... | collective-permute-start | bytes 49160 | tf_op jit(solution)/shard_map/ppermute | solution.py:340
  2.5 1.3 %collective-permute-done.10.refs_1_ = bf16[4,2048]{1,0:T(4,128)(2,1)S(1)} collective-permute-done((bf16[4,2048]{1,0:T(4,128)(2,1)}, bf16[4,2048]{1,0:T(4,128)(2,1)S(1)}, u32[]{:S(2)}, u32[]{:S(2)}) %collective-permute-start.10) | collective-permute-done | bytes 16416 | tf_op jit(solution)/shard_map/ppermute | solution.py:340
  3.8 0.7 copy-done.1
  4.5 3.1 %collective-permute-start.11 = (bf16[8,2048]{1,0:T(8,128)(2,1)S(1)}, bf16[8,2048]{1,0:T(8,128)(2,1)S(1)}, u32[]{:S(2)}, u32[]{:S(2)}) collective-permute-start(bf16[8,2048]{1,0:T(8,128)(2,1)S(1)} %shard_map.100.refs_0_), channel_id=1, source_target_pairs={{0,4},{1,5},{2,6},{3,7},{4,0},{5,1},{6,2},{7,3},{8,12},{9,13},{10,... | collective-permute-start | bytes 98312 | tf_op jit(solution)/shard_map/ppermute | solution.py:340
  7.6 1.3 %collective-permute-done.11.refs_1_ = bf16[8,2048]{1,0:T(8,128)(2,1)S(1)} collective-permute-done((bf16[8,2048]{1,0:T(8,128)(2,1)S(1)}, bf16[8,2048]{1,0:T(8,128)(2,1)S(1)}, u32[]{:S(2)}, u32[]{:S(2)}) %collective-permute-start.11) | collective-permute-done | bytes 32800 | tf_op jit(solution)/shard_map/ppermute | solution.py:340
  8.9 4.8 %collective-permute-start.12 = (bf16[16,2048]{1,0:T(8,128)(2,1)S(1)}, bf16[16,2048]{1,0:T(8,128)(2,1)S(1)}, u32[]{:S(2)}, u32[]{:S(2)}) collective-permute-start(bf16[16,2048]{1,0:T(8,128)(2,1)S(1)} %shard_map.101.refs_0_), channel_id=1, source_target_pairs={{0,14},{1,15},{2,12},{3,13},{4,10},{5,11},{6,8},{7,9},{8,6},{9,7},... | collective-permute-start | bytes 196616 | tf_op jit(solution)/shard_map/ppermute | solution.py:340
  13.7 2.0 %collective-permute-done.12.refs_1_ = bf16[16,2048]{1,0:T(8,128)(2,1)S(1)} collective-permute-done((bf16[16,2048]{1,0:T(8,128)(2,1)S(1)}, bf16[16,2048]{1,0:T(8,128)(2,1)S(1)}, u32[]{:S(2)}, u32[]{:S(2)}) %collective-permute-start.12) | collective-permute-done | bytes 65568 | tf_op jit(solution)/shard_map/ppermute | solution.py:340
  15.7 1.3 %collective-permute-start.13 = (bf16[32,2048]{1,0:T(8,128)(2,1)S(1)}, bf16[32,2048]{1,0:T(8,128)(2,1)S(1)}, u32[]{:S(2)}, u32[]{:S(2)}) collective-permute-start(bf16[32,2048]{1,0:T(8,128)(2,1)S(1)} %shard_map.102.refs_0_), channel_id=1, source_target_pairs={{0,16},{1,17},{2,18},{3,19},{4,20},{5,21},{6,22},{7,23},{8,24},{9,... | collective-permute-start | bytes 393224 | tf_op jit(solution)/shard_map/ppermute | solution.py:340
  17.0 2.6 %collective-permute-done.13.refs_1_ = bf16[32,2048]{1,0:T(8,128)(2,1)S(1)} collective-permute-done((bf16[32,2048]{1,0:T(8,128)(2,1)S(1)}, bf16[32,2048]{1,0:T(8,128)(2,1)S(1)}, u32[]{:S(2)}, u32[]{:S(2)}) %collective-permute-start.13) | collective-permute-done | bytes 131104 | tf_op jit(solution)/shard_map/ppermute | solution.py:340
  19.6 2.6 %collective-permute-start.14 = (bf16[64,2048]{1,0:T(8,128)(2,1)S(1)}, bf16[64,2048]{1,0:T(8,128)(2,1)S(1)}, u32[]{:S(2)}, u32[]{:S(2)}) collective-permute-start(bf16[64,2048]{1,0:T(8,128)(2,1)S(1)} %shard_map.103.refs_0_), channel_id=1, source_target_pairs={{0,48},{1,49},{2,50},{3,51},{4,52},{5,53},{6,54},{7,55},{8,56},{9,... | collective-permute-start | bytes 786440 | tf_op jit(solution)/shard_map/ppermute | solution.py:340
  22.2 4.0 %collective-permute-done.14.refs_1_ = bf16[64,2048]{1,0:T(8,128)(2,1)S(1)} collective-permute-done((bf16[64,2048]{1,0:T(8,128)(2,1)S(1)}, bf16[64,2048]{1,0:T(8,128)(2,1)S(1)}, u32[]{:S(2)}, u32[]{:S(2)}) %collective-permute-start.14) | collective-permute-done | bytes 262176 | tf_op jit(solution)/shard_map/ppermute | solution.py:340
  26.2 6.7 %collective-permute-start.15 = (bf16[128,2048]{1,0:T(8,128)(2,1)S(1)}, bf16[128,2048]{1,0:T(8,128)(2,1)S(1)}, u32[]{:S(2)}, u32[]{:S(2)}) collective-permute-start(bf16[128,2048]{1,0:T(8,128)(2,1)S(1)} %shard_map.104.near_ref), channel_id=1, source_target_pairs={{0,1},{1,0},{2,3},{3,2},{4,5},{5,4},{6,7},{7,6},{8,9},{9,8},{10,11... | collective-permute-start | bytes 1572872 | tf_op jit(solution)/shard_map/ppermute | solution.py:340
  32.9 2.6 %prepare.1 = (bf16[2048,128]{1,0:T(8,128)(2,1)S(1)}, bf16[512,128]{1,0:T(8,128)(2,1)S(1)}, bf16[128,4096]{1,0:T(8,128)(2,1)S(1)}, f32[512,512]{1,0:T(8,128)S(1)}, f32[512,1536]{1,0:T(8,128)S(1)}) custom-call(f32[22,2048]{1,0:T(8,128)} %refs_0_.2, f32[1,2048]{1,0:T(1,128)} %bitcast.3, f32[22,512]{1,0:T(8,128)} %refs_2_.1, f32[1,22]{1,0:T(1,128)} %bitcast.4, ...), custom_call_target="tpu_custom_call" | custom-call | flops 10000000 | bytes 8388608 | tf_op jit(solution)/shard_map/prepare/pallas_call | solution.py:107
  35.5 0.7 collective-permute-start
  36.2 0.7 collective-permute-start.1
  36.9 1.3 %collective-permute-start.2 = (f32[4,512]{1,0:T(4,128)S(1)}, f32[4,512]{1,0:T(4,128)S(1)}, u32[]{:S(2)}, u32[]{:S(2)}) collective-permute-start(f32[4,512]{1,0:T(4,128)S(1)} %get-tuple-element.46), channel_id=1, source_target_pairs={{64,0},{65,1},{66,2},{67,3},{68,4},{69,5},{70,6},{71,7},{72,8},{73... | collective-permute-start | bytes 24584 | tf_op jit(solution)/shard_map/ppermute | solution.py:439
  38.2 12.4 %collective-permute-done.2.refs_0_ = f32[4,512]{1,0:T(4,128)S(1)} collective-permute-done((f32[4,512]{1,0:T(4,128)S(1)}, f32[4,512]{1,0:T(4,128)S(1)}, u32[]{:S(2)}, u32[]{:S(2)}) %collective-permute-start.2) | collective-permute-done | bytes 8224 | tf_op jit(solution)/shard_map/ppermute | solution.py:439
  50.6 0.5 shard_map.94.refs_0_
  51.1 1.0 collective-permute-start.3
  52.1 1.5 %collective-permute-done.3.refs_1_ = bf16[4,512]{1,0:T(4,128)(2,1)S(1)} collective-permute-done((bf16[4,512]{1,0:T(4,128)(2,1)S(1)}, bf16[4,512]{1,0:T(4,128)(2,1)S(1)}, u32[]{:S(2)}, u32[]{:S(2)}) %collective-permute-start.3) | collective-permute-done | bytes 4128 | tf_op jit(solution)/shard_map/ppermute | solution.py:340
  53.6 1.5 %collective-permute-start.4 = (bf16[8,512]{1,0:T(8,128)(2,1)S(1)}, bf16[8,512]{1,0:T(8,128)(2,1)S(1)}, u32[]{:S(2)}, u32[]{:S(2)}) collective-permute-start(bf16[8,512]{1,0:T(8,128)(2,1)S(1)} %shard_map.95.refs_0_), channel_id=1, source_target_pairs={{0,4},{1,5},{2,6},{3,7},{4,0},{5,1},{6,2},{7,3},{8,12},{9,13},{10,... | collective-permute-start | bytes 24584 | tf_op jit(solution)/shard_map/ppermute | solution.py:340
  55.1 1.9 %collective-permute-done.4.refs_1_ = bf16[8,512]{1,0:T(8,128)(2,1)S(1)} collective-permute-done((bf16[8,512]{1,0:T(8,128)(2,1)S(1)}, bf16[8,512]{1,0:T(8,128)(2,1)S(1)}, u32[]{:S(2)}, u32[]{:S(2)}) %collective-permute-start.4) | collective-permute-done | bytes 8224 | tf_op jit(solution)/shard_map/ppermute | solution.py:340
  57.1 3.2 %collective-permute-start.5 = (bf16[16,512]{1,0:T(8,128)(2,1)S(1)}, bf16[16,512]{1,0:T(8,128)(2,1)S(1)}, u32[]{:S(2)}, u32[]{:S(2)}) collective-permute-start(bf16[16,512]{1,0:T(8,128)(2,1)S(1)} %shard_map.96.refs_0_), channel_id=1, source_target_pairs={{0,14},{1,15},{2,12},{3,13},{4,10},{5,11},{6,8},{7,9},{8,6},{9,7},... | collective-permute-start | bytes 49160 | tf_op jit(solution)/shard_map/ppermute | solution.py:340
  60.3 1.1 collective-permute-done.5.refs_1_
  61.4 2.5 %collective-permute-start.7 = (bf16[32,512]{1,0:T(8,128)(2,1)S(1)}, bf16[32,512]{1,0:T(8,128)(2,1)S(1)}, u32[]{:S(2)}, u32[]{:S(2)}) collective-permute-start(bf16[32,512]{1,0:T(8,128)(2,1)S(1)} %shard_map.97.refs_0_), channel_id=1, source_target_pairs={{0,48},{1,49},{2,50},{3,51},{4,52},{5,53},{6,54},{7,55},{8,56},{9,... | collective-permute-start | bytes 98312 | tf_op jit(solution)/shard_map/ppermute | solution.py:340
  63.9 1.2 collective-permute-start.8
  65.4 2.8 %collective-permute-done.8.refs_3_ = bf16[32,512]{1,0:T(8,128)(2,1)S(1)} collective-permute-done((bf16[32,512]{1,0:T(8,128)(2,1)S(1)}, bf16[32,512]{1,0:T(8,128)(2,1)S(1)}, u32[]{:S(2)}, u32[]{:S(2)}) %collective-permute-start.8) | collective-permute-done | bytes 32800 | tf_op jit(solution)/shard_map/ppermute | solution.py:340
  68.2 6.9 %collective-permute-start.9 = (bf16[128,512]{1,0:T(8,128)(2,1)S(1)}, bf16[128,512]{1,0:T(8,128)(2,1)S(1)}, u32[]{:S(2)}, u32[]{:S(2)}) collective-permute-start(bf16[128,512]{1,0:T(8,128)(2,1)S(1)} %shard_map.98.near_ref), channel_id=1, source_target_pairs={{0,1},{1,0},{2,3},{3,2},{4,5},{5,4},{6,7},{7,6},{8,9},{9,8},{10,11... | collective-permute-start | bytes 393224 | tf_op jit(solution)/shard_map/ppermute | solution.py:340
  75.1 2.4 %shard_map.110 = (bf16[2048,512]{1,0:T(8,128)(2,1)S(1)}, bf16[512,512]{1,0:T(8,128)(2,1)S(1)}) custom-call(bf16[2048,128]{1,0:T(8,128)(2,1)S(1)} %get-tuple-element.48.turns_ref, bf16[512,128]{1,0:T(8,128)(2,1)S(1)} %get-tuple-element.49.exponent_ref, bf16[128,4096]{1,0:T(8,128)(2,1)S(1)} %get-tuple-element.50.levels_ref), custom_call_target="tpu_custom_call" | custom-call | flops 31457280 | bytes 2621440 | tf_op jit(solution)/shard_map/pallas_call | solution.py:160
  77.5 2.4 %shard_map.111 = (bf16[2048,512]{1,0:T(8,128)(2,1)S(1)}, bf16[512,512]{1,0:T(8,128)(2,1)S(1)}) custom-call(bf16[2048,128]{1,0:T(8,128)(2,1)S(1)} %get-tuple-element.48.turns_ref, bf16[512,128]{1,0:T(8,128)(2,1)S(1)} %get-tuple-element.49.exponent_ref, bf16[128,4096]{1,0:T(8,128)(2,1)S(1)} %get-tuple-element.50.levels_ref), custom_call_target="tpu_custom_call" | custom-call | flops 31457280 | bytes 2621440 | tf_op jit(solution)/shard_map/pallas_call | solution.py:160
  79.8 2.4 %shard_map.112 = (bf16[2048,512]{1,0:T(8,128)(2,1)S(1)}, bf16[512,512]{1,0:T(8,128)(2,1)S(1)}) custom-call(bf16[2048,128]{1,0:T(8,128)(2,1)S(1)} %get-tuple-element.48.turns_ref, bf16[512,128]{1,0:T(8,128)(2,1)S(1)} %get-tuple-element.49.exponent_ref, bf16[128,4096]{1,0:T(8,128)(2,1)S(1)} %get-tuple-element.50.levels_ref), custom_call_target="tpu_custom_call" | custom-call | flops 31457280 | bytes 2621440 | tf_op jit(solution)/shard_map/pallas_call | solution.py:160
  82.2 2.4 %shard_map.113 = (bf16[2048,512]{1,0:T(8,128)(2,1)S(1)}, bf16[512,512]{1,0:T(8,128)(2,1)S(1)}) custom-call(bf16[2048,128]{1,0:T(8,128)(2,1)S(1)} %get-tuple-element.48.turns_ref, bf16[512,128]{1,0:T(8,128)(2,1)S(1)} %get-tuple-element.49.exponent_ref, bf16[128,4096]{1,0:T(8,128)(2,1)S(1)} %get-tuple-element.50.levels_ref), custom_call_target="tpu_custom_call" | custom-call | flops 31457280 | bytes 2621440 | tf_op jit(solution)/shard_map/pallas_call | solution.py:160
  84.6 2.4 %shard_map.114 = (bf16[2048,512]{1,0:T(8,128)(2,1)S(1)}, bf16[512,512]{1,0:T(8,128)(2,1)S(1)}) custom-call(bf16[2048,128]{1,0:T(8,128)(2,1)S(1)} %get-tuple-element.48.turns_ref, bf16[512,128]{1,0:T(8,128)(2,1)S(1)} %get-tuple-element.49.exponent_ref, bf16[128,4096]{1,0:T(8,128)(2,1)S(1)} %get-tuple-element.50.levels_ref), custom_call_target="tpu_custom_call" | custom-call | flops 31457280 | bytes 2621440 | tf_op jit(solution)/shard_map/pallas_call | solution.py:160
  87.0 2.4 %shard_map.115 = (bf16[2048,512]{1,0:T(8,128)(2,1)S(1)}, bf16[512,512]{1,0:T(8,128)(2,1)S(1)}) custom-call(bf16[2048,128]{1,0:T(8,128)(2,1)S(1)} %get-tuple-element.48.turns_ref, bf16[512,128]{1,0:T(8,128)(2,1)S(1)} %get-tuple-element.49.exponent_ref, bf16[128,4096]{1,0:T(8,128)(2,1)S(1)} %get-tuple-element.50.levels_ref), custom_call_target="tpu_custom_call" | custom-call | flops 31457280 | bytes 2621440 | tf_op jit(solution)/shard_map/pallas_call | solution.py:160
  90.1 3.4 %shard_map.116.prior_ref = f32[256,3072]{1,0:T(8,128)S(1)} custom-call(bf16[256,2048]{1,0:T(8,128)(2,1)S(1)} %shard_map.105.coef_ref, bf16[2048,512]{1,0:T(8,128)(2,1)S(1)} %get-tuple-element.59.refs_0_, bf16[2048,512]{1,0:T(8,128)(2,1)S(1)} %get-tuple-element.60.refs_1_, bf16[2048,512]{1,0:T(8,128)(2,1)S(1)} %get-tuple-element.61.refs_2_, ...), custom_call_target="tpu_custom_call" | custom-call | flops 3221225472 | bytes 12582912 | tf_op jit(solution)/shard_map/pallas_call | solution.py:247
  93.5 1.0 shard_map.117
  94.7 2.6 %collective-permute-start.21 = (bf16[64,3072]{1,0:T(8,128)(2,1)S(1)}, bf16[64,3072]{1,0:T(8,128)(2,1)S(1)}, u32[]{:S(2)}, u32[]{:S(2)}) collective-permute-start(bf16[64,3072]{1,0:T(8,128)(2,1)S(1)} %get-tuple-element.74), channel_id=1, source_target_pairs={{0,192},{64,0},{128,64},{192,128},{1,193},{65,1},{129,65},{193,129... | collective-permute-start | bytes 1179656 | tf_op jit(solution)/shard_map/ppermute | solution.py:472
  97.3 2.4 %shard_map.106 = (bf16[2048,512]{1,0:T(8,128)(2,1)S(1)}, bf16[512,512]{1,0:T(8,128)(2,1)S(1)}) custom-call(bf16[2048,128]{1,0:T(8,128)(2,1)S(1)} %get-tuple-element.48.turns_ref, bf16[512,128]{1,0:T(8,128)(2,1)S(1)} %get-tuple-element.49.exponent_ref, bf16[128,4096]{1,0:T(8,128)(2,1)S(1)} %get-tuple-element.50.levels_ref), custom_call_target="tpu_custom_call" | custom-call | flops 31457280 | bytes 2621440 | tf_op jit(solution)/shard_map/pallas_call | solution.py:160
  99.7 2.4 %shard_map.107 = (bf16[2048,512]{1,0:T(8,128)(2,1)S(1)}, bf16[512,512]{1,0:T(8,128)(2,1)S(1)}) custom-call(bf16[2048,128]{1,0:T(8,128)(2,1)S(1)} %get-tuple-element.48.turns_ref, bf16[512,128]{1,0:T(8,128)(2,1)S(1)} %get-tuple-element.49.exponent_ref, bf16[128,4096]{1,0:T(8,128)(2,1)S(1)} %get-tuple-element.50.levels_ref), custom_call_target="tpu_custom_call" | custom-call | flops 31457280 | bytes 2621440 | tf_op jit(solution)/shard_map/pallas_call | solution.py:160
  102.0 1.2 %shard_map.108.prior_ref = f32[256,1024]{1,0:T(8,128)S(1)} custom-call(bf16[256,2048]{1,0:T(8,128)(2,1)S(1)} %shard_map.105.coef_ref, bf16[2048,512]{1,0:T(8,128)(2,1)S(1)} %get-tuple-element.51.refs_0_, bf16[2048,512]{1,0:T(8,128)(2,1)S(1)} %get-tuple-element.52.refs_1_), custom_call_target="tpu_custom_call" | custom-call | flops 1073741824 | bytes 4194304 | tf_op jit(solution)/shard_map/pallas_call | solution.py:247
  103.3 0.4 shard_map.109
  103.7 0.7 collective-permute-start.16
  104.4 1.9 %collective-permute-start.17 = (bf16[64,1024]{1,0:T(8,128)(2,1)S(1)}, bf16[64,1024]{1,0:T(8,128)(2,1)S(1)}, u32[]{:S(2)}, u32[]{:S(2)}) collective-permute-start(bf16[64,1024]{1,0:T(8,128)(2,1)S(1)} %get-tuple-element.57), channel_id=1, source_target_pairs={{0,128},{64,192},{128,0},{192,64},{1,129},{65,193},{129,1},{193,65... | collective-permute-start | bytes 393224 | tf_op jit(solution)/shard_map/ppermute | solution.py:472
  106.3 11.4 %collective-permute-done.19.refs_1_ = bf16[64,3072]{1,0:T(8,128)(2,1)S(1)} collective-permute-done((bf16[64,3072]{1,0:T(8,128)(2,1)S(1)}, bf16[64,3072]{1,0:T(8,128)(2,1)S(1)}, u32[]{:S(2)}, u32[]{:S(2)}) %collective-permute-start.19) | collective-permute-done | bytes 393248 | tf_op jit(solution)/shard_map/ppermute | solution.py:472
  117.7 1.0 shard_map.118.refs_4_
  118.7 1.7 %collective-permute-done.16.refs_1_ = bf16[64,1024]{1,0:T(8,128)(2,1)S(1)} collective-permute-done((bf16[64,1024]{1,0:T(8,128)(2,1)S(1)}, bf16[64,1024]{1,0:T(8,128)(2,1)S(1)}, u32[]{:S(2)}, u32[]{:S(2)}) %collective-permute-start.16) | collective-permute-done | bytes 131104 | tf_op jit(solution)/shard_map/ppermute | solution.py:472
  120.5 1.0 collective-permute-done.18.refs_3_
  121.5 0.8 shard_map.119
  (30 shorter events, 1.4 us)
Async XLA Ops:
  0.0 3.8 %collective-permute-start.10 = (bf16[4,2048]{1,0:T(4,128)(2,1)}, bf16[4,2048]{1,0:T(4,128)(2,1)S(1)}, u32[]{:S(2)}, u32[]{:S(2)}) collective-permute-start(bf16[4,2048]{1,0:T(4,128)(2,1)} %refs_0_.3), channel_id=1, source_target_pairs={{0,2},{1,3},{2,0},{3,1},{4,6},{5,7},{6,4},{7,5},{8,10},{9,11},{10,... | collective-permute-start | bytes 49160 | tf_op jit(solution)/shard_map/ppermute | solution.py:340
  3.8 0.7 copy-start.1
  4.5 4.4 %collective-permute-start.11 = (bf16[8,2048]{1,0:T(8,128)(2,1)S(1)}, bf16[8,2048]{1,0:T(8,128)(2,1)S(1)}, u32[]{:S(2)}, u32[]{:S(2)}) collective-permute-start(bf16[8,2048]{1,0:T(8,128)(2,1)S(1)} %shard_map.100.refs_0_), channel_id=1, source_target_pairs={{0,4},{1,5},{2,6},{3,7},{4,0},{5,1},{6,2},{7,3},{8,12},{9,13},{10,... | collective-permute-start | bytes 98312 | tf_op jit(solution)/shard_map/ppermute | solution.py:340
  8.9 6.8 %collective-permute-start.12 = (bf16[16,2048]{1,0:T(8,128)(2,1)S(1)}, bf16[16,2048]{1,0:T(8,128)(2,1)S(1)}, u32[]{:S(2)}, u32[]{:S(2)}) collective-permute-start(bf16[16,2048]{1,0:T(8,128)(2,1)S(1)} %shard_map.101.refs_0_), channel_id=1, source_target_pairs={{0,14},{1,15},{2,12},{3,13},{4,10},{5,11},{6,8},{7,9},{8,6},{9,7},... | collective-permute-start | bytes 196616 | tf_op jit(solution)/shard_map/ppermute | solution.py:340
  15.7 3.9 %collective-permute-start.13 = (bf16[32,2048]{1,0:T(8,128)(2,1)S(1)}, bf16[32,2048]{1,0:T(8,128)(2,1)S(1)}, u32[]{:S(2)}, u32[]{:S(2)}) collective-permute-start(bf16[32,2048]{1,0:T(8,128)(2,1)S(1)} %shard_map.102.refs_0_), channel_id=1, source_target_pairs={{0,16},{1,17},{2,18},{3,19},{4,20},{5,21},{6,22},{7,23},{8,24},{9,... | collective-permute-start | bytes 393224 | tf_op jit(solution)/shard_map/ppermute | solution.py:340
  19.6 6.5 %collective-permute-start.14 = (bf16[64,2048]{1,0:T(8,128)(2,1)S(1)}, bf16[64,2048]{1,0:T(8,128)(2,1)S(1)}, u32[]{:S(2)}, u32[]{:S(2)}) collective-permute-start(bf16[64,2048]{1,0:T(8,128)(2,1)S(1)} %shard_map.103.refs_0_), channel_id=1, source_target_pairs={{0,48},{1,49},{2,50},{3,51},{4,52},{5,53},{6,54},{7,55},{8,56},{9,... | collective-permute-start | bytes 786440 | tf_op jit(solution)/shard_map/ppermute | solution.py:340
  26.2 63.5 %collective-permute-start.15 = (bf16[128,2048]{1,0:T(8,128)(2,1)S(1)}, bf16[128,2048]{1,0:T(8,128)(2,1)S(1)}, u32[]{:S(2)}, u32[]{:S(2)}) collective-permute-start(bf16[128,2048]{1,0:T(8,128)(2,1)S(1)} %shard_map.104.near_ref), channel_id=1, source_target_pairs={{0,1},{1,0},{2,3},{3,2},{4,5},{5,4},{6,7},{7,6},{8,9},{9,8},{10,11... | collective-permute-start | bytes 1572872 | tf_op jit(solution)/shard_map/ppermute | solution.py:340
  32.9 2.6 %copy-start = (f32[4,512]{1,0:T(4,128)S(1)}, f32[4,512]{1,0:T(4,128)}, u32[]{:S(2)}) copy-start(f32[4,512]{1,0:T(4,128)} %whitened_ref.7) | copy-start | bytes 24580
  35.5 0.7 collective-permute-start
  36.2 0.7 collective-permute-start.1
  36.9 13.7 %collective-permute-start.2 = (f32[4,512]{1,0:T(4,128)S(1)}, f32[4,512]{1,0:T(4,128)S(1)}, u32[]{:S(2)}, u32[]{:S(2)}) collective-permute-start(f32[4,512]{1,0:T(4,128)S(1)} %get-tuple-element.46), channel_id=1, source_target_pairs={{64,0},{65,1},{66,2},{67,3},{68,4},{69,5},{70,6},{71,7},{72,8},{73... | collective-permute-start | bytes 24584 | tf_op jit(solution)/shard_map/ppermute | solution.py:439
  51.1 2.5 %collective-permute-start.3 = (bf16[4,512]{1,0:T(4,128)(2,1)S(1)}, bf16[4,512]{1,0:T(4,128)(2,1)S(1)}, u32[]{:S(2)}, u32[]{:S(2)}) collective-permute-start(bf16[4,512]{1,0:T(4,128)(2,1)S(1)} %shard_map.94.refs_0_), channel_id=1, source_target_pairs={{0,2},{1,3},{2,0},{3,1},{4,6},{5,7},{6,4},{7,5},{8,10},{9,11},{10,... | collective-permute-start | bytes 12296 | tf_op jit(solution)/shard_map/ppermute | solution.py:340
  53.6 3.4 %collective-permute-start.4 = (bf16[8,512]{1,0:T(8,128)(2,1)S(1)}, bf16[8,512]{1,0:T(8,128)(2,1)S(1)}, u32[]{:S(2)}, u32[]{:S(2)}) collective-permute-start(bf16[8,512]{1,0:T(8,128)(2,1)S(1)} %shard_map.95.refs_0_), channel_id=1, source_target_pairs={{0,4},{1,5},{2,6},{3,7},{4,0},{5,1},{6,2},{7,3},{8,12},{9,13},{10,... | collective-permute-start | bytes 24584 | tf_op jit(solution)/shard_map/ppermute | solution.py:340
  57.1 4.3 %collective-permute-start.5 = (bf16[16,512]{1,0:T(8,128)(2,1)S(1)}, bf16[16,512]{1,0:T(8,128)(2,1)S(1)}, u32[]{:S(2)}, u32[]{:S(2)}) collective-permute-start(bf16[16,512]{1,0:T(8,128)(2,1)S(1)} %shard_map.96.refs_0_), channel_id=1, source_target_pairs={{0,14},{1,15},{2,12},{3,13},{4,10},{5,11},{6,8},{7,9},{8,6},{9,7},... | collective-permute-start | bytes 49160 | tf_op jit(solution)/shard_map/ppermute | solution.py:340
  61.4 3.7 %collective-permute-start.6 = (bf16[32,512]{1,0:T(8,128)(2,1)S(1)}, bf16[32,512]{1,0:T(8,128)(2,1)S(1)}, u32[]{:S(2)}, u32[]{:S(2)}) collective-permute-start(bf16[32,512]{1,0:T(8,128)(2,1)S(1)} %shard_map.97.refs_0_), channel_id=1, source_target_pairs={{0,16},{1,17},{2,18},{3,19},{4,20},{5,21},{6,22},{7,23},{8,24},{9,... | collective-permute-start | bytes 98312 | tf_op jit(solution)/shard_map/ppermute | solution.py:340
  61.4 4.0 %collective-permute-start.7 = (bf16[32,512]{1,0:T(8,128)(2,1)S(1)}, bf16[32,512]{1,0:T(8,128)(2,1)S(1)}, u32[]{:S(2)}, u32[]{:S(2)}) collective-permute-start(bf16[32,512]{1,0:T(8,128)(2,1)S(1)} %shard_map.97.refs_0_), channel_id=1, source_target_pairs={{0,48},{1,49},{2,50},{3,51},{4,52},{5,53},{6,54},{7,55},{8,56},{9,... | collective-permute-start | bytes 98312 | tf_op jit(solution)/shard_map/ppermute | solution.py:340
  63.9 4.3 %collective-permute-start.8 = (bf16[32,512]{1,0:T(8,128)(2,1)S(1)}, bf16[32,512]{1,0:T(8,128)(2,1)S(1)}, u32[]{:S(2)}, u32[]{:S(2)}) collective-permute-start(bf16[32,512]{1,0:T(8,128)(2,1)S(1)} %shard_map.97.refs_0_), channel_id=1, source_target_pairs={{0,32},{1,33},{2,34},{3,35},{4,36},{5,37},{6,38},{7,39},{8,40},{9,... | collective-permute-start | bytes 98312 | tf_op jit(solution)/shard_map/ppermute | solution.py:340
  68.2 21.3 %collective-permute-start.9 = (bf16[128,512]{1,0:T(8,128)(2,1)S(1)}, bf16[128,512]{1,0:T(8,128)(2,1)S(1)}, u32[]{:S(2)}, u32[]{:S(2)}) collective-permute-start(bf16[128,512]{1,0:T(8,128)(2,1)S(1)} %shard_map.98.near_ref), channel_id=1, source_target_pairs={{0,1},{1,0},{2,3},{3,2},{4,5},{5,4},{6,7},{7,6},{8,9},{9,8},{10,11... | collective-permute-start | bytes 393224 | tf_op jit(solution)/shard_map/ppermute | solution.py:340
  94.5 23.2 %collective-permute-start.19 = (bf16[64,3072]{1,0:T(8,128)(2,1)S(1)}, bf16[64,3072]{1,0:T(8,128)(2,1)S(1)}, u32[]{:S(2)}, u32[]{:S(2)}) collective-permute-start(bf16[64,3072]{1,0:T(8,128)(2,1)S(1)} %get-tuple-element.72), channel_id=1, source_target_pairs={{0,64},{64,128},{128,192},{192,0},{1,65},{65,129},{129,193},{193,1... | collective-permute-start | bytes 1179656 | tf_op jit(solution)/shard_map/ppermute | solution.py:472
  94.6 23.1 %collective-permute-start.20 = (bf16[64,3072]{1,0:T(8,128)(2,1)S(1)}, bf16[64,3072]{1,0:T(8,128)(2,1)S(1)}, u32[]{:S(2)}, u32[]{:S(2)}) collective-permute-start(bf16[64,3072]{1,0:T(8,128)(2,1)S(1)} %get-tuple-element.73), channel_id=1, source_target_pairs={{0,128},{64,192},{128,0},{192,64},{1,129},{65,193},{129,1},{193,65... | collective-permute-start | bytes 1179656 | tf_op jit(solution)/shard_map/ppermute | solution.py:472
  94.7 23.0 %collective-permute-start.21 = (bf16[64,3072]{1,0:T(8,128)(2,1)S(1)}, bf16[64,3072]{1,0:T(8,128)(2,1)S(1)}, u32[]{:S(2)}, u32[]{:S(2)}) collective-permute-start(bf16[64,3072]{1,0:T(8,128)(2,1)S(1)} %get-tuple-element.74), channel_id=1, source_target_pairs={{0,192},{64,0},{128,64},{192,128},{1,193},{65,1},{129,65},{193,129... | collective-permute-start | bytes 1179656 | tf_op jit(solution)/shard_map/ppermute | solution.py:472
  103.7 16.8 %collective-permute-start.16 = (bf16[64,1024]{1,0:T(8,128)(2,1)S(1)}, bf16[64,1024]{1,0:T(8,128)(2,1)S(1)}, u32[]{:S(2)}, u32[]{:S(2)}) collective-permute-start(bf16[64,1024]{1,0:T(8,128)(2,1)S(1)} %get-tuple-element.56), channel_id=1, source_target_pairs={{0,64},{64,128},{128,192},{192,0},{1,65},{65,129},{129,193},{193,1... | collective-permute-start | bytes 393224 | tf_op jit(solution)/shard_map/ppermute | solution.py:472
  104.4 16.1 %collective-permute-start.17 = (bf16[64,1024]{1,0:T(8,128)(2,1)S(1)}, bf16[64,1024]{1,0:T(8,128)(2,1)S(1)}, u32[]{:S(2)}, u32[]{:S(2)}) collective-permute-start(bf16[64,1024]{1,0:T(8,128)(2,1)S(1)} %get-tuple-element.57), channel_id=1, source_target_pairs={{0,128},{64,192},{128,0},{192,64},{1,129},{65,193},{129,1},{193,65... | collective-permute-start | bytes 393224 | tf_op jit(solution)/shard_map/ppermute | solution.py:472
  117.7 3.8 %collective-permute-start.18 = (bf16[64,1024]{1,0:T(8,128)(2,1)S(1)}, bf16[64,1024]{1,0:T(8,128)(2,1)S(1)}, u32[]{:S(2)}, u32[]{:S(2)}) collective-permute-start(bf16[64,1024]{1,0:T(8,128)(2,1)S(1)} %get-tuple-element.58), channel_id=1, source_target_pairs={{0,192},{64,0},{128,64},{192,128},{1,193},{65,1},{129,65},{193,129... | collective-permute-start | bytes 393224 | tf_op jit(solution)/shard_map/ppermute | solution.py:472

commit v6 on v5

--- a/solution.py
+++ b/solution.py
@@ -228,17 +228,41 @@
 
 
 def cross_kernel(weight_ref, prior_ref, *refs):
-    kernels, outs = refs[:-WIDTHS], refs[-WIDTHS:]
+    kernels, (own_ref, up_ref, down_ref, far_up_ref, far_down_ref) = refs[:-5], refs[-5:]
     block = weight_ref.shape[0] // WIDTHS
     cands = kernels[0].shape[1]
+    half = far_up_ref.shape[1]
     for chunk, kernel_ref in enumerate(kernels):
         cols = slice(chunk * cands, (chunk + 1) * cands)
         total = prior_ref[:, cols] + jnp.dot(
             weight_ref[...], kernel_ref[...], preferred_element_type=F32
         )
-        for target, out in enumerate(outs):
-            rows = slice(target * block, (target + 1) * block)
-            out[:, cols] = total[rows].astype(out.dtype)
+        own_ref[:, cols] = total[:block]
+        up_ref[:, cols] = total[block : 2 * block]
+        down_ref[:, cols] = total[3 * block :]
+        far_ref, first = (far_up_ref, 0) if cols.start < half else (far_down_ref, half)
+        far_ref[:, cols.start - first : cols.stop - first] = total[2 * block : 3 * block].astype(BF16)
+
+
+def merge_kernel(up_ref, down_ref, far_up_ref, far_down_ref, up_out, down_out):
+    half = far_up_ref.shape[1]
+    up_out[:, :half] = (up_ref[:, :half] + far_up_ref[...].astype(F32)).astype(BF16)
+    up_out[:, half:] = up_ref[:, half:].astype(BF16)
+    down_out[:, :half] = down_ref[:, :half].astype(BF16)
+    down_out[:, half:] = (down_ref[:, half:] + far_down_ref[...].astype(F32)).astype(BF16)
+
+
+def merge(up, down, far_up, far_down):
+    return pl.pallas_call(
+        merge_kernel,
+        out_shape=(jax.ShapeDtypeStruct(up.shape, BF16),) * 2,
+        in_specs=[whole()] * 4,
+        out_specs=(whole(),) * 2,
+        compiler_params=params(),
+        cost_estimate=pl.CostEstimate(
+            flops=2 * up.size, transcendentals=0, bytes_accessed=14 * up.size
+        ),
+    )(up, down, far_up, far_down)
 
 
 def prior_product(coefs, features):
@@ -259,15 +283,15 @@
 def cross_product(weights, prior, kernels):
     rows, cands = prior.shape
     obs = weights.shape[1]
-    shape = (rows // WIDTHS, cands)
-    out_shapes = (jax.ShapeDtypeStruct(shape, F32),) + (jax.ShapeDtypeStruct(shape, BF16),) * (
-        WIDTHS - 1
-    )
+    block = rows // WIDTHS
+    out_shapes = (jax.ShapeDtypeStruct((block, cands), F32),) * 3 + (
+        jax.ShapeDtypeStruct((block, cands // 2), BF16),
+    ) * 2
     return pl.pallas_call(
         cross_kernel,
         out_shape=out_shapes,
         in_specs=[whole()] * (2 + len(kernels)),
-        out_specs=(whole(),) * WIDTHS,
+        out_specs=(whole(),) * 5,
         compiler_params=params(),
         cost_estimate=pl.CostEstimate(
             flops=2 * rows * obs * cands, transcendentals=0, bytes_accessed=8 * rows * cands
@@ -278,7 +302,7 @@
 def total_kernel(first, *refs):
     *parts, out_ref, sums, sem = refs
     total = parts[0][...]
-    for part in parts[1:WIDTHS]:
+    for part in parts[1:3]:
         total = total + part[...].astype(F32)
     sums[...] = total
     copy = pltpu.make_async_copy(sums, out_ref.at[:, first : first + total.shape[1]], sem)
@@ -335,7 +359,7 @@
     )(*pieces)
 
 
-def spread(piece, at_once):
+def spread(piece):
     def swap(held, pairs):
         return lax.ppermute(held, "cand", pairs)
 
@@ -344,12 +368,8 @@
         other = swap(held, exchange_pairs(hop * CORES))
         held = stack([held, other])
     step = DEPTHS * CORES
-    if at_once:
-        others = [swap(held, exchange_pairs(hop * step)) for hop in (1, 3, 2)]
-        near = stack([held] + others)
-    else:
-        near = stack([held, swap(held, exchange_pairs(step))])
-        near = stack([near, swap(near, exchange_pairs(3 * step))])
+    near = stack([held, swap(held, exchange_pairs(step))])
+    near = stack([near, swap(near, exchange_pairs(3 * step))])
     return near, swap(near, exchange_pairs(1))
 
 
@@ -454,22 +474,27 @@
     turns, exponent, levels, inverse, factor = prepare(
         frequencies, phases, observed, inv_length, grid_coords, diag_inv, factor_rows
     )
-    coef_near, coef_far = spread(prior_coef, False)
+    coef_near, coef_far = spread(prior_coef)
     weights = solve_chain(whitened, factor, inverse)
-    weight_near, weight_far = spread(weights, True)
+    weight_near, weight_far = spread(weights)
     made = [tiles(turns, exponent, levels, chunk) for chunk in range(CHUNKS)]
     coefs = in_order(coef_near, coef_far)
     solved = in_order(weight_near, weight_far)
     rows = lax.axis_size("rows")
+
+    def beside(block, step):
+        return lax.ppermute(block, "rows", [(i, (i + step) % rows) for i in range(rows)])
+
     result = None
     for first, last in PARTS:
         mine = made[first:last]
         prior = prior_product(coefs, [m[0] for m in mine])
-        own, *away = cross_product(solved, prior, [m[1] for m in mine])
-        arrived = []
-        for shift, block in enumerate(away, 1):
-            pairs = [(i, (i + shift) % rows) for i in range(rows)]
-            arrived.append(lax.ppermute(block, "rows", pairs))
+        kernels = [m[1] for m in mine]
+        own, up, down, far_up, far_down = cross_product(solved, prior, kernels)
+        far_up = beside(far_up, 1)
+        far_down = beside(far_down, -1)
+        up, down = merge(up, down, far_up, far_down)
+        arrived = [beside(up, 1), beside(down, -1)]
         cands = grid_coords.shape[1]
         start = first * (cands // CHUNKS)
         result = total([own] + arrived, start, cands, result)

time: 125 us -> 127 us (1.016)
  the two profiles are of different devices: /device:TPU:1 before, /device:TPU:62 now
where the time goes in v6:
time: 127 us
  waiting for transfers between devices  54.1 us (43%)
  starting transfers between devices  39.7 us (31%)
  Pallas kernels  32.2 us (25%)
    ppermute x12, waiting for transfers between devices, swap(): return lax.ppermute(held, 'cand', pairs)  36.1 us
    pallas_call x8, Pallas kernels, tiles(): pl.pallas_call(tile_kernel, out_shape=(jax.ShapeDtypeStruct((feats, cands...  19 us
    ppermute x8, starting transfers between devices, beside(): lax.ppermute(block, 'rows', [(i, (i + step) % rows) for i in range(rows)])  18.7 us
    ppermute x12, starting transfers between devices, swap(): return lax.ppermute(held, 'cand', pairs)  18.4 us
    ppermute x8, waiting for transfers between devices, beside(): lax.ppermute(block, 'rows', [(i, (i + step) % rows) for i in range(rows)])  16.4 us
    pallas_call x2, Pallas kernels, prior_product(): pl.pallas_call(prior_kernel, out_shape=jax.ShapeDtypeStruct((rows, cands)...  4.64 us
    ppermute x3, starting transfers between devices, solve_chain(): carried = lax.ppermute(carried, 'rows', [(section, section - 1)])  2.6 us
    pallas_call x1, Pallas kernels, prepare(): pl.pallas_call(prepare_kernel, out_shape=(jax.ShapeDtypeStruct((feats, LA...  2.57 us
  transfers between devices with their start and end apart: 23, of which 17 were waited for; matrix products, arithmetic and copies ran while one was open for 0% of the time, Pallas kernels for 21%

profile of v6, /device:TPU:62, one launch (start us, length us, event | category | flops | bytes accessed | tf_op | source)
XLA Modules:
  0.0 127.1 jit_solution(17658954427300693555)
XLA Ops:
  0.1 3.8 %collective-permute-done.9.refs_1_ = bf16[4,2048]{1,0:T(4,128)(2,1)S(1)} collective-permute-done((bf16[4,2048]{1,0:T(4,128)(2,1)}, bf16[4,2048]{1,0:T(4,128)(2,1)S(1)}, u32[]{:S(2)}, u32[]{:S(2)}) %collective-permute-start.9) | collective-permute-done | bytes 16416 | tf_op jit(solution)/shard_map/ppermute | solution.py:364
  4.0 0.7 copy-done.1
  4.7 3.4 %collective-permute-start.10 = (bf16[8,2048]{1,0:T(8,128)(2,1)S(1)}, bf16[8,2048]{1,0:T(8,128)(2,1)S(1)}, u32[]{:S(2)}, u32[]{:S(2)}) collective-permute-start(bf16[8,2048]{1,0:T(8,128)(2,1)S(1)} %shard_map.101.refs_0_), channel_id=1, source_target_pairs={{0,4},{1,5},{2,6},{3,7},{4,0},{5,1},{6,2},{7,3},{8,12},{9,13},{10,... | collective-permute-start | bytes 98312 | tf_op jit(solution)/shard_map/ppermute | solution.py:364
  8.0 1.9 %collective-permute-done.10.refs_1_ = bf16[8,2048]{1,0:T(8,128)(2,1)S(1)} collective-permute-done((bf16[8,2048]{1,0:T(8,128)(2,1)S(1)}, bf16[8,2048]{1,0:T(8,128)(2,1)S(1)}, u32[]{:S(2)}, u32[]{:S(2)}) %collective-permute-start.10) | collective-permute-done | bytes 32800 | tf_op jit(solution)/shard_map/ppermute | solution.py:364
  9.9 5.5 %collective-permute-start.11 = (bf16[16,2048]{1,0:T(8,128)(2,1)S(1)}, bf16[16,2048]{1,0:T(8,128)(2,1)S(1)}, u32[]{:S(2)}, u32[]{:S(2)}) collective-permute-start(bf16[16,2048]{1,0:T(8,128)(2,1)S(1)} %shard_map.102.refs_0_), channel_id=1, source_target_pairs={{0,14},{1,15},{2,12},{3,13},{4,10},{5,11},{6,8},{7,9},{8,6},{9,7},... | collective-permute-start | bytes 196616 | tf_op jit(solution)/shard_map/ppermute | solution.py:364
  15.4 2.3 %collective-permute-done.11.refs_1_ = bf16[16,2048]{1,0:T(8,128)(2,1)S(1)} collective-permute-done((bf16[16,2048]{1,0:T(8,128)(2,1)S(1)}, bf16[16,2048]{1,0:T(8,128)(2,1)S(1)}, u32[]{:S(2)}, u32[]{:S(2)}) %collective-permute-start.11) | collective-permute-done | bytes 65568 | tf_op jit(solution)/shard_map/ppermute | solution.py:364
  17.8 0.9 collective-permute-start.12
  18.7 4.1 %collective-permute-done.12.refs_1_ = bf16[32,2048]{1,0:T(8,128)(2,1)S(1)} collective-permute-done((bf16[32,2048]{1,0:T(8,128)(2,1)S(1)}, bf16[32,2048]{1,0:T(8,128)(2,1)S(1)}, u32[]{:S(2)}, u32[]{:S(2)}) %collective-permute-start.12) | collective-permute-done | bytes 131104 | tf_op jit(solution)/shard_map/ppermute | solution.py:364
  22.9 0.6 collective-permute-start.13
  23.4 7.1 %collective-permute-done.13.refs_1_ = bf16[64,2048]{1,0:T(8,128)(2,1)S(1)} collective-permute-done((bf16[64,2048]{1,0:T(8,128)(2,1)S(1)}, bf16[64,2048]{1,0:T(8,128)(2,1)S(1)}, u32[]{:S(2)}, u32[]{:S(2)}) %collective-permute-start.13) | collective-permute-done | bytes 262176 | tf_op jit(solution)/shard_map/ppermute | solution.py:364
  30.7 2.6 %prepare.1 = (bf16[2048,128]{1,0:T(8,128)(2,1)S(1)}, bf16[512,128]{1,0:T(8,128)(2,1)S(1)}, bf16[128,4096]{1,0:T(8,128)(2,1)S(1)}, f32[512,512]{1,0:T(8,128)S(1)}, f32[512,1536]{1,0:T(8,128)S(1)}) custom-call(f32[22,2048]{1,0:T(8,128)} %refs_0_.2, f32[1,2048]{1,0:T(1,128)} %bitcast.3, f32[22,512]{1,0:T(8,128)} %refs_2_.1, f32[1,22]{1,0:T(1,128)} %bitcast.4, ...), custom_call_target="tpu_custom_call" | custom-call | flops 10000000 | bytes 8388608 | tf_op jit(solution)/shard_map/prepare/pallas_call | solution.py:107
  33.3 1.8 %shard_map.91 = (f32[4,1536]{1,0:T(4,128)S(1)}, bf16[4,512]{1,0:T(4,128)(2,1)S(1)}) custom-call(f32[4,512]{1,0:T(4,128)S(1)} %copy-done, f32[512,512]{1,0:T(8,128)S(1)} %get-tuple-element.46.inverse_ref, f32[512,1536]{1,0:T(8,128)S(1)} %get-tuple-element.47.factor_ref), custom_call_target="tpu_custom_call" | custom-call | flops 75497472 | bytes 4194304 | tf_op jit(solution)/shard_map/pallas_call | solution.py:439
  35.1 1.3 %collective-permute-start = (f32[4,1536]{1,0:T(4,128)S(1)}, f32[4,1536]{1,0:T(4,128)S(1)}, u32[]{:S(2)}, u32[]{:S(2)}) collective-permute-start(f32[4,1536]{1,0:T(4,128)S(1)} %get-tuple-element.48), channel_id=1, source_target_pairs={{192,128},{193,129},{194,130},{195,131},{196,132},{197,133},{198,1... | collective-permute-start | bytes 73736 | tf_op jit(solution)/shard_map/ppermute | solution.py:459
  36.4 1.5 %collective-permute-done.refs_0_ = f32[4,1536]{1,0:T(4,128)S(1)} collective-permute-done((f32[4,1536]{1,0:T(4,128)S(1)}, f32[4,1536]{1,0:T(4,128)S(1)}, u32[]{:S(2)}, u32[]{:S(2)}) %collective-permute-start) | collective-permute-done | bytes 24608 | tf_op jit(solution)/shard_map/ppermute | solution.py:459
  37.9 0.7 collective-permute-start.1
  38.6 0.7 collective-permute-start.2
  39.3 0.9 collective-permute-start.3
  40.2 2.8 %collective-permute-done.3.refs_1_ = bf16[4,512]{1,0:T(4,128)(2,1)S(1)} collective-permute-done((bf16[4,512]{1,0:T(4,128)(2,1)S(1)}, bf16[4,512]{1,0:T(4,128)(2,1)S(1)}, u32[]{:S(2)}, u32[]{:S(2)}) %collective-permute-start.3) | collective-permute-done | bytes 4128 | tf_op jit(solution)/shard_map/ppermute | solution.py:364
  43.0 1.3 collective-permute-start.4
  44.3 3.3 %collective-permute-done.4.refs_1_ = bf16[8,512]{1,0:T(8,128)(2,1)S(1)} collective-permute-done((bf16[8,512]{1,0:T(8,128)(2,1)S(1)}, bf16[8,512]{1,0:T(8,128)(2,1)S(1)}, u32[]{:S(2)}, u32[]{:S(2)}) %collective-permute-start.4) | collective-permute-done | bytes 8224 | tf_op jit(solution)/shard_map/ppermute | solution.py:364
  47.6 4.9 %collective-permute-start.5 = (bf16[16,512]{1,0:T(8,128)(2,1)S(1)}, bf16[16,512]{1,0:T(8,128)(2,1)S(1)}, u32[]{:S(2)}, u32[]{:S(2)}) collective-permute-start(bf16[16,512]{1,0:T(8,128)(2,1)S(1)} %shard_map.96.refs_0_), channel_id=1, source_target_pairs={{0,14},{1,15},{2,12},{3,13},{4,10},{5,11},{6,8},{7,9},{8,6},{9,7},... | collective-permute-start | bytes 49160 | tf_op jit(solution)/shard_map/ppermute | solution.py:364
  52.5 1.8 %collective-permute-done.5.refs_1_ = bf16[16,512]{1,0:T(8,128)(2,1)S(1)} collective-permute-done((bf16[16,512]{1,0:T(8,128)(2,1)S(1)}, bf16[16,512]{1,0:T(8,128)(2,1)S(1)}, u32[]{:S(2)}, u32[]{:S(2)}) %collective-permute-start.5) | collective-permute-done | bytes 16416 | tf_op jit(solution)/shard_map/ppermute | solution.py:364
  54.3 3.9 %collective-permute-done.6.refs_1_ = bf16[32,512]{1,0:T(8,128)(2,1)S(1)} collective-permute-done((bf16[32,512]{1,0:T(8,128)(2,1)S(1)}, bf16[32,512]{1,0:T(8,128)(2,1)S(1)}, u32[]{:S(2)}, u32[]{:S(2)}) %collective-permute-start.6) | collective-permute-done | bytes 32800 | tf_op jit(solution)/shard_map/ppermute | solution.py:364
  58.7 5.0 %collective-permute-done.7.refs_1_ = bf16[64,512]{1,0:T(8,128)(2,1)S(1)} collective-permute-done((bf16[64,512]{1,0:T(8,128)(2,1)S(1)}, bf16[64,512]{1,0:T(8,128)(2,1)S(1)}, u32[]{:S(2)}, u32[]{:S(2)}) %collective-permute-start.7) | collective-permute-done | bytes 65568 | tf_op jit(solution)/shard_map/ppermute | solution.py:364
  64.0 2.4 %shard_map.112 = (bf16[2048,512]{1,0:T(8,128)(2,1)S(1)}, bf16[512,512]{1,0:T(8,128)(2,1)S(1)}) custom-call(bf16[2048,128]{1,0:T(8,128)(2,1)S(1)} %get-tuple-element.54.turns_ref, bf16[512,128]{1,0:T(8,128)(2,1)S(1)} %get-tuple-element.55.exponent_ref, bf16[128,4096]{1,0:T(8,128)(2,1)S(1)} %get-tuple-element.56.levels_ref), custom_call_target="tpu_custom_call" | custom-call | flops 31457280 | bytes 2621440 | tf_op jit(solution)/shard_map/pallas_call | solution.py:160
  66.4 2.4 %shard_map.113 = (bf16[2048,512]{1,0:T(8,128)(2,1)S(1)}, bf16[512,512]{1,0:T(8,128)(2,1)S(1)}) custom-call(bf16[2048,128]{1,0:T(8,128)(2,1)S(1)} %get-tuple-element.54.turns_ref, bf16[512,128]{1,0:T(8,128)(2,1)S(1)} %get-tuple-element.55.exponent_ref, bf16[128,4096]{1,0:T(8,128)(2,1)S(1)} %get-tuple-element.56.levels_ref), custom_call_target="tpu_custom_call" | custom-call | flops 31457280 | bytes 2621440 | tf_op jit(solution)/shard_map/pallas_call | solution.py:160
  68.8 2.4 %shard_map.114 = (bf16[2048,512]{1,0:T(8,128)(2,1)S(1)}, bf16[512,512]{1,0:T(8,128)(2,1)S(1)}) custom-call(bf16[2048,128]{1,0:T(8,128)(2,1)S(1)} %get-tuple-element.54.turns_ref, bf16[512,128]{1,0:T(8,128)(2,1)S(1)} %get-tuple-element.55.exponent_ref, bf16[128,4096]{1,0:T(8,128)(2,1)S(1)} %get-tuple-element.56.levels_ref), custom_call_target="tpu_custom_call" | custom-call | flops 31457280 | bytes 2621440 | tf_op jit(solution)/shard_map/pallas_call | solution.py:160
  71.2 2.4 %shard_map.115 = (bf16[2048,512]{1,0:T(8,128)(2,1)S(1)}, bf16[512,512]{1,0:T(8,128)(2,1)S(1)}) custom-call(bf16[2048,128]{1,0:T(8,128)(2,1)S(1)} %get-tuple-element.54.turns_ref, bf16[512,128]{1,0:T(8,128)(2,1)S(1)} %get-tuple-element.55.exponent_ref, bf16[128,4096]{1,0:T(8,128)(2,1)S(1)} %get-tuple-element.56.levels_ref), custom_call_target="tpu_custom_call" | custom-call | flops 31457280 | bytes 2621440 | tf_op jit(solution)/shard_map/pallas_call | solution.py:160
  73.6 2.4 %shard_map.116 = (bf16[2048,512]{1,0:T(8,128)(2,1)S(1)}, bf16[512,512]{1,0:T(8,128)(2,1)S(1)}) custom-call(bf16[2048,128]{1,0:T(8,128)(2,1)S(1)} %get-tuple-element.54.turns_ref, bf16[512,128]{1,0:T(8,128)(2,1)S(1)} %get-tuple-element.55.exponent_ref, bf16[128,4096]{1,0:T(8,128)(2,1)S(1)} %get-tuple-element.56.levels_ref), custom_call_target="tpu_custom_call" | custom-call | flops 31457280 | bytes 2621440 | tf_op jit(solution)/shard_map/pallas_call | solution.py:160
  76.0 2.4 %shard_map.117 = (bf16[2048,512]{1,0:T(8,128)(2,1)S(1)}, bf16[512,512]{1,0:T(8,128)(2,1)S(1)}) custom-call(bf16[2048,128]{1,0:T(8,128)(2,1)S(1)} %get-tuple-element.54.turns_ref, bf16[512,128]{1,0:T(8,128)(2,1)S(1)} %get-tuple-element.55.exponent_ref, bf16[128,4096]{1,0:T(8,128)(2,1)S(1)} %get-tuple-element.56.levels_ref), custom_call_target="tpu_custom_call" | custom-call | flops 31457280 | bytes 2621440 | tf_op jit(solution)/shard_map/pallas_call | solution.py:160
  79.1 3.4 %shard_map.118.prior_ref = f32[256,3072]{1,0:T(8,128)S(1)} custom-call(bf16[256,2048]{1,0:T(8,128)(2,1)S(1)} %shard_map.106.coef_ref, bf16[2048,512]{1,0:T(8,128)(2,1)S(1)} %get-tuple-element.68.refs_0_, bf16[2048,512]{1,0:T(8,128)(2,1)S(1)} %get-tuple-element.69.refs_1_, bf16[2048,512]{1,0:T(8,128)(2,1)S(1)} %get-tuple-element.70.refs_2_, ...), custom_call_target="tpu_custom_call" | custom-call | flops 3221225472 | bytes 12582912 | tf_op jit(solution)/shard_map/pallas_call | solution.py:271
  82.5 1.0 shard_map.119
  83.5 12.2 %collective-permute-start.19 = (bf16[64,1536]{1,0:T(8,128)(2,1)S(1)}, bf16[64,1536]{1,0:T(8,128)(2,1)S(1)}, u32[]{:S(2)}, u32[]{:S(2)}) collective-permute-start(bf16[64,1536]{1,0:T(8,128)(2,1)S(1)} %get-tuple-element.83), channel_id=1, source_target_pairs={{0,64},{64,128},{128,192},{192,0},{1,65},{65,129},{129,193},{193,1... | collective-permute-start | bytes 589832 | tf_op jit(solution)/shard_map/ppermute | solution.py:486
  95.7 4.8 %collective-permute-done.19.far_up_ref = bf16[64,1536]{1,0:T(8,128)(2,1)S(1)} collective-permute-done((bf16[64,1536]{1,0:T(8,128)(2,1)S(1)}, bf16[64,1536]{1,0:T(8,128)(2,1)S(1)}, u32[]{:S(2)}, u32[]{:S(2)}) %collective-permute-start.19) | collective-permute-done | bytes 196640 | tf_op jit(solution)/shard_map/ppermute | solution.py:486
  100.5 3.4 %collective-permute-done.20.far_down_ref = bf16[64,1536]{1,0:T(8,128)(2,1)S(1)} collective-permute-done((bf16[64,1536]{1,0:T(8,128)(2,1)S(1)}, bf16[64,1536]{1,0:T(8,128)(2,1)S(1)}, u32[]{:S(2)}, u32[]{:S(2)}) %collective-permute-start.20) | collective-permute-done | bytes 196640 | tf_op jit(solution)/shard_map/ppermute | solution.py:486
  104.0 0.6 collective-permute-start.21
  104.6 1.7 %collective-permute-start.22 = (bf16[64,3072]{1,0:T(8,128)(2,1)S(1)}, bf16[64,3072]{1,0:T(8,128)(2,1)S(1)}, u32[]{:S(2)}, u32[]{:S(2)}) collective-permute-start(bf16[64,3072]{1,0:T(8,128)(2,1)S(1)} %get-tuple-element.86), channel_id=1, source_target_pairs={{0,192},{64,0},{128,64},{192,128},{1,193},{65,1},{129,65},{193,129... | collective-permute-start | bytes 1179656 | tf_op jit(solution)/shard_map/ppermute | solution.py:486
  106.3 2.4 %shard_map.107 = (bf16[2048,512]{1,0:T(8,128)(2,1)S(1)}, bf16[512,512]{1,0:T(8,128)(2,1)S(1)}) custom-call(bf16[2048,128]{1,0:T(8,128)(2,1)S(1)} %get-tuple-element.54.turns_ref, bf16[512,128]{1,0:T(8,128)(2,1)S(1)} %get-tuple-element.55.exponent_ref, bf16[128,4096]{1,0:T(8,128)(2,1)S(1)} %get-tuple-element.56.levels_ref), custom_call_target="tpu_custom_call" | custom-call | flops 31457280 | bytes 2621440 | tf_op jit(solution)/shard_map/pallas_call | solution.py:160
  108.7 2.4 %shard_map.108 = (bf16[2048,512]{1,0:T(8,128)(2,1)S(1)}, bf16[512,512]{1,0:T(8,128)(2,1)S(1)}) custom-call(bf16[2048,128]{1,0:T(8,128)(2,1)S(1)} %get-tuple-element.54.turns_ref, bf16[512,128]{1,0:T(8,128)(2,1)S(1)} %get-tuple-element.55.exponent_ref, bf16[128,4096]{1,0:T(8,128)(2,1)S(1)} %get-tuple-element.56.levels_ref), custom_call_target="tpu_custom_call" | custom-call | flops 31457280 | bytes 2621440 | tf_op jit(solution)/shard_map/pallas_call | solution.py:160
  111.1 1.2 shard_map.109.prior_ref
  112.8 1.6 %collective-permute-start.15 = (bf16[64,512]{1,0:T(8,128)(2,1)S(1)}, bf16[64,512]{1,0:T(8,128)(2,1)S(1)}, u32[]{:S(2)}, u32[]{:S(2)}) collective-permute-start(bf16[64,512]{1,0:T(8,128)(2,1)S(1)} %get-tuple-element.64), channel_id=1, source_target_pairs={{0,64},{64,128},{128,192},{192,0},{1,65},{65,129},{129,193},{193,1... | collective-permute-start | bytes 196616 | tf_op jit(solution)/shard_map/ppermute | solution.py:486
  114.9 2.2 %collective-permute-done.15.far_up_ref = bf16[64,512]{1,0:T(8,128)(2,1)S(1)} collective-permute-done((bf16[64,512]{1,0:T(8,128)(2,1)S(1)}, bf16[64,512]{1,0:T(8,128)(2,1)S(1)}, u32[]{:S(2)}, u32[]{:S(2)}) %collective-permute-start.15) | collective-permute-done | bytes 65568 | tf_op jit(solution)/shard_map/ppermute | solution.py:486
  117.1 2.7 %collective-permute-done.16.far_down_ref = bf16[64,512]{1,0:T(8,128)(2,1)S(1)} collective-permute-done((bf16[64,512]{1,0:T(8,128)(2,1)S(1)}, bf16[64,512]{1,0:T(8,128)(2,1)S(1)}, u32[]{:S(2)}, u32[]{:S(2)}) %collective-permute-start.16) | collective-permute-done | bytes 65568 | tf_op jit(solution)/shard_map/ppermute | solution.py:486
  120.0 2.0 %collective-permute-start.18 = (bf16[64,1024]{1,0:T(8,128)(2,1)S(1)}, bf16[64,1024]{1,0:T(8,128)(2,1)S(1)}, u32[]{:S(2)}, u32[]{:S(2)}) collective-permute-start(bf16[64,1024]{1,0:T(8,128)(2,1)S(1)} %get-tuple-element.67), channel_id=1, source_target_pairs={{0,192},{64,0},{128,64},{192,128},{1,193},{65,1},{129,65},{193,129... | collective-permute-start | bytes 393224 | tf_op jit(solution)/shard_map/ppermute | solution.py:486
  122.0 1.0 shard_map.121.refs_3_
  123.0 1.9 %collective-permute-done.17.refs_1_ = bf16[64,1024]{1,0:T(8,128)(2,1)S(1)} collective-permute-done((bf16[64,1024]{1,0:T(8,128)(2,1)S(1)}, bf16[64,1024]{1,0:T(8,128)(2,1)S(1)}, u32[]{:S(2)}, u32[]{:S(2)}) %collective-permute-start.17) | collective-permute-done | bytes 131104 | tf_op jit(solution)/shard_map/ppermute | solution.py:486
  124.9 1.3 %collective-permute-done.18.refs_2_ = bf16[64,1024]{1,0:T(8,128)(2,1)S(1)} collective-permute-done((bf16[64,1024]{1,0:T(8,128)(2,1)S(1)}, bf16[64,1024]{1,0:T(8,128)(2,1)S(1)}, u32[]{:S(2)}, u32[]{:S(2)}) %collective-permute-start.18) | collective-permute-done | bytes 131104 | tf_op jit(solution)/shard_map/ppermute | solution.py:486
  126.2 0.7 shard_map.122
  (35 shorter events, 3.0 us)
Async XLA Ops:
  0.0 3.9 %collective-permute-start.9 = (bf16[4,2048]{1,0:T(4,128)(2,1)}, bf16[4,2048]{1,0:T(4,128)(2,1)S(1)}, u32[]{:S(2)}, u32[]{:S(2)}) collective-permute-start(bf16[4,2048]{1,0:T(4,128)(2,1)} %refs_0_.3), channel_id=1, source_target_pairs={{0,2},{1,3},{2,0},{3,1},{4,6},{5,7},{6,4},{7,5},{8,10},{9,11},{10,... | collective-permute-start | bytes 49160 | tf_op jit(solution)/shard_map/ppermute | solution.py:364
  4.0 0.7 copy-start.1
  4.7 5.3 %collective-permute-start.10 = (bf16[8,2048]{1,0:T(8,128)(2,1)S(1)}, bf16[8,2048]{1,0:T(8,128)(2,1)S(1)}, u32[]{:S(2)}, u32[]{:S(2)}) collective-permute-start(bf16[8,2048]{1,0:T(8,128)(2,1)S(1)} %shard_map.101.refs_0_), channel_id=1, source_target_pairs={{0,4},{1,5},{2,6},{3,7},{4,0},{5,1},{6,2},{7,3},{8,12},{9,13},{10,... | collective-permute-start | bytes 98312 | tf_op jit(solution)/shard_map/ppermute | solution.py:364
  9.9 7.8 %collective-permute-start.11 = (bf16[16,2048]{1,0:T(8,128)(2,1)S(1)}, bf16[16,2048]{1,0:T(8,128)(2,1)S(1)}, u32[]{:S(2)}, u32[]{:S(2)}) collective-permute-start(bf16[16,2048]{1,0:T(8,128)(2,1)S(1)} %shard_map.102.refs_0_), channel_id=1, source_target_pairs={{0,14},{1,15},{2,12},{3,13},{4,10},{5,11},{6,8},{7,9},{8,6},{9,7},... | collective-permute-start | bytes 196616 | tf_op jit(solution)/shard_map/ppermute | solution.py:364
  17.8 5.1 %collective-permute-start.12 = (bf16[32,2048]{1,0:T(8,128)(2,1)S(1)}, bf16[32,2048]{1,0:T(8,128)(2,1)S(1)}, u32[]{:S(2)}, u32[]{:S(2)}) collective-permute-start(bf16[32,2048]{1,0:T(8,128)(2,1)S(1)} %shard_map.103.refs_0_), channel_id=1, source_target_pairs={{0,16},{1,17},{2,18},{3,19},{4,20},{5,21},{6,22},{7,23},{8,24},{9,... | collective-permute-start | bytes 393224 | tf_op jit(solution)/shard_map/ppermute | solution.py:364
  22.9 7.7 %collective-permute-start.13 = (bf16[64,2048]{1,0:T(8,128)(2,1)S(1)}, bf16[64,2048]{1,0:T(8,128)(2,1)S(1)}, u32[]{:S(2)}, u32[]{:S(2)}) collective-permute-start(bf16[64,2048]{1,0:T(8,128)(2,1)S(1)} %shard_map.104.refs_0_), channel_id=1, source_target_pairs={{0,48},{1,49},{2,50},{3,51},{4,52},{5,53},{6,54},{7,55},{8,56},{9,... | collective-permute-start | bytes 786440 | tf_op jit(solution)/shard_map/ppermute | solution.py:364
  30.6 48.0 %collective-permute-start.14 = (bf16[128,2048]{1,0:T(8,128)(2,1)S(1)}, bf16[128,2048]{1,0:T(8,128)(2,1)S(1)}, u32[]{:S(2)}, u32[]{:S(2)}) collective-permute-start(bf16[128,2048]{1,0:T(8,128)(2,1)S(1)} %shard_map.105.near_ref), channel_id=1, source_target_pairs={{0,1},{1,0},{2,3},{3,2},{4,5},{5,4},{6,7},{7,6},{8,9},{9,8},{10,11... | collective-permute-start | bytes 1572872 | tf_op jit(solution)/shard_map/ppermute | solution.py:364
  30.7 2.6 %copy-start = (f32[4,512]{1,0:T(4,128)S(1)}, f32[4,512]{1,0:T(4,128)}, u32[]{:S(2)}) copy-start(f32[4,512]{1,0:T(4,128)} %whitened_ref.7) | copy-start | bytes 24580
  35.1 2.8 %collective-permute-start = (f32[4,1536]{1,0:T(4,128)S(1)}, f32[4,1536]{1,0:T(4,128)S(1)}, u32[]{:S(2)}, u32[]{:S(2)}) collective-permute-start(f32[4,1536]{1,0:T(4,128)S(1)} %get-tuple-element.48), channel_id=1, source_target_pairs={{192,128},{193,129},{194,130},{195,131},{196,132},{197,133},{198,1... | collective-permute-start | bytes 73736 | tf_op jit(solution)/shard_map/ppermute | solution.py:459
  37.9 0.7 collective-permute-start.1
  38.6 0.7 collective-permute-start.2
  39.3 3.7 %collective-permute-start.3 = (bf16[4,512]{1,0:T(4,128)(2,1)S(1)}, bf16[4,512]{1,0:T(4,128)(2,1)S(1)}, u32[]{:S(2)}, u32[]{:S(2)}) collective-permute-start(bf16[4,512]{1,0:T(4,128)(2,1)S(1)} %shard_map.94.refs_0_), channel_id=1, source_target_pairs={{0,2},{1,3},{2,0},{3,1},{4,6},{5,7},{6,4},{7,5},{8,10},{9,11},{10,... | collective-permute-start | bytes 12296 | tf_op jit(solution)/shard_map/ppermute | solution.py:364
  43.0 4.5 %collective-permute-start.4 = (bf16[8,512]{1,0:T(8,128)(2,1)S(1)}, bf16[8,512]{1,0:T(8,128)(2,1)S(1)}, u32[]{:S(2)}, u32[]{:S(2)}) collective-permute-start(bf16[8,512]{1,0:T(8,128)(2,1)S(1)} %shard_map.95.refs_0_), channel_id=1, source_target_pairs={{0,4},{1,5},{2,6},{3,7},{4,0},{5,1},{6,2},{7,3},{8,12},{9,13},{10,... | collective-permute-start | bytes 24584 | tf_op jit(solution)/shard_map/ppermute | solution.py:364
  47.6 6.7 %collective-permute-start.5 = (bf16[16,512]{1,0:T(8,128)(2,1)S(1)}, bf16[16,512]{1,0:T(8,128)(2,1)S(1)}, u32[]{:S(2)}, u32[]{:S(2)}) collective-permute-start(bf16[16,512]{1,0:T(8,128)(2,1)S(1)} %shard_map.96.refs_0_), channel_id=1, source_target_pairs={{0,14},{1,15},{2,12},{3,13},{4,10},{5,11},{6,8},{7,9},{8,6},{9,7},... | collective-permute-start | bytes 49160 | tf_op jit(solution)/shard_map/ppermute | solution.py:364
  54.3 3.9 %collective-permute-start.6 = (bf16[32,512]{1,0:T(8,128)(2,1)S(1)}, bf16[32,512]{1,0:T(8,128)(2,1)S(1)}, u32[]{:S(2)}, u32[]{:S(2)}) collective-permute-start(bf16[32,512]{1,0:T(8,128)(2,1)S(1)} %shard_map.97.refs_0_), channel_id=1, source_target_pairs={{0,16},{1,17},{2,18},{3,19},{4,20},{5,21},{6,22},{7,23},{8,24},{9,... | collective-permute-start | bytes 98312 | tf_op jit(solution)/shard_map/ppermute | solution.py:364
  58.3 5.5 %collective-permute-start.7 = (bf16[64,512]{1,0:T(8,128)(2,1)S(1)}, bf16[64,512]{1,0:T(8,128)(2,1)S(1)}, u32[]{:S(2)}, u32[]{:S(2)}) collective-permute-start(bf16[64,512]{1,0:T(8,128)(2,1)S(1)} %shard_map.98.refs_0_), channel_id=1, source_target_pairs={{0,48},{1,49},{2,50},{3,51},{4,52},{5,53},{6,54},{7,55},{8,56},{9,... | collective-permute-start | bytes 196616 | tf_op jit(solution)/shard_map/ppermute | solution.py:364
  63.7 14.6 %collective-permute-start.8 = (bf16[128,512]{1,0:T(8,128)(2,1)S(1)}, bf16[128,512]{1,0:T(8,128)(2,1)S(1)}, u32[]{:S(2)}, u32[]{:S(2)}) collective-permute-start(bf16[128,512]{1,0:T(8,128)(2,1)S(1)} %shard_map.99.near_ref), channel_id=1, source_target_pairs={{0,1},{1,0},{2,3},{3,2},{4,5},{5,4},{6,7},{7,6},{8,9},{9,8},{10,11... | collective-permute-start | bytes 393224 | tf_op jit(solution)/shard_map/ppermute | solution.py:364
  83.5 17.0 %collective-permute-start.19 = (bf16[64,1536]{1,0:T(8,128)(2,1)S(1)}, bf16[64,1536]{1,0:T(8,128)(2,1)S(1)}, u32[]{:S(2)}, u32[]{:S(2)}) collective-permute-start(bf16[64,1536]{1,0:T(8,128)(2,1)S(1)} %get-tuple-element.83), channel_id=1, source_target_pairs={{0,64},{64,128},{128,192},{192,0},{1,65},{65,129},{129,193},{193,1... | collective-permute-start | bytes 589832 | tf_op jit(solution)/shard_map/ppermute | solution.py:486
  95.7 8.2 %collective-permute-start.20 = (bf16[64,1536]{1,0:T(8,128)(2,1)S(1)}, bf16[64,1536]{1,0:T(8,128)(2,1)S(1)}, u32[]{:S(2)}, u32[]{:S(2)}) collective-permute-start(bf16[64,1536]{1,0:T(8,128)(2,1)S(1)} %get-tuple-element.84), channel_id=1, source_target_pairs={{0,192},{64,0},{128,64},{192,128},{1,193},{65,1},{129,65},{193,129... | collective-permute-start | bytes 589832 | tf_op jit(solution)/shard_map/ppermute | solution.py:486
  104.0 18.0 %collective-permute-start.21 = (bf16[64,3072]{1,0:T(8,128)(2,1)S(1)}, bf16[64,3072]{1,0:T(8,128)(2,1)S(1)}, u32[]{:S(2)}, u32[]{:S(2)}) collective-permute-start(bf16[64,3072]{1,0:T(8,128)(2,1)S(1)} %get-tuple-element.85), channel_id=1, source_target_pairs={{0,64},{64,128},{128,192},{192,0},{1,65},{65,129},{129,193},{193,1... | collective-permute-start | bytes 1179656 | tf_op jit(solution)/shard_map/ppermute | solution.py:486
  104.6 17.4 %collective-permute-start.22 = (bf16[64,3072]{1,0:T(8,128)(2,1)S(1)}, bf16[64,3072]{1,0:T(8,128)(2,1)S(1)}, u32[]{:S(2)}, u32[]{:S(2)}) collective-permute-start(bf16[64,3072]{1,0:T(8,128)(2,1)S(1)} %get-tuple-element.86), channel_id=1, source_target_pairs={{0,192},{64,0},{128,64},{192,128},{1,193},{65,1},{129,65},{193,129... | collective-permute-start | bytes 1179656 | tf_op jit(solution)/shard_map/ppermute | solution.py:486
  112.8 4.3 %collective-permute-start.15 = (bf16[64,512]{1,0:T(8,128)(2,1)S(1)}, bf16[64,512]{1,0:T(8,128)(2,1)S(1)}, u32[]{:S(2)}, u32[]{:S(2)}) collective-permute-start(bf16[64,512]{1,0:T(8,128)(2,1)S(1)} %get-tuple-element.64), channel_id=1, source_target_pairs={{0,64},{64,128},{128,192},{192,0},{1,65},{65,129},{129,193},{193,1... | collective-permute-start | bytes 196616 | tf_op jit(solution)/shard_map/ppermute | solution.py:486
  114.3 5.5 %collective-permute-start.16 = (bf16[64,512]{1,0:T(8,128)(2,1)S(1)}, bf16[64,512]{1,0:T(8,128)(2,1)S(1)}, u32[]{:S(2)}, u32[]{:S(2)}) collective-permute-start(bf16[64,512]{1,0:T(8,128)(2,1)S(1)} %get-tuple-element.65), channel_id=1, source_target_pairs={{0,192},{64,0},{128,64},{192,128},{1,193},{65,1},{129,65},{193,129... | collective-permute-start | bytes 196616 | tf_op jit(solution)/shard_map/ppermute | solution.py:486
  119.9 5.0 %collective-permute-start.17 = (bf16[64,1024]{1,0:T(8,128)(2,1)S(1)}, bf16[64,1024]{1,0:T(8,128)(2,1)S(1)}, u32[]{:S(2)}, u32[]{:S(2)}) collective-permute-start(bf16[64,1024]{1,0:T(8,128)(2,1)S(1)} %get-tuple-element.66), channel_id=1, source_target_pairs={{0,64},{64,128},{128,192},{192,0},{1,65},{65,129},{129,193},{193,1... | collective-permute-start | bytes 393224 | tf_op jit(solution)/shard_map/ppermute | solution.py:486
  120.0 6.3 %collective-permute-start.18 = (bf16[64,1024]{1,0:T(8,128)(2,1)S(1)}, bf16[64,1024]{1,0:T(8,128)(2,1)S(1)}, u32[]{:S(2)}, u32[]{:S(2)}) collective-permute-start(bf16[64,1024]{1,0:T(8,128)(2,1)S(1)} %get-tuple-element.67), channel_id=1, source_target_pairs={{0,192},{64,0},{128,64},{192,128},{1,193},{65,1},{129,65},{193,129... | collective-permute-start | bytes 393224 | tf_op jit(solution)/shard_map/ppermute | solution.py:486

commit v7 on v5

--- a/solution.py
+++ b/solution.py
@@ -19,7 +19,7 @@
 ROW_CHUNK = 256
 CAND_TILE = 256
 CHUNKS = 8
-PARTS = ((0, 6), (6, 8))
+PARTS = ((0, 5), (5, 8))
 VMEM_BYTES = 16 * 2**20
 LOG2E = 1.4426950408889634
 INV_TURN = 0.15915494309189535
@@ -356,19 +356,17 @@
 def exact_lines(left, lines):
     rows = left.shape[0]
     lines[...] = jnp.zeros_like(lines)
-    for index, piece in enumerate(three_pieces(left)):
+    for index, piece in enumerate(three_pieces(left)[:2]):
         lines[index * rows : (index + 1) * rows, :] = piece
     return lines[...].astype(BF16)
 
 
 def exact_dot(lines, rows, right):
-    total = None
-    for piece, count in zip(three_pieces(right)[::-1], (1, 2, 3)):
-        product = jnp.dot(lines, piece.astype(BF16), preferred_element_type=F32)
-        for index in reversed(range(count)):
-            term = product[index * rows : (index + 1) * rows]
-            total = term if total is None else total + term
-    return total
+    high = right.astype(BF16)
+    middle = (right - high.astype(F32)).astype(BF16)
+    first = jnp.dot(lines, high, preferred_element_type=F32)
+    second = jnp.dot(lines, middle, preferred_element_type=F32)
+    return second[:rows] + first[rows : 2 * rows] + first[:rows]
 
 
 def solve_kernel(
@@ -424,7 +422,7 @@
         scratch_shapes=[pltpu.VMEM((16, width), F32)],
         compiler_params=params(),
         cost_estimate=pl.CostEstimate(
-            flops=2 * 36 * width * columns, transcendentals=0, bytes_accessed=4 * width * columns
+            flops=2 * 32 * width * columns, transcendentals=0, bytes_accessed=4 * width * columns
         ),
     )(whitened, diag_inv, factor_rows, *held)
     return results if section > 0 else (None, results[0])

time: 125 us -> 126 us (level); the launches traced: 122 us -> 125 us
  starting transfers between devices: 45 us -> 47.8 us
    ppermute x6, starting transfers between devices: 5.28 us -> 7.54 us  [body(): arrived.append(lax.ppermute(block, 'rows', pairs))]
    ppermute x3, waiting for transfers between devices: 12.4 us -> 10.5 us  [solve_chain(): carried = lax.ppermute(carried, 'rows', [(section, section - 1)])]
    ppermute x6, waiting for transfers between devices: 14.2 us -> 15.7 us  [body(): arrived.append(lax.ppermute(block, 'rows', pairs))]
  transfers between devices with their start and end apart: 22 -> 22, of which waited for: 14 -> 15; matrix products, arithmetic and copies ran while one was open for 0% -> 0% of each run, Pallas kernels for 20% -> 20%
where the time goes in v7:
time: 126 us; the launch traced here: 125 us
  starting transfers between devices  47.8 us (38%)
  waiting for transfers between devices  45.2 us (36%)
  Pallas kernels  30.6 us (24%)
    ppermute x13, starting transfers between devices, swap(): return lax.ppermute(held, 'cand', pairs)  37.7 us
    pallas_call x8, Pallas kernels, tiles(): pl.pallas_call(tile_kernel, out_shape=(jax.ShapeDtypeStruct((feats, cands...  19 us
    ppermute x13, waiting for transfers between devices, swap(): return lax.ppermute(held, 'cand', pairs)  18.9 us
    ppermute x6, waiting for transfers between devices, body(): arrived.append(lax.ppermute(block, 'rows', pairs))  15.7 us
    ppermute x3, waiting for transfers between devices, solve_chain(): carried = lax.ppermute(carried, 'rows', [(section, section - 1)])  10.5 us
    ppermute x6, starting transfers between devices, body(): arrived.append(lax.ppermute(block, 'rows', pairs))  7.54 us
    pallas_call x2, Pallas kernels, prior_product(): pl.pallas_call(prior_kernel, out_shape=jax.ShapeDtypeStruct((rows, cands)...  4.64 us
    ppermute x3, starting transfers between devices, solve_chain(): carried = lax.ppermute(carried, 'rows', [(section, section - 1)])  2.62 us
  transfers between devices with their start and end apart: 22, of which 15 were waited for; matrix products, arithmetic and copies ran while one was open for 0% of the time, Pallas kernels for 20%

profile of v7, /device:TPU:1, one launch (start us, length us, event | category | flops | bytes accessed | tf_op | source)
XLA Modules:
  0.0 124.8 jit_solution(10218525993206110337)
XLA Ops:
  0.0 2.5 %collective-permute-start.10 = (bf16[4,2048]{1,0:T(4,128)(2,1)}, bf16[4,2048]{1,0:T(4,128)(2,1)S(1)}, u32[]{:S(2)}, u32[]{:S(2)}) collective-permute-start(bf16[4,2048]{1,0:T(4,128)(2,1)} %refs_0_.3), channel_id=1, source_target_pairs={{0,2},{1,3},{2,0},{3,1},{4,6},{5,7},{6,4},{7,5},{8,10},{9,11},{10,... | collective-permute-start | bytes 49160 | tf_op jit(solution)/shard_map/ppermute | solution.py:340
  2.5 1.3 %collective-permute-done.10.refs_1_ = bf16[4,2048]{1,0:T(4,128)(2,1)S(1)} collective-permute-done((bf16[4,2048]{1,0:T(4,128)(2,1)}, bf16[4,2048]{1,0:T(4,128)(2,1)S(1)}, u32[]{:S(2)}, u32[]{:S(2)}) %collective-permute-start.10) | collective-permute-done | bytes 16416 | tf_op jit(solution)/shard_map/ppermute | solution.py:340
  3.8 0.7 copy-done.1
  4.5 3.1 %collective-permute-start.11 = (bf16[8,2048]{1,0:T(8,128)(2,1)S(1)}, bf16[8,2048]{1,0:T(8,128)(2,1)S(1)}, u32[]{:S(2)}, u32[]{:S(2)}) collective-permute-start(bf16[8,2048]{1,0:T(8,128)(2,1)S(1)} %shard_map.100.refs_0_), channel_id=1, source_target_pairs={{0,4},{1,5},{2,6},{3,7},{4,0},{5,1},{6,2},{7,3},{8,12},{9,13},{10,... | collective-permute-start | bytes 98312 | tf_op jit(solution)/shard_map/ppermute | solution.py:340
  7.6 1.3 %collective-permute-done.11.refs_1_ = bf16[8,2048]{1,0:T(8,128)(2,1)S(1)} collective-permute-done((bf16[8,2048]{1,0:T(8,128)(2,1)S(1)}, bf16[8,2048]{1,0:T(8,128)(2,1)S(1)}, u32[]{:S(2)}, u32[]{:S(2)}) %collective-permute-start.11) | collective-permute-done | bytes 32800 | tf_op jit(solution)/shard_map/ppermute | solution.py:340
  8.9 4.8 %collective-permute-start.12 = (bf16[16,2048]{1,0:T(8,128)(2,1)S(1)}, bf16[16,2048]{1,0:T(8,128)(2,1)S(1)}, u32[]{:S(2)}, u32[]{:S(2)}) collective-permute-start(bf16[16,2048]{1,0:T(8,128)(2,1)S(1)} %shard_map.101.refs_0_), channel_id=1, source_target_pairs={{0,14},{1,15},{2,12},{3,13},{4,10},{5,11},{6,8},{7,9},{8,6},{9,7},... | collective-permute-start | bytes 196616 | tf_op jit(solution)/shard_map/ppermute | solution.py:340
  13.7 2.0 %collective-permute-done.12.refs_1_ = bf16[16,2048]{1,0:T(8,128)(2,1)S(1)} collective-permute-done((bf16[16,2048]{1,0:T(8,128)(2,1)S(1)}, bf16[16,2048]{1,0:T(8,128)(2,1)S(1)}, u32[]{:S(2)}, u32[]{:S(2)}) %collective-permute-start.12) | collective-permute-done | bytes 65568 | tf_op jit(solution)/shard_map/ppermute | solution.py:340
  15.7 1.3 %collective-permute-start.13 = (bf16[32,2048]{1,0:T(8,128)(2,1)S(1)}, bf16[32,2048]{1,0:T(8,128)(2,1)S(1)}, u32[]{:S(2)}, u32[]{:S(2)}) collective-permute-start(bf16[32,2048]{1,0:T(8,128)(2,1)S(1)} %shard_map.102.refs_0_), channel_id=1, source_target_pairs={{0,16},{1,17},{2,18},{3,19},{4,20},{5,21},{6,22},{7,23},{8,24},{9,... | collective-permute-start | bytes 393224 | tf_op jit(solution)/shard_map/ppermute | solution.py:340
  17.0 2.6 %collective-permute-done.13.refs_1_ = bf16[32,2048]{1,0:T(8,128)(2,1)S(1)} collective-permute-done((bf16[32,2048]{1,0:T(8,128)(2,1)S(1)}, bf16[32,2048]{1,0:T(8,128)(2,1)S(1)}, u32[]{:S(2)}, u32[]{:S(2)}) %collective-permute-start.13) | collective-permute-done | bytes 131104 | tf_op jit(solution)/shard_map/ppermute | solution.py:340
  19.6 2.6 %collective-permute-start.14 = (bf16[64,2048]{1,0:T(8,128)(2,1)S(1)}, bf16[64,2048]{1,0:T(8,128)(2,1)S(1)}, u32[]{:S(2)}, u32[]{:S(2)}) collective-permute-start(bf16[64,2048]{1,0:T(8,128)(2,1)S(1)} %shard_map.103.refs_0_), channel_id=1, source_target_pairs={{0,48},{1,49},{2,50},{3,51},{4,52},{5,53},{6,54},{7,55},{8,56},{9,... | collective-permute-start | bytes 786440 | tf_op jit(solution)/shard_map/ppermute | solution.py:340
  22.2 4.0 %collective-permute-done.14.refs_1_ = bf16[64,2048]{1,0:T(8,128)(2,1)S(1)} collective-permute-done((bf16[64,2048]{1,0:T(8,128)(2,1)S(1)}, bf16[64,2048]{1,0:T(8,128)(2,1)S(1)}, u32[]{:S(2)}, u32[]{:S(2)}) %collective-permute-start.14) | collective-permute-done | bytes 262176 | tf_op jit(solution)/shard_map/ppermute | solution.py:340
  26.2 6.7 %collective-permute-start.15 = (bf16[128,2048]{1,0:T(8,128)(2,1)S(1)}, bf16[128,2048]{1,0:T(8,128)(2,1)S(1)}, u32[]{:S(2)}, u32[]{:S(2)}) collective-permute-start(bf16[128,2048]{1,0:T(8,128)(2,1)S(1)} %shard_map.104.near_ref), channel_id=1, source_target_pairs={{0,1},{1,0},{2,3},{3,2},{4,5},{5,4},{6,7},{7,6},{8,9},{9,8},{10,11... | collective-permute-start | bytes 1572872 | tf_op jit(solution)/shard_map/ppermute | solution.py:340
  32.9 2.6 %prepare.1 = (bf16[2048,128]{1,0:T(8,128)(2,1)S(1)}, bf16[512,128]{1,0:T(8,128)(2,1)S(1)}, bf16[128,4096]{1,0:T(8,128)(2,1)S(1)}, f32[512,512]{1,0:T(8,128)S(1)}, f32[512,1536]{1,0:T(8,128)S(1)}) custom-call(f32[22,2048]{1,0:T(8,128)} %refs_0_.2, f32[1,2048]{1,0:T(1,128)} %bitcast.3, f32[22,512]{1,0:T(8,128)} %refs_2_.1, f32[1,22]{1,0:T(1,128)} %bitcast.4, ...), custom_call_target="tpu_custom_call" | custom-call | flops 10000000 | bytes 8388608 | tf_op jit(solution)/shard_map/prepare/pallas_call | solution.py:107
  35.5 0.7 collective-permute-start
  36.2 0.7 collective-permute-start.1
  36.9 1.3 %collective-permute-start.2 = (f32[4,512]{1,0:T(4,128)S(1)}, f32[4,512]{1,0:T(4,128)S(1)}, u32[]{:S(2)}, u32[]{:S(2)}) collective-permute-start(f32[4,512]{1,0:T(4,128)S(1)} %get-tuple-element.46), channel_id=1, source_target_pairs={{64,0},{65,1},{66,2},{67,3},{68,4},{69,5},{70,6},{71,7},{72,8},{73... | collective-permute-start | bytes 24584 | tf_op jit(solution)/shard_map/ppermute | solution.py:437
  38.2 10.5 %collective-permute-done.2.refs_0_ = f32[4,512]{1,0:T(4,128)S(1)} collective-permute-done((f32[4,512]{1,0:T(4,128)S(1)}, f32[4,512]{1,0:T(4,128)S(1)}, u32[]{:S(2)}, u32[]{:S(2)}) %collective-permute-start.2) | collective-permute-done | bytes 8224 | tf_op jit(solution)/shard_map/ppermute | solution.py:437
  49.0 1.0 collective-permute-start.3
  50.0 1.5 %collective-permute-done.3.refs_1_ = bf16[4,512]{1,0:T(4,128)(2,1)S(1)} collective-permute-done((bf16[4,512]{1,0:T(4,128)(2,1)S(1)}, bf16[4,512]{1,0:T(4,128)(2,1)S(1)}, u32[]{:S(2)}, u32[]{:S(2)}) %collective-permute-start.3) | collective-permute-done | bytes 4128 | tf_op jit(solution)/shard_map/ppermute | solution.py:340
  51.6 1.5 %collective-permute-start.4 = (bf16[8,512]{1,0:T(8,128)(2,1)S(1)}, bf16[8,512]{1,0:T(8,128)(2,1)S(1)}, u32[]{:S(2)}, u32[]{:S(2)}) collective-permute-start(bf16[8,512]{1,0:T(8,128)(2,1)S(1)} %shard_map.95.refs_0_), channel_id=1, source_target_pairs={{0,4},{1,5},{2,6},{3,7},{4,0},{5,1},{6,2},{7,3},{8,12},{9,13},{10,... | collective-permute-start | bytes 24584 | tf_op jit(solution)/shard_map/ppermute | solution.py:340
  53.0 2.0 %collective-permute-done.4.refs_1_ = bf16[8,512]{1,0:T(8,128)(2,1)S(1)} collective-permute-done((bf16[8,512]{1,0:T(8,128)(2,1)S(1)}, bf16[8,512]{1,0:T(8,128)(2,1)S(1)}, u32[]{:S(2)}, u32[]{:S(2)}) %collective-permute-start.4) | collective-permute-done | bytes 8224 | tf_op jit(solution)/shard_map/ppermute | solution.py:340
  55.0 3.2 %collective-permute-start.5 = (bf16[16,512]{1,0:T(8,128)(2,1)S(1)}, bf16[16,512]{1,0:T(8,128)(2,1)S(1)}, u32[]{:S(2)}, u32[]{:S(2)}) collective-permute-start(bf16[16,512]{1,0:T(8,128)(2,1)S(1)} %shard_map.96.refs_0_), channel_id=1, source_target_pairs={{0,14},{1,15},{2,12},{3,13},{4,10},{5,11},{6,8},{7,9},{8,6},{9,7},... | collective-permute-start | bytes 49160 | tf_op jit(solution)/shard_map/ppermute | solution.py:340
  58.2 1.1 collective-permute-done.5.refs_1_
  59.3 2.5 %collective-permute-start.7 = (bf16[32,512]{1,0:T(8,128)(2,1)S(1)}, bf16[32,512]{1,0:T(8,128)(2,1)S(1)}, u32[]{:S(2)}, u32[]{:S(2)}) collective-permute-start(bf16[32,512]{1,0:T(8,128)(2,1)S(1)} %shard_map.97.refs_0_), channel_id=1, source_target_pairs={{0,48},{1,49},{2,50},{3,51},{4,52},{5,53},{6,54},{7,55},{8,56},{9,... | collective-permute-start | bytes 98312 | tf_op jit(solution)/shard_map/ppermute | solution.py:340
  61.8 1.2 collective-permute-start.8
  63.3 2.8 %collective-permute-done.8.refs_3_ = bf16[32,512]{1,0:T(8,128)(2,1)S(1)} collective-permute-done((bf16[32,512]{1,0:T(8,128)(2,1)S(1)}, bf16[32,512]{1,0:T(8,128)(2,1)S(1)}, u32[]{:S(2)}, u32[]{:S(2)}) %collective-permute-start.8) | collective-permute-done | bytes 32800 | tf_op jit(solution)/shard_map/ppermute | solution.py:340
  66.1 7.5 %collective-permute-start.9 = (bf16[128,512]{1,0:T(8,128)(2,1)S(1)}, bf16[128,512]{1,0:T(8,128)(2,1)S(1)}, u32[]{:S(2)}, u32[]{:S(2)}) collective-permute-start(bf16[128,512]{1,0:T(8,128)(2,1)S(1)} %shard_map.98.near_ref), channel_id=1, source_target_pairs={{0,1},{1,0},{2,3},{3,2},{4,5},{5,4},{6,7},{7,6},{8,9},{9,8},{10,11... | collective-permute-start | bytes 393224 | tf_op jit(solution)/shard_map/ppermute | solution.py:340
  73.6 2.4 %shard_map.111 = (bf16[2048,512]{1,0:T(8,128)(2,1)S(1)}, bf16[512,512]{1,0:T(8,128)(2,1)S(1)}) custom-call(bf16[2048,128]{1,0:T(8,128)(2,1)S(1)} %get-tuple-element.48.turns_ref, bf16[512,128]{1,0:T(8,128)(2,1)S(1)} %get-tuple-element.49.exponent_ref, bf16[128,4096]{1,0:T(8,128)(2,1)S(1)} %get-tuple-element.50.levels_ref), custom_call_target="tpu_custom_call" | custom-call | flops 31457280 | bytes 2621440 | tf_op jit(solution)/shard_map/pallas_call | solution.py:160
  75.9 2.4 %shard_map.112 = (bf16[2048,512]{1,0:T(8,128)(2,1)S(1)}, bf16[512,512]{1,0:T(8,128)(2,1)S(1)}) custom-call(bf16[2048,128]{1,0:T(8,128)(2,1)S(1)} %get-tuple-element.48.turns_ref, bf16[512,128]{1,0:T(8,128)(2,1)S(1)} %get-tuple-element.49.exponent_ref, bf16[128,4096]{1,0:T(8,128)(2,1)S(1)} %get-tuple-element.50.levels_ref), custom_call_target="tpu_custom_call" | custom-call | flops 31457280 | bytes 2621440 | tf_op jit(solution)/shard_map/pallas_call | solution.py:160
  78.3 2.4 %shard_map.113 = (bf16[2048,512]{1,0:T(8,128)(2,1)S(1)}, bf16[512,512]{1,0:T(8,128)(2,1)S(1)}) custom-call(bf16[2048,128]{1,0:T(8,128)(2,1)S(1)} %get-tuple-element.48.turns_ref, bf16[512,128]{1,0:T(8,128)(2,1)S(1)} %get-tuple-element.49.exponent_ref, bf16[128,4096]{1,0:T(8,128)(2,1)S(1)} %get-tuple-element.50.levels_ref), custom_call_target="tpu_custom_call" | custom-call | flops 31457280 | bytes 2621440 | tf_op jit(solution)/shard_map/pallas_call | solution.py:160
  80.7 2.4 %shard_map.114 = (bf16[2048,512]{1,0:T(8,128)(2,1)S(1)}, bf16[512,512]{1,0:T(8,128)(2,1)S(1)}) custom-call(bf16[2048,128]{1,0:T(8,128)(2,1)S(1)} %get-tuple-element.48.turns_ref, bf16[512,128]{1,0:T(8,128)(2,1)S(1)} %get-tuple-element.49.exponent_ref, bf16[128,4096]{1,0:T(8,128)(2,1)S(1)} %get-tuple-element.50.levels_ref), custom_call_target="tpu_custom_call" | custom-call | flops 31457280 | bytes 2621440 | tf_op jit(solution)/shard_map/pallas_call | solution.py:160
  83.1 2.4 %shard_map.115 = (bf16[2048,512]{1,0:T(8,128)(2,1)S(1)}, bf16[512,512]{1,0:T(8,128)(2,1)S(1)}) custom-call(bf16[2048,128]{1,0:T(8,128)(2,1)S(1)} %get-tuple-element.48.turns_ref, bf16[512,128]{1,0:T(8,128)(2,1)S(1)} %get-tuple-element.49.exponent_ref, bf16[128,4096]{1,0:T(8,128)(2,1)S(1)} %get-tuple-element.50.levels_ref), custom_call_target="tpu_custom_call" | custom-call | flops 31457280 | bytes 2621440 | tf_op jit(solution)/shard_map/pallas_call | solution.py:160
  86.2 2.9 %shard_map.116.prior_ref = f32[256,2560]{1,0:T(8,128)S(1)} custom-call(bf16[256,2048]{1,0:T(8,128)(2,1)S(1)} %shard_map.105.coef_ref, bf16[2048,512]{1,0:T(8,128)(2,1)S(1)} %get-tuple-element.61.refs_0_, bf16[2048,512]{1,0:T(8,128)(2,1)S(1)} %get-tuple-element.62.refs_1_, bf16[2048,512]{1,0:T(8,128)(2,1)S(1)} %get-tuple-element.63.refs_2_, ...), custom_call_target="tpu_custom_call" | custom-call | flops 2684354560 | bytes 10485760 | tf_op jit(solution)/shard_map/pallas_call | solution.py:247
  89.1 0.8 shard_map.117
  90.3 2.4 %shard_map.106 = (bf16[2048,512]{1,0:T(8,128)(2,1)S(1)}, bf16[512,512]{1,0:T(8,128)(2,1)S(1)}) custom-call(bf16[2048,128]{1,0:T(8,128)(2,1)S(1)} %get-tuple-element.48.turns_ref, bf16[512,128]{1,0:T(8,128)(2,1)S(1)} %get-tuple-element.49.exponent_ref, bf16[128,4096]{1,0:T(8,128)(2,1)S(1)} %get-tuple-element.50.levels_ref), custom_call_target="tpu_custom_call" | custom-call | flops 31457280 | bytes 2621440 | tf_op jit(solution)/shard_map/pallas_call | solution.py:160
  92.6 2.4 %shard_map.107 = (bf16[2048,512]{1,0:T(8,128)(2,1)S(1)}, bf16[512,512]{1,0:T(8,128)(2,1)S(1)}) custom-call(bf16[2048,128]{1,0:T(8,128)(2,1)S(1)} %get-tuple-element.48.turns_ref, bf16[512,128]{1,0:T(8,128)(2,1)S(1)} %get-tuple-element.49.exponent_ref, bf16[128,4096]{1,0:T(8,128)(2,1)S(1)} %get-tuple-element.50.levels_ref), custom_call_target="tpu_custom_call" | custom-call | flops 31457280 | bytes 2621440 | tf_op jit(solution)/shard_map/pallas_call | solution.py:160
  95.0 2.4 %shard_map.108 = (bf16[2048,512]{1,0:T(8,128)(2,1)S(1)}, bf16[512,512]{1,0:T(8,128)(2,1)S(1)}) custom-call(bf16[2048,128]{1,0:T(8,128)(2,1)S(1)} %get-tuple-element.48.turns_ref, bf16[512,128]{1,0:T(8,128)(2,1)S(1)} %get-tuple-element.49.exponent_ref, bf16[128,4096]{1,0:T(8,128)(2,1)S(1)} %get-tuple-element.50.levels_ref), custom_call_target="tpu_custom_call" | custom-call | flops 31457280 | bytes 2621440 | tf_op jit(solution)/shard_map/pallas_call | solution.py:160
  97.5 2.7 %collective-permute-start.21 = (bf16[64,2560]{1,0:T(8,128)(2,1)S(1)}, bf16[64,2560]{1,0:T(8,128)(2,1)S(1)}, u32[]{:S(2)}, u32[]{:S(2)}) collective-permute-start(bf16[64,2560]{1,0:T(8,128)(2,1)S(1)} %get-tuple-element.74), channel_id=1, source_target_pairs={{0,192},{64,0},{128,64},{192,128},{1,193},{65,1},{129,65},{193,129... | collective-permute-start | bytes 983048 | tf_op jit(solution)/shard_map/ppermute | solution.py:470
  100.3 1.8 %shard_map.109.prior_ref = f32[256,1536]{1,0:T(8,128)S(1)} custom-call(bf16[256,2048]{1,0:T(8,128)(2,1)S(1)} %shard_map.105.coef_ref, bf16[2048,512]{1,0:T(8,128)(2,1)S(1)} %get-tuple-element.51.refs_0_, bf16[2048,512]{1,0:T(8,128)(2,1)S(1)} %get-tuple-element.52.refs_1_, bf16[2048,512]{1,0:T(8,128)(2,1)S(1)} %get-tuple-element.53.refs_2_), custom_call_target="tpu_custom_call" | custom-call | flops 1610612736 | bytes 6291456 | tf_op jit(solution)/shard_map/pallas_call | solution.py:247
  102.0 0.6 shard_map.110
  102.6 0.6 collective-permute-start.16
  103.2 1.9 %collective-permute-start.17 = (bf16[64,1536]{1,0:T(8,128)(2,1)S(1)}, bf16[64,1536]{1,0:T(8,128)(2,1)S(1)}, u32[]{:S(2)}, u32[]{:S(2)}) collective-permute-start(bf16[64,1536]{1,0:T(8,128)(2,1)S(1)} %get-tuple-element.59), channel_id=1, source_target_pairs={{0,128},{64,192},{128,0},{192,64},{1,129},{65,193},{129,1},{193,65... | collective-permute-start | bytes 589832 | tf_op jit(solution)/shard_map/ppermute | solution.py:470
  105.1 2.0 %collective-permute-start.18 = (bf16[64,1536]{1,0:T(8,128)(2,1)S(1)}, bf16[64,1536]{1,0:T(8,128)(2,1)S(1)}, u32[]{:S(2)}, u32[]{:S(2)}) collective-permute-start(bf16[64,1536]{1,0:T(8,128)(2,1)S(1)} %get-tuple-element.60), channel_id=1, source_target_pairs={{0,192},{64,0},{128,64},{192,128},{1,193},{65,1},{129,65},{193,129... | collective-permute-start | bytes 589832 | tf_op jit(solution)/shard_map/ppermute | solution.py:470
  107.0 1.3 %collective-permute-done.20.refs_2_ = bf16[64,2560]{1,0:T(8,128)(2,1)S(1)} collective-permute-done((bf16[64,2560]{1,0:T(8,128)(2,1)S(1)}, bf16[64,2560]{1,0:T(8,128)(2,1)S(1)}, u32[]{:S(2)}, u32[]{:S(2)}) %collective-permute-start.20) | collective-permute-done | bytes 327712 | tf_op jit(solution)/shard_map/ppermute | solution.py:470
  108.3 7.0 %collective-permute-done.21.refs_3_ = bf16[64,2560]{1,0:T(8,128)(2,1)S(1)} collective-permute-done((bf16[64,2560]{1,0:T(8,128)(2,1)S(1)}, bf16[64,2560]{1,0:T(8,128)(2,1)S(1)}, u32[]{:S(2)}, u32[]{:S(2)}) %collective-permute-start.21) | collective-permute-done | bytes 327712 | tf_op jit(solution)/shard_map/ppermute | solution.py:470
  115.3 1.0 shard_map.118.refs_4_
  116.7 7.1 %collective-permute-done.18.refs_3_ = bf16[64,1536]{1,0:T(8,128)(2,1)S(1)} collective-permute-done((bf16[64,1536]{1,0:T(8,128)(2,1)S(1)}, bf16[64,1536]{1,0:T(8,128)(2,1)S(1)}, u32[]{:S(2)}, u32[]{:S(2)}) %collective-permute-start.18) | collective-permute-done | bytes 196640 | tf_op jit(solution)/shard_map/ppermute | solution.py:470
  123.8 0.8 shard_map.119
  (30 shorter events, 2.3 us)
Async XLA Ops:
  0.0 3.8 %collective-permute-start.10 = (bf16[4,2048]{1,0:T(4,128)(2,1)}, bf16[4,2048]{1,0:T(4,128)(2,1)S(1)}, u32[]{:S(2)}, u32[]{:S(2)}) collective-permute-start(bf16[4,2048]{1,0:T(4,128)(2,1)} %refs_0_.3), channel_id=1, source_target_pairs={{0,2},{1,3},{2,0},{3,1},{4,6},{5,7},{6,4},{7,5},{8,10},{9,11},{10,... | collective-permute-start | bytes 49160 | tf_op jit(solution)/shard_map/ppermute | solution.py:340
  3.8 0.7 copy-start.1
  4.5 4.4 %collective-permute-start.11 = (bf16[8,2048]{1,0:T(8,128)(2,1)S(1)}, bf16[8,2048]{1,0:T(8,128)(2,1)S(1)}, u32[]{:S(2)}, u32[]{:S(2)}) collective-permute-start(bf16[8,2048]{1,0:T(8,128)(2,1)S(1)} %shard_map.100.refs_0_), channel_id=1, source_target_pairs={{0,4},{1,5},{2,6},{3,7},{4,0},{5,1},{6,2},{7,3},{8,12},{9,13},{10,... | collective-permute-start | bytes 98312 | tf_op jit(solution)/shard_map/ppermute | solution.py:340
  8.9 6.8 %collective-permute-start.12 = (bf16[16,2048]{1,0:T(8,128)(2,1)S(1)}, bf16[16,2048]{1,0:T(8,128)(2,1)S(1)}, u32[]{:S(2)}, u32[]{:S(2)}) collective-permute-start(bf16[16,2048]{1,0:T(8,128)(2,1)S(1)} %shard_map.101.refs_0_), channel_id=1, source_target_pairs={{0,14},{1,15},{2,12},{3,13},{4,10},{5,11},{6,8},{7,9},{8,6},{9,7},... | collective-permute-start | bytes 196616 | tf_op jit(solution)/shard_map/ppermute | solution.py:340
  15.7 3.9 %collective-permute-start.13 = (bf16[32,2048]{1,0:T(8,128)(2,1)S(1)}, bf16[32,2048]{1,0:T(8,128)(2,1)S(1)}, u32[]{:S(2)}, u32[]{:S(2)}) collective-permute-start(bf16[32,2048]{1,0:T(8,128)(2,1)S(1)} %shard_map.102.refs_0_), channel_id=1, source_target_pairs={{0,16},{1,17},{2,18},{3,19},{4,20},{5,21},{6,22},{7,23},{8,24},{9,... | collective-permute-start | bytes 393224 | tf_op jit(solution)/shard_map/ppermute | solution.py:340
  19.6 6.5 %collective-permute-start.14 = (bf16[64,2048]{1,0:T(8,128)(2,1)S(1)}, bf16[64,2048]{1,0:T(8,128)(2,1)S(1)}, u32[]{:S(2)}, u32[]{:S(2)}) collective-permute-start(bf16[64,2048]{1,0:T(8,128)(2,1)S(1)} %shard_map.103.refs_0_), channel_id=1, source_target_pairs={{0,48},{1,49},{2,50},{3,51},{4,52},{5,53},{6,54},{7,55},{8,56},{9,... | collective-permute-start | bytes 786440 | tf_op jit(solution)/shard_map/ppermute | solution.py:340
  26.2 59.6 %collective-permute-start.15 = (bf16[128,2048]{1,0:T(8,128)(2,1)S(1)}, bf16[128,2048]{1,0:T(8,128)(2,1)S(1)}, u32[]{:S(2)}, u32[]{:S(2)}) collective-permute-start(bf16[128,2048]{1,0:T(8,128)(2,1)S(1)} %shard_map.104.near_ref), channel_id=1, source_target_pairs={{0,1},{1,0},{2,3},{3,2},{4,5},{5,4},{6,7},{7,6},{8,9},{9,8},{10,11... | collective-permute-start | bytes 1572872 | tf_op jit(solution)/shard_map/ppermute | solution.py:340
  32.9 2.6 %copy-start = (f32[4,512]{1,0:T(4,128)S(1)}, f32[4,512]{1,0:T(4,128)}, u32[]{:S(2)}) copy-start(f32[4,512]{1,0:T(4,128)} %whitened_ref.7) | copy-start | bytes 24580
  35.5 0.7 collective-permute-start
  36.2 0.7 collective-permute-start.1
  36.9 11.8 %collective-permute-start.2 = (f32[4,512]{1,0:T(4,128)S(1)}, f32[4,512]{1,0:T(4,128)S(1)}, u32[]{:S(2)}, u32[]{:S(2)}) collective-permute-start(f32[4,512]{1,0:T(4,128)S(1)} %get-tuple-element.46), channel_id=1, source_target_pairs={{64,0},{65,1},{66,2},{67,3},{68,4},{69,5},{70,6},{71,7},{72,8},{73... | collective-permute-start | bytes 24584 | tf_op jit(solution)/shard_map/ppermute | solution.py:437
  49.0 2.5 %collective-permute-start.3 = (bf16[4,512]{1,0:T(4,128)(2,1)S(1)}, bf16[4,512]{1,0:T(4,128)(2,1)S(1)}, u32[]{:S(2)}, u32[]{:S(2)}) collective-permute-start(bf16[4,512]{1,0:T(4,128)(2,1)S(1)} %shard_map.94.refs_0_), channel_id=1, source_target_pairs={{0,2},{1,3},{2,0},{3,1},{4,6},{5,7},{6,4},{7,5},{8,10},{9,11},{10,... | collective-permute-start | bytes 12296 | tf_op jit(solution)/shard_map/ppermute | solution.py:340
  51.6 3.4 %collective-permute-start.4 = (bf16[8,512]{1,0:T(8,128)(2,1)S(1)}, bf16[8,512]{1,0:T(8,128)(2,1)S(1)}, u32[]{:S(2)}, u32[]{:S(2)}) collective-permute-start(bf16[8,512]{1,0:T(8,128)(2,1)S(1)} %shard_map.95.refs_0_), channel_id=1, source_target_pairs={{0,4},{1,5},{2,6},{3,7},{4,0},{5,1},{6,2},{7,3},{8,12},{9,13},{10,... | collective-permute-start | bytes 24584 | tf_op jit(solution)/shard_map/ppermute | solution.py:340
  55.0 4.3 %collective-permute-start.5 = (bf16[16,512]{1,0:T(8,128)(2,1)S(1)}, bf16[16,512]{1,0:T(8,128)(2,1)S(1)}, u32[]{:S(2)}, u32[]{:S(2)}) collective-permute-start(bf16[16,512]{1,0:T(8,128)(2,1)S(1)} %shard_map.96.refs_0_), channel_id=1, source_target_pairs={{0,14},{1,15},{2,12},{3,13},{4,10},{5,11},{6,8},{7,9},{8,6},{9,7},... | collective-permute-start | bytes 49160 | tf_op jit(solution)/shard_map/ppermute | solution.py:340
  59.3 3.7 %collective-permute-start.6 = (bf16[32,512]{1,0:T(8,128)(2,1)S(1)}, bf16[32,512]{1,0:T(8,128)(2,1)S(1)}, u32[]{:S(2)}, u32[]{:S(2)}) collective-permute-start(bf16[32,512]{1,0:T(8,128)(2,1)S(1)} %shard_map.97.refs_0_), channel_id=1, source_target_pairs={{0,16},{1,17},{2,18},{3,19},{4,20},{5,21},{6,22},{7,23},{8,24},{9,... | collective-permute-start | bytes 98312 | tf_op jit(solution)/shard_map/ppermute | solution.py:340
  59.3 4.0 %collective-permute-start.7 = (bf16[32,512]{1,0:T(8,128)(2,1)S(1)}, bf16[32,512]{1,0:T(8,128)(2,1)S(1)}, u32[]{:S(2)}, u32[]{:S(2)}) collective-permute-start(bf16[32,512]{1,0:T(8,128)(2,1)S(1)} %shard_map.97.refs_0_), channel_id=1, source_target_pairs={{0,48},{1,49},{2,50},{3,51},{4,52},{5,53},{6,54},{7,55},{8,56},{9,... | collective-permute-start | bytes 98312 | tf_op jit(solution)/shard_map/ppermute | solution.py:340
  61.8 4.3 %collective-permute-start.8 = (bf16[32,512]{1,0:T(8,128)(2,1)S(1)}, bf16[32,512]{1,0:T(8,128)(2,1)S(1)}, u32[]{:S(2)}, u32[]{:S(2)}) collective-permute-start(bf16[32,512]{1,0:T(8,128)(2,1)S(1)} %shard_map.97.refs_0_), channel_id=1, source_target_pairs={{0,32},{1,33},{2,34},{3,35},{4,36},{5,37},{6,38},{7,39},{8,40},{9,... | collective-permute-start | bytes 98312 | tf_op jit(solution)/shard_map/ppermute | solution.py:340
  66.1 19.4 %collective-permute-start.9 = (bf16[128,512]{1,0:T(8,128)(2,1)S(1)}, bf16[128,512]{1,0:T(8,128)(2,1)S(1)}, u32[]{:S(2)}, u32[]{:S(2)}) collective-permute-start(bf16[128,512]{1,0:T(8,128)(2,1)S(1)} %shard_map.98.near_ref), channel_id=1, source_target_pairs={{0,1},{1,0},{2,3},{3,2},{4,5},{5,4},{6,7},{7,6},{8,9},{9,8},{10,11... | collective-permute-start | bytes 393224 | tf_op jit(solution)/shard_map/ppermute | solution.py:340
  89.9 15.1 %collective-permute-start.19 = (bf16[64,2560]{1,0:T(8,128)(2,1)S(1)}, bf16[64,2560]{1,0:T(8,128)(2,1)S(1)}, u32[]{:S(2)}, u32[]{:S(2)}) collective-permute-start(bf16[64,2560]{1,0:T(8,128)(2,1)S(1)} %get-tuple-element.72), channel_id=1, source_target_pairs={{0,64},{64,128},{128,192},{192,0},{1,65},{65,129},{129,193},{193,1... | collective-permute-start | bytes 983048 | tf_op jit(solution)/shard_map/ppermute | solution.py:470
  97.4 10.9 %collective-permute-start.20 = (bf16[64,2560]{1,0:T(8,128)(2,1)S(1)}, bf16[64,2560]{1,0:T(8,128)(2,1)S(1)}, u32[]{:S(2)}, u32[]{:S(2)}) collective-permute-start(bf16[64,2560]{1,0:T(8,128)(2,1)S(1)} %get-tuple-element.73), channel_id=1, source_target_pairs={{0,128},{64,192},{128,0},{192,64},{1,129},{65,193},{129,1},{193,65... | collective-permute-start | bytes 983048 | tf_op jit(solution)/shard_map/ppermute | solution.py:470
  97.5 17.8 %collective-permute-start.21 = (bf16[64,2560]{1,0:T(8,128)(2,1)S(1)}, bf16[64,2560]{1,0:T(8,128)(2,1)S(1)}, u32[]{:S(2)}, u32[]{:S(2)}) collective-permute-start(bf16[64,2560]{1,0:T(8,128)(2,1)S(1)} %get-tuple-element.74), channel_id=1, source_target_pairs={{0,192},{64,0},{128,64},{192,128},{1,193},{65,1},{129,65},{193,129... | collective-permute-start | bytes 983048 | tf_op jit(solution)/shard_map/ppermute | solution.py:470
  102.6 13.7 %collective-permute-start.16 = (bf16[64,1536]{1,0:T(8,128)(2,1)S(1)}, bf16[64,1536]{1,0:T(8,128)(2,1)S(1)}, u32[]{:S(2)}, u32[]{:S(2)}) collective-permute-start(bf16[64,1536]{1,0:T(8,128)(2,1)S(1)} %get-tuple-element.58), channel_id=1, source_target_pairs={{0,64},{64,128},{128,192},{192,0},{1,65},{65,129},{129,193},{193,1... | collective-permute-start | bytes 589832 | tf_op jit(solution)/shard_map/ppermute | solution.py:470
  103.2 13.5 %collective-permute-start.17 = (bf16[64,1536]{1,0:T(8,128)(2,1)S(1)}, bf16[64,1536]{1,0:T(8,128)(2,1)S(1)}, u32[]{:S(2)}, u32[]{:S(2)}) collective-permute-start(bf16[64,1536]{1,0:T(8,128)(2,1)S(1)} %get-tuple-element.59), channel_id=1, source_target_pairs={{0,128},{64,192},{128,0},{192,64},{1,129},{65,193},{129,1},{193,65... | collective-permute-start | bytes 589832 | tf_op jit(solution)/shard_map/ppermute | solution.py:470
  105.1 18.7 %collective-permute-start.18 = (bf16[64,1536]{1,0:T(8,128)(2,1)S(1)}, bf16[64,1536]{1,0:T(8,128)(2,1)S(1)}, u32[]{:S(2)}, u32[]{:S(2)}) collective-permute-start(bf16[64,1536]{1,0:T(8,128)(2,1)S(1)} %get-tuple-element.60), channel_id=1, source_target_pairs={{0,192},{64,0},{128,64},{192,128},{1,193},{65,1},{129,65},{193,129... | collective-permute-start | bytes 589832 | tf_op jit(solution)/shard_map/ppermute | solution.py:470

commit v8 on v7

--- a/solution.py
+++ b/solution.py
@@ -141,38 +141,33 @@
     return (0.015625 - sine * sine).astype(BF16)
 
 
-def tile_kernel(turns_ref, exponent_ref, levels_ref, features_ref, kernel_ref):
-    levels = levels_ref[...]
-    for start in range(0, turns_ref.shape[0], ROW_CHUNK):
-        rows = slice(start, start + ROW_CHUNK)
-        turns = jnp.dot(turns_ref[rows, :], levels, preferred_element_type=F32)
-        features_ref[rows, :] = cosine(turns)
-    for start in range(0, exponent_ref.shape[0], ROW_CHUNK):
-        rows = slice(start, start + ROW_CHUNK)
-        exponent = jnp.dot(exponent_ref[rows, :], levels, preferred_element_type=F32)
-        kernel_ref[rows, :] = jnp.exp2(exponent).astype(BF16)
+def tile_kernel(first, turns_ref, exponent_ref, levels_ref, features_ref, kernel_ref):
+    @pl.loop(0, features_ref.shape[1] // CAND_TILE)
+    def _(tile):
+        start = pl.multiple_of(tile * CAND_TILE, CAND_TILE)
+        cols = pl.ds(start, CAND_TILE)
+        levels = levels_ref[:, pl.ds(pl.multiple_of(first + start, CAND_TILE), CAND_TILE)]
+        for start in range(0, turns_ref.shape[0], ROW_CHUNK):
+            rows = slice(start, start + ROW_CHUNK)
+            turns = jnp.dot(turns_ref[rows, :], levels, preferred_element_type=F32)
+            features_ref[rows, cols] = cosine(turns)
+        for start in range(0, exponent_ref.shape[0], ROW_CHUNK):
+            rows = slice(start, start + ROW_CHUNK)
+            exponent = jnp.dot(exponent_ref[rows, :], levels, preferred_element_type=F32)
+            kernel_ref[rows, cols] = jnp.exp2(exponent).astype(BF16)
 
 
 def tiles(turns, exponent, levels, chunk):
     feats, obs = turns.shape[0], exponent.shape[0]
     cands = levels.shape[1] // CHUNKS
-    steps = cands // CAND_TILE
-    return pl.pallas_call(
-        tile_kernel,
+    return pl.pallas_call(
+        functools.partial(tile_kernel, chunk * cands),
         out_shape=(
             jax.ShapeDtypeStruct((feats, cands), BF16),
             jax.ShapeDtypeStruct((obs, cands), BF16),
         ),
-        grid=(steps,),
-        in_specs=[
-            whole(),
-            whole(),
-            pl.BlockSpec((LANES, CAND_TILE), lambda i: (0, i + chunk * steps)),
-        ],
-        out_specs=(
-            pl.BlockSpec((feats, CAND_TILE), lambda i: (0, i)),
-            pl.BlockSpec((obs, CAND_TILE), lambda i: (0, i)),
-        ),
+        in_specs=[whole()] * 3,
+        out_specs=(whole(),) * 2,
         compiler_params=params(),
         cost_estimate=pl.CostEstimate(
             flops=24 * (feats + obs) * cands,

time: 126 us -> 124 us (0.984)
  Pallas kernels: 30.6 us -> 28.6 us
    pallas_call x8, Pallas kernels: 19 us -> 17.1 us  [tiles(): pl.pallas_call(functools.partial(tile_kernel, chunk * cands), out_shape=(...]
  transfers between devices with their start and end apart: 22 -> 22, of which waited for: 15 -> 15; matrix products, arithmetic and copies ran while one was open for 0% -> 0% of each run, Pallas kernels for 20% -> 19%
where the time goes in v8:
time: 124 us; the launch traced here: 123 us
  starting transfers between devices  47.8 us (39%)
  waiting for transfers between devices  45.2 us (36%)
  Pallas kernels  28.6 us (23%)
    ppermute x13, starting transfers between devices, swap(): return lax.ppermute(held, 'cand', pairs)  37.7 us
    ppermute x13, waiting for transfers between devices, swap(): return lax.ppermute(held, 'cand', pairs)  18.9 us
    pallas_call x8, Pallas kernels, tiles(): pl.pallas_call(functools.partial(tile_kernel, chunk * cands), out_shape=(...  17.1 us
    ppermute x6, waiting for transfers between devices, body(): arrived.append(lax.ppermute(block, 'rows', pairs))  15.7 us
    ppermute x3, waiting for transfers between devices, solve_chain(): carried = lax.ppermute(carried, 'rows', [(section, section - 1)])  10.5 us
    ppermute x6, starting transfers between devices, body(): arrived.append(lax.ppermute(block, 'rows', pairs))  7.56 us
    pallas_call x2, Pallas kernels, prior_product(): pl.pallas_call(prior_kernel, out_shape=jax.ShapeDtypeStruct((rows, cands)...  4.64 us
    ppermute x3, starting transfers between devices, solve_chain(): carried = lax.ppermute(carried, 'rows', [(section, section - 1)])  2.62 us
  transfers between devices with their start and end apart: 22, of which 15 were waited for; matrix products, arithmetic and copies ran while one was open for 0% of the time, Pallas kernels for 19%

profile of v8, /device:TPU:1, one launch (start us, length us, event | category | flops | bytes accessed | tf_op | source)
XLA Modules:
  0.0 122.8 jit_solution(16091011506318397028)
XLA Ops:
  0.0 2.5 %collective-permute-start.10 = (bf16[4,2048]{1,0:T(4,128)(2,1)}, bf16[4,2048]{1,0:T(4,128)(2,1)S(1)}, u32[]{:S(2)}, u32[]{:S(2)}) collective-permute-start(bf16[4,2048]{1,0:T(4,128)(2,1)} %refs_0_.3), channel_id=1, source_target_pairs={{0,2},{1,3},{2,0},{3,1},{4,6},{5,7},{6,4},{7,5},{8,10},{9,11},{10,... | collective-permute-start | bytes 49160 | tf_op jit(solution)/shard_map/ppermute | solution.py:335
  2.5 1.3 %collective-permute-done.10.refs_1_ = bf16[4,2048]{1,0:T(4,128)(2,1)S(1)} collective-permute-done((bf16[4,2048]{1,0:T(4,128)(2,1)}, bf16[4,2048]{1,0:T(4,128)(2,1)S(1)}, u32[]{:S(2)}, u32[]{:S(2)}) %collective-permute-start.10) | collective-permute-done | bytes 16416 | tf_op jit(solution)/shard_map/ppermute | solution.py:335
  3.8 0.7 copy-done.1
  4.5 3.1 %collective-permute-start.11 = (bf16[8,2048]{1,0:T(8,128)(2,1)S(1)}, bf16[8,2048]{1,0:T(8,128)(2,1)S(1)}, u32[]{:S(2)}, u32[]{:S(2)}) collective-permute-start(bf16[8,2048]{1,0:T(8,128)(2,1)S(1)} %shard_map.100.refs_0_), channel_id=1, source_target_pairs={{0,4},{1,5},{2,6},{3,7},{4,0},{5,1},{6,2},{7,3},{8,12},{9,13},{10,... | collective-permute-start | bytes 98312 | tf_op jit(solution)/shard_map/ppermute | solution.py:335
  7.6 1.3 %collective-permute-done.11.refs_1_ = bf16[8,2048]{1,0:T(8,128)(2,1)S(1)} collective-permute-done((bf16[8,2048]{1,0:T(8,128)(2,1)S(1)}, bf16[8,2048]{1,0:T(8,128)(2,1)S(1)}, u32[]{:S(2)}, u32[]{:S(2)}) %collective-permute-start.11) | collective-permute-done | bytes 32800 | tf_op jit(solution)/shard_map/ppermute | solution.py:335
  8.9 4.8 %collective-permute-start.12 = (bf16[16,2048]{1,0:T(8,128)(2,1)S(1)}, bf16[16,2048]{1,0:T(8,128)(2,1)S(1)}, u32[]{:S(2)}, u32[]{:S(2)}) collective-permute-start(bf16[16,2048]{1,0:T(8,128)(2,1)S(1)} %shard_map.101.refs_0_), channel_id=1, source_target_pairs={{0,14},{1,15},{2,12},{3,13},{4,10},{5,11},{6,8},{7,9},{8,6},{9,7},... | collective-permute-start | bytes 196616 | tf_op jit(solution)/shard_map/ppermute | solution.py:335
  13.7 2.0 %collective-permute-done.12.refs_1_ = bf16[16,2048]{1,0:T(8,128)(2,1)S(1)} collective-permute-done((bf16[16,2048]{1,0:T(8,128)(2,1)S(1)}, bf16[16,2048]{1,0:T(8,128)(2,1)S(1)}, u32[]{:S(2)}, u32[]{:S(2)}) %collective-permute-start.12) | collective-permute-done | bytes 65568 | tf_op jit(solution)/shard_map/ppermute | solution.py:335
  15.7 1.3 %collective-permute-start.13 = (bf16[32,2048]{1,0:T(8,128)(2,1)S(1)}, bf16[32,2048]{1,0:T(8,128)(2,1)S(1)}, u32[]{:S(2)}, u32[]{:S(2)}) collective-permute-start(bf16[32,2048]{1,0:T(8,128)(2,1)S(1)} %shard_map.102.refs_0_), channel_id=1, source_target_pairs={{0,16},{1,17},{2,18},{3,19},{4,20},{5,21},{6,22},{7,23},{8,24},{9,... | collective-permute-start | bytes 393224 | tf_op jit(solution)/shard_map/ppermute | solution.py:335
  17.0 2.6 %collective-permute-done.13.refs_1_ = bf16[32,2048]{1,0:T(8,128)(2,1)S(1)} collective-permute-done((bf16[32,2048]{1,0:T(8,128)(2,1)S(1)}, bf16[32,2048]{1,0:T(8,128)(2,1)S(1)}, u32[]{:S(2)}, u32[]{:S(2)}) %collective-permute-start.13) | collective-permute-done | bytes 131104 | tf_op jit(solution)/shard_map/ppermute | solution.py:335
  19.6 2.6 %collective-permute-start.14 = (bf16[64,2048]{1,0:T(8,128)(2,1)S(1)}, bf16[64,2048]{1,0:T(8,128)(2,1)S(1)}, u32[]{:S(2)}, u32[]{:S(2)}) collective-permute-start(bf16[64,2048]{1,0:T(8,128)(2,1)S(1)} %shard_map.103.refs_0_), channel_id=1, source_target_pairs={{0,48},{1,49},{2,50},{3,51},{4,52},{5,53},{6,54},{7,55},{8,56},{9,... | collective-permute-start | bytes 786440 | tf_op jit(solution)/shard_map/ppermute | solution.py:335
  22.2 4.0 %collective-permute-done.14.refs_1_ = bf16[64,2048]{1,0:T(8,128)(2,1)S(1)} collective-permute-done((bf16[64,2048]{1,0:T(8,128)(2,1)S(1)}, bf16[64,2048]{1,0:T(8,128)(2,1)S(1)}, u32[]{:S(2)}, u32[]{:S(2)}) %collective-permute-start.14) | collective-permute-done | bytes 262176 | tf_op jit(solution)/shard_map/ppermute | solution.py:335
  26.2 6.7 %collective-permute-start.15 = (bf16[128,2048]{1,0:T(8,128)(2,1)S(1)}, bf16[128,2048]{1,0:T(8,128)(2,1)S(1)}, u32[]{:S(2)}, u32[]{:S(2)}) collective-permute-start(bf16[128,2048]{1,0:T(8,128)(2,1)S(1)} %shard_map.104.near_ref), channel_id=1, source_target_pairs={{0,1},{1,0},{2,3},{3,2},{4,5},{5,4},{6,7},{7,6},{8,9},{9,8},{10,11... | collective-permute-start | bytes 1572872 | tf_op jit(solution)/shard_map/ppermute | solution.py:335
  32.9 2.6 %prepare.1 = (bf16[2048,128]{1,0:T(8,128)(2,1)S(1)}, bf16[512,128]{1,0:T(8,128)(2,1)S(1)}, bf16[128,4096]{1,0:T(8,128)(2,1)S(1)}, f32[512,512]{1,0:T(8,128)S(1)}, f32[512,1536]{1,0:T(8,128)S(1)}) custom-call(f32[22,2048]{1,0:T(8,128)} %refs_0_.2, f32[1,2048]{1,0:T(1,128)} %bitcast.3, f32[22,512]{1,0:T(8,128)} %refs_2_.1, f32[1,22]{1,0:T(1,128)} %bitcast.4, ...), custom_call_target="tpu_custom_call" | custom-call | flops 10000000 | bytes 8388608 | tf_op jit(solution)/shard_map/prepare/pallas_call | solution.py:107
  35.5 0.7 collective-permute-start
  36.2 0.7 collective-permute-start.1
  36.9 1.3 %collective-permute-start.2 = (f32[4,512]{1,0:T(4,128)S(1)}, f32[4,512]{1,0:T(4,128)S(1)}, u32[]{:S(2)}, u32[]{:S(2)}) collective-permute-start(f32[4,512]{1,0:T(4,128)S(1)} %get-tuple-element.46), channel_id=1, source_target_pairs={{64,0},{65,1},{66,2},{67,3},{68,4},{69,5},{70,6},{71,7},{72,8},{73... | collective-permute-start | bytes 24584 | tf_op jit(solution)/shard_map/ppermute | solution.py:432
  38.2 10.5 %collective-permute-done.2.refs_0_ = f32[4,512]{1,0:T(4,128)S(1)} collective-permute-done((f32[4,512]{1,0:T(4,128)S(1)}, f32[4,512]{1,0:T(4,128)S(1)}, u32[]{:S(2)}, u32[]{:S(2)}) %collective-permute-start.2) | collective-permute-done | bytes 8224 | tf_op jit(solution)/shard_map/ppermute | solution.py:432
  49.0 1.0 collective-permute-start.3
  50.0 1.5 %collective-permute-done.3.refs_1_ = bf16[4,512]{1,0:T(4,128)(2,1)S(1)} collective-permute-done((bf16[4,512]{1,0:T(4,128)(2,1)S(1)}, bf16[4,512]{1,0:T(4,128)(2,1)S(1)}, u32[]{:S(2)}, u32[]{:S(2)}) %collective-permute-start.3) | collective-permute-done | bytes 4128 | tf_op jit(solution)/shard_map/ppermute | solution.py:335
  51.6 1.5 %collective-permute-start.4 = (bf16[8,512]{1,0:T(8,128)(2,1)S(1)}, bf16[8,512]{1,0:T(8,128)(2,1)S(1)}, u32[]{:S(2)}, u32[]{:S(2)}) collective-permute-start(bf16[8,512]{1,0:T(8,128)(2,1)S(1)} %shard_map.95.refs_0_), channel_id=1, source_target_pairs={{0,4},{1,5},{2,6},{3,7},{4,0},{5,1},{6,2},{7,3},{8,12},{9,13},{10,... | collective-permute-start | bytes 24584 | tf_op jit(solution)/shard_map/ppermute | solution.py:335
  53.0 2.0 %collective-permute-done.4.refs_1_ = bf16[8,512]{1,0:T(8,128)(2,1)S(1)} collective-permute-done((bf16[8,512]{1,0:T(8,128)(2,1)S(1)}, bf16[8,512]{1,0:T(8,128)(2,1)S(1)}, u32[]{:S(2)}, u32[]{:S(2)}) %collective-permute-start.4) | collective-permute-done | bytes 8224 | tf_op jit(solution)/shard_map/ppermute | solution.py:335
  55.0 3.2 %collective-permute-start.5 = (bf16[16,512]{1,0:T(8,128)(2,1)S(1)}, bf16[16,512]{1,0:T(8,128)(2,1)S(1)}, u32[]{:S(2)}, u32[]{:S(2)}) collective-permute-start(bf16[16,512]{1,0:T(8,128)(2,1)S(1)} %shard_map.96.refs_0_), channel_id=1, source_target_pairs={{0,14},{1,15},{2,12},{3,13},{4,10},{5,11},{6,8},{7,9},{8,6},{9,7},... | collective-permute-start | bytes 49160 | tf_op jit(solution)/shard_map/ppermute | solution.py:335
  58.2 1.1 collective-permute-done.5.refs_1_
  59.3 2.5 %collective-permute-start.7 = (bf16[32,512]{1,0:T(8,128)(2,1)S(1)}, bf16[32,512]{1,0:T(8,128)(2,1)S(1)}, u32[]{:S(2)}, u32[]{:S(2)}) collective-permute-start(bf16[32,512]{1,0:T(8,128)(2,1)S(1)} %shard_map.97.refs_0_), channel_id=1, source_target_pairs={{0,48},{1,49},{2,50},{3,51},{4,52},{5,53},{6,54},{7,55},{8,56},{9,... | collective-permute-start | bytes 98312 | tf_op jit(solution)/shard_map/ppermute | solution.py:335
  61.8 1.2 collective-permute-start.8
  63.3 2.8 %collective-permute-done.8.refs_3_ = bf16[32,512]{1,0:T(8,128)(2,1)S(1)} collective-permute-done((bf16[32,512]{1,0:T(8,128)(2,1)S(1)}, bf16[32,512]{1,0:T(8,128)(2,1)S(1)}, u32[]{:S(2)}, u32[]{:S(2)}) %collective-permute-start.8) | collective-permute-done | bytes 32800 | tf_op jit(solution)/shard_map/ppermute | solution.py:335
  66.1 7.5 %collective-permute-start.9 = (bf16[128,512]{1,0:T(8,128)(2,1)S(1)}, bf16[128,512]{1,0:T(8,128)(2,1)S(1)}, u32[]{:S(2)}, u32[]{:S(2)}) collective-permute-start(bf16[128,512]{1,0:T(8,128)(2,1)S(1)} %shard_map.98.near_ref), channel_id=1, source_target_pairs={{0,1},{1,0},{2,3},{3,2},{4,5},{5,4},{6,7},{7,6},{8,9},{9,8},{10,11... | collective-permute-start | bytes 393224 | tf_op jit(solution)/shard_map/ppermute | solution.py:335
  73.6 2.1 %shard_map.111 = (bf16[2048,512]{1,0:T(8,128)(2,1)S(1)}, bf16[512,512]{1,0:T(8,128)(2,1)S(1)}) custom-call(bf16[2048,128]{1,0:T(8,128)(2,1)S(1)} %get-tuple-element.48.turns_ref, bf16[512,128]{1,0:T(8,128)(2,1)S(1)} %get-tuple-element.49.exponent_ref, bf16[128,4096]{1,0:T(8,128)(2,1)S(1)} %get-tuple-element.50.levels_ref), custom_call_target="tpu_custom_call" | custom-call | flops 31457280 | bytes 2621440 | tf_op jit(solution)/shard_map/pallas_call | solution.py:163
  75.7 2.1 %shard_map.112 = (bf16[2048,512]{1,0:T(8,128)(2,1)S(1)}, bf16[512,512]{1,0:T(8,128)(2,1)S(1)}) custom-call(bf16[2048,128]{1,0:T(8,128)(2,1)S(1)} %get-tuple-element.48.turns_ref, bf16[512,128]{1,0:T(8,128)(2,1)S(1)} %get-tuple-element.49.exponent_ref, bf16[128,4096]{1,0:T(8,128)(2,1)S(1)} %get-tuple-element.50.levels_ref), custom_call_target="tpu_custom_call" | custom-call | flops 31457280 | bytes 2621440 | tf_op jit(solution)/shard_map/pallas_call | solution.py:163
  77.8 2.1 %shard_map.113 = (bf16[2048,512]{1,0:T(8,128)(2,1)S(1)}, bf16[512,512]{1,0:T(8,128)(2,1)S(1)}) custom-call(bf16[2048,128]{1,0:T(8,128)(2,1)S(1)} %get-tuple-element.48.turns_ref, bf16[512,128]{1,0:T(8,128)(2,1)S(1)} %get-tuple-element.49.exponent_ref, bf16[128,4096]{1,0:T(8,128)(2,1)S(1)} %get-tuple-element.50.levels_ref), custom_call_target="tpu_custom_call" | custom-call | flops 31457280 | bytes 2621440 | tf_op jit(solution)/shard_map/pallas_call | solution.py:163
  80.0 2.1 %shard_map.114 = (bf16[2048,512]{1,0:T(8,128)(2,1)S(1)}, bf16[512,512]{1,0:T(8,128)(2,1)S(1)}) custom-call(bf16[2048,128]{1,0:T(8,128)(2,1)S(1)} %get-tuple-element.48.turns_ref, bf16[512,128]{1,0:T(8,128)(2,1)S(1)} %get-tuple-element.49.exponent_ref, bf16[128,4096]{1,0:T(8,128)(2,1)S(1)} %get-tuple-element.50.levels_ref), custom_call_target="tpu_custom_call" | custom-call | flops 31457280 | bytes 2621440 | tf_op jit(solution)/shard_map/pallas_call | solution.py:163
  82.1 2.1 %shard_map.115 = (bf16[2048,512]{1,0:T(8,128)(2,1)S(1)}, bf16[512,512]{1,0:T(8,128)(2,1)S(1)}) custom-call(bf16[2048,128]{1,0:T(8,128)(2,1)S(1)} %get-tuple-element.48.turns_ref, bf16[512,128]{1,0:T(8,128)(2,1)S(1)} %get-tuple-element.49.exponent_ref, bf16[128,4096]{1,0:T(8,128)(2,1)S(1)} %get-tuple-element.50.levels_ref), custom_call_target="tpu_custom_call" | custom-call | flops 31457280 | bytes 2621440 | tf_op jit(solution)/shard_map/pallas_call | solution.py:163
  85.0 2.9 %shard_map.116.prior_ref = f32[256,2560]{1,0:T(8,128)S(1)} custom-call(bf16[256,2048]{1,0:T(8,128)(2,1)S(1)} %shard_map.105.coef_ref, bf16[2048,512]{1,0:T(8,128)(2,1)S(1)} %get-tuple-element.61.refs_0_, bf16[2048,512]{1,0:T(8,128)(2,1)S(1)} %get-tuple-element.62.refs_1_, bf16[2048,512]{1,0:T(8,128)(2,1)S(1)} %get-tuple-element.63.refs_2_, ...), custom_call_target="tpu_custom_call" | custom-call | flops 2684354560 | bytes 10485760 | tf_op jit(solution)/shard_map/pallas_call | solution.py:242
  87.9 0.8 shard_map.117
  88.8 2.1 %shard_map.106 = (bf16[2048,512]{1,0:T(8,128)(2,1)S(1)}, bf16[512,512]{1,0:T(8,128)(2,1)S(1)}) custom-call(bf16[2048,128]{1,0:T(8,128)(2,1)S(1)} %get-tuple-element.48.turns_ref, bf16[512,128]{1,0:T(8,128)(2,1)S(1)} %get-tuple-element.49.exponent_ref, bf16[128,4096]{1,0:T(8,128)(2,1)S(1)} %get-tuple-element.50.levels_ref), custom_call_target="tpu_custom_call" | custom-call | flops 31457280 | bytes 2621440 | tf_op jit(solution)/shard_map/pallas_call | solution.py:163
  90.9 2.1 %shard_map.107 = (bf16[2048,512]{1,0:T(8,128)(2,1)S(1)}, bf16[512,512]{1,0:T(8,128)(2,1)S(1)}) custom-call(bf16[2048,128]{1,0:T(8,128)(2,1)S(1)} %get-tuple-element.48.turns_ref, bf16[512,128]{1,0:T(8,128)(2,1)S(1)} %get-tuple-element.49.exponent_ref, bf16[128,4096]{1,0:T(8,128)(2,1)S(1)} %get-tuple-element.50.levels_ref), custom_call_target="tpu_custom_call" | custom-call | flops 31457280 | bytes 2621440 | tf_op jit(solution)/shard_map/pallas_call | solution.py:163
  93.1 2.1 %shard_map.108 = (bf16[2048,512]{1,0:T(8,128)(2,1)S(1)}, bf16[512,512]{1,0:T(8,128)(2,1)S(1)}) custom-call(bf16[2048,128]{1,0:T(8,128)(2,1)S(1)} %get-tuple-element.48.turns_ref, bf16[512,128]{1,0:T(8,128)(2,1)S(1)} %get-tuple-element.49.exponent_ref, bf16[128,4096]{1,0:T(8,128)(2,1)S(1)} %get-tuple-element.50.levels_ref), custom_call_target="tpu_custom_call" | custom-call | flops 31457280 | bytes 2621440 | tf_op jit(solution)/shard_map/pallas_call | solution.py:163
  95.6 2.7 %collective-permute-start.21 = (bf16[64,2560]{1,0:T(8,128)(2,1)S(1)}, bf16[64,2560]{1,0:T(8,128)(2,1)S(1)}, u32[]{:S(2)}, u32[]{:S(2)}) collective-permute-start(bf16[64,2560]{1,0:T(8,128)(2,1)S(1)} %get-tuple-element.74), channel_id=1, source_target_pairs={{0,192},{64,0},{128,64},{192,128},{1,193},{65,1},{129,65},{193,129... | collective-permute-start | bytes 983048 | tf_op jit(solution)/shard_map/ppermute | solution.py:465
  98.3 1.8 %shard_map.109.prior_ref = f32[256,1536]{1,0:T(8,128)S(1)} custom-call(bf16[256,2048]{1,0:T(8,128)(2,1)S(1)} %shard_map.105.coef_ref, bf16[2048,512]{1,0:T(8,128)(2,1)S(1)} %get-tuple-element.51.refs_0_, bf16[2048,512]{1,0:T(8,128)(2,1)S(1)} %get-tuple-element.52.refs_1_, bf16[2048,512]{1,0:T(8,128)(2,1)S(1)} %get-tuple-element.53.refs_2_), custom_call_target="tpu_custom_call" | custom-call | flops 1610612736 | bytes 6291456 | tf_op jit(solution)/shard_map/pallas_call | solution.py:242
  100.1 0.6 shard_map.110
  100.7 0.6 collective-permute-start.16
  101.2 1.9 %collective-permute-start.17 = (bf16[64,1536]{1,0:T(8,128)(2,1)S(1)}, bf16[64,1536]{1,0:T(8,128)(2,1)S(1)}, u32[]{:S(2)}, u32[]{:S(2)}) collective-permute-start(bf16[64,1536]{1,0:T(8,128)(2,1)S(1)} %get-tuple-element.59), channel_id=1, source_target_pairs={{0,128},{64,192},{128,0},{192,64},{1,129},{65,193},{129,1},{193,65... | collective-permute-start | bytes 589832 | tf_op jit(solution)/shard_map/ppermute | solution.py:465
  103.1 2.0 %collective-permute-start.18 = (bf16[64,1536]{1,0:T(8,128)(2,1)S(1)}, bf16[64,1536]{1,0:T(8,128)(2,1)S(1)}, u32[]{:S(2)}, u32[]{:S(2)}) collective-permute-start(bf16[64,1536]{1,0:T(8,128)(2,1)S(1)} %get-tuple-element.60), channel_id=1, source_target_pairs={{0,192},{64,0},{128,64},{192,128},{1,193},{65,1},{129,65},{193,129... | collective-permute-start | bytes 589832 | tf_op jit(solution)/shard_map/ppermute | solution.py:465
  105.1 1.2 collective-permute-done.20.refs_2_
  106.3 7.0 %collective-permute-done.21.refs_3_ = bf16[64,2560]{1,0:T(8,128)(2,1)S(1)} collective-permute-done((bf16[64,2560]{1,0:T(8,128)(2,1)S(1)}, bf16[64,2560]{1,0:T(8,128)(2,1)S(1)}, u32[]{:S(2)}, u32[]{:S(2)}) %collective-permute-start.21) | collective-permute-done | bytes 327712 | tf_op jit(solution)/shard_map/ppermute | solution.py:465
  113.3 1.0 shard_map.118.refs_4_
  114.7 7.1 %collective-permute-done.18.refs_3_ = bf16[64,1536]{1,0:T(8,128)(2,1)S(1)} collective-permute-done((bf16[64,1536]{1,0:T(8,128)(2,1)S(1)}, bf16[64,1536]{1,0:T(8,128)(2,1)S(1)}, u32[]{:S(2)}, u32[]{:S(2)}) %collective-permute-start.18) | collective-permute-done | bytes 196640 | tf_op jit(solution)/shard_map/ppermute | solution.py:465
  121.8 0.8 shard_map.119
  (30 shorter events, 2.2 us)
Async XLA Ops:
  0.0 3.8 %collective-permute-start.10 = (bf16[4,2048]{1,0:T(4,128)(2,1)}, bf16[4,2048]{1,0:T(4,128)(2,1)S(1)}, u32[]{:S(2)}, u32[]{:S(2)}) collective-permute-start(bf16[4,2048]{1,0:T(4,128)(2,1)} %refs_0_.3), channel_id=1, source_target_pairs={{0,2},{1,3},{2,0},{3,1},{4,6},{5,7},{6,4},{7,5},{8,10},{9,11},{10,... | collective-permute-start | bytes 49160 | tf_op jit(solution)/shard_map/ppermute | solution.py:335
  3.8 0.7 copy-start.1
  4.5 4.4 %collective-permute-start.11 = (bf16[8,2048]{1,0:T(8,128)(2,1)S(1)}, bf16[8,2048]{1,0:T(8,128)(2,1)S(1)}, u32[]{:S(2)}, u32[]{:S(2)}) collective-permute-start(bf16[8,2048]{1,0:T(8,128)(2,1)S(1)} %shard_map.100.refs_0_), channel_id=1, source_target_pairs={{0,4},{1,5},{2,6},{3,7},{4,0},{5,1},{6,2},{7,3},{8,12},{9,13},{10,... | collective-permute-start | bytes 98312 | tf_op jit(solution)/shard_map/ppermute | solution.py:335
  8.9 6.8 %collective-permute-start.12 = (bf16[16,2048]{1,0:T(8,128)(2,1)S(1)}, bf16[16,2048]{1,0:T(8,128)(2,1)S(1)}, u32[]{:S(2)}, u32[]{:S(2)}) collective-permute-start(bf16[16,2048]{1,0:T(8,128)(2,1)S(1)} %shard_map.101.refs_0_), channel_id=1, source_target_pairs={{0,14},{1,15},{2,12},{3,13},{4,10},{5,11},{6,8},{7,9},{8,6},{9,7},... | collective-permute-start | bytes 196616 | tf_op jit(solution)/shard_map/ppermute | solution.py:335
  15.7 3.9 %collective-permute-start.13 = (bf16[32,2048]{1,0:T(8,128)(2,1)S(1)}, bf16[32,2048]{1,0:T(8,128)(2,1)S(1)}, u32[]{:S(2)}, u32[]{:S(2)}) collective-permute-start(bf16[32,2048]{1,0:T(8,128)(2,1)S(1)} %shard_map.102.refs_0_), channel_id=1, source_target_pairs={{0,16},{1,17},{2,18},{3,19},{4,20},{5,21},{6,22},{7,23},{8,24},{9,... | collective-permute-start | bytes 393224 | tf_op jit(solution)/shard_map/ppermute | solution.py:335
  19.6 6.5 %collective-permute-start.14 = (bf16[64,2048]{1,0:T(8,128)(2,1)S(1)}, bf16[64,2048]{1,0:T(8,128)(2,1)S(1)}, u32[]{:S(2)}, u32[]{:S(2)}) collective-permute-start(bf16[64,2048]{1,0:T(8,128)(2,1)S(1)} %shard_map.103.refs_0_), channel_id=1, source_target_pairs={{0,48},{1,49},{2,50},{3,51},{4,52},{5,53},{6,54},{7,55},{8,56},{9,... | collective-permute-start | bytes 786440 | tf_op jit(solution)/shard_map/ppermute | solution.py:335
  26.2 58.3 %collective-permute-start.15 = (bf16[128,2048]{1,0:T(8,128)(2,1)S(1)}, bf16[128,2048]{1,0:T(8,128)(2,1)S(1)}, u32[]{:S(2)}, u32[]{:S(2)}) collective-permute-start(bf16[128,2048]{1,0:T(8,128)(2,1)S(1)} %shard_map.104.near_ref), channel_id=1, source_target_pairs={{0,1},{1,0},{2,3},{3,2},{4,5},{5,4},{6,7},{7,6},{8,9},{9,8},{10,11... | collective-permute-start | bytes 1572872 | tf_op jit(solution)/shard_map/ppermute | solution.py:335
  32.9 2.6 %copy-start = (f32[4,512]{1,0:T(4,128)S(1)}, f32[4,512]{1,0:T(4,128)}, u32[]{:S(2)}) copy-start(f32[4,512]{1,0:T(4,128)} %whitened_ref.7) | copy-start | bytes 24580
  35.5 0.7 collective-permute-start
  36.2 0.7 collective-permute-start.1
  36.9 11.8 %collective-permute-start.2 = (f32[4,512]{1,0:T(4,128)S(1)}, f32[4,512]{1,0:T(4,128)S(1)}, u32[]{:S(2)}, u32[]{:S(2)}) collective-permute-start(f32[4,512]{1,0:T(4,128)S(1)} %get-tuple-element.46), channel_id=1, source_target_pairs={{64,0},{65,1},{66,2},{67,3},{68,4},{69,5},{70,6},{71,7},{72,8},{73... | collective-permute-start | bytes 24584 | tf_op jit(solution)/shard_map/ppermute | solution.py:432
  49.0 2.5 %collective-permute-start.3 = (bf16[4,512]{1,0:T(4,128)(2,1)S(1)}, bf16[4,512]{1,0:T(4,128)(2,1)S(1)}, u32[]{:S(2)}, u32[]{:S(2)}) collective-permute-start(bf16[4,512]{1,0:T(4,128)(2,1)S(1)} %shard_map.94.refs_0_), channel_id=1, source_target_pairs={{0,2},{1,3},{2,0},{3,1},{4,6},{5,7},{6,4},{7,5},{8,10},{9,11},{10,... | collective-permute-start | bytes 12296 | tf_op jit(solution)/shard_map/ppermute | solution.py:335
  51.6 3.4 %collective-permute-start.4 = (bf16[8,512]{1,0:T(8,128)(2,1)S(1)}, bf16[8,512]{1,0:T(8,128)(2,1)S(1)}, u32[]{:S(2)}, u32[]{:S(2)}) collective-permute-start(bf16[8,512]{1,0:T(8,128)(2,1)S(1)} %shard_map.95.refs_0_), channel_id=1, source_target_pairs={{0,4},{1,5},{2,6},{3,7},{4,0},{5,1},{6,2},{7,3},{8,12},{9,13},{10,... | collective-permute-start | bytes 24584 | tf_op jit(solution)/shard_map/ppermute | solution.py:335
  55.0 4.3 %collective-permute-start.5 = (bf16[16,512]{1,0:T(8,128)(2,1)S(1)}, bf16[16,512]{1,0:T(8,128)(2,1)S(1)}, u32[]{:S(2)}, u32[]{:S(2)}) collective-permute-start(bf16[16,512]{1,0:T(8,128)(2,1)S(1)} %shard_map.96.refs_0_), channel_id=1, source_target_pairs={{0,14},{1,15},{2,12},{3,13},{4,10},{5,11},{6,8},{7,9},{8,6},{9,7},... | collective-permute-start | bytes 49160 | tf_op jit(solution)/shard_map/ppermute | solution.py:335
  59.3 3.7 %collective-permute-start.6 = (bf16[32,512]{1,0:T(8,128)(2,1)S(1)}, bf16[32,512]{1,0:T(8,128)(2,1)S(1)}, u32[]{:S(2)}, u32[]{:S(2)}) collective-permute-start(bf16[32,512]{1,0:T(8,128)(2,1)S(1)} %shard_map.97.refs_0_), channel_id=1, source_target_pairs={{0,16},{1,17},{2,18},{3,19},{4,20},{5,21},{6,22},{7,23},{8,24},{9,... | collective-permute-start | bytes 98312 | tf_op jit(solution)/shard_map/ppermute | solution.py:335
  59.3 4.0 %collective-permute-start.7 = (bf16[32,512]{1,0:T(8,128)(2,1)S(1)}, bf16[32,512]{1,0:T(8,128)(2,1)S(1)}, u32[]{:S(2)}, u32[]{:S(2)}) collective-permute-start(bf16[32,512]{1,0:T(8,128)(2,1)S(1)} %shard_map.97.refs_0_), channel_id=1, source_target_pairs={{0,48},{1,49},{2,50},{3,51},{4,52},{5,53},{6,54},{7,55},{8,56},{9,... | collective-permute-start | bytes 98312 | tf_op jit(solution)/shard_map/ppermute | solution.py:335
  61.8 4.3 %collective-permute-start.8 = (bf16[32,512]{1,0:T(8,128)(2,1)S(1)}, bf16[32,512]{1,0:T(8,128)(2,1)S(1)}, u32[]{:S(2)}, u32[]{:S(2)}) collective-permute-start(bf16[32,512]{1,0:T(8,128)(2,1)S(1)} %shard_map.97.refs_0_), channel_id=1, source_target_pairs={{0,32},{1,33},{2,34},{3,35},{4,36},{5,37},{6,38},{7,39},{8,40},{9,... | collective-permute-start | bytes 98312 | tf_op jit(solution)/shard_map/ppermute | solution.py:335
  66.1 18.2 %collective-permute-start.9 = (bf16[128,512]{1,0:T(8,128)(2,1)S(1)}, bf16[128,512]{1,0:T(8,128)(2,1)S(1)}, u32[]{:S(2)}, u32[]{:S(2)}) collective-permute-start(bf16[128,512]{1,0:T(8,128)(2,1)S(1)} %shard_map.98.near_ref), channel_id=1, source_target_pairs={{0,1},{1,0},{2,3},{3,2},{4,5},{5,4},{6,7},{7,6},{8,9},{9,8},{10,11... | collective-permute-start | bytes 393224 | tf_op jit(solution)/shard_map/ppermute | solution.py:335
  88.7 14.4 %collective-permute-start.19 = (bf16[64,2560]{1,0:T(8,128)(2,1)S(1)}, bf16[64,2560]{1,0:T(8,128)(2,1)S(1)}, u32[]{:S(2)}, u32[]{:S(2)}) collective-permute-start(bf16[64,2560]{1,0:T(8,128)(2,1)S(1)} %get-tuple-element.72), channel_id=1, source_target_pairs={{0,64},{64,128},{128,192},{192,0},{1,65},{65,129},{129,193},{193,1... | collective-permute-start | bytes 983048 | tf_op jit(solution)/shard_map/ppermute | solution.py:465
  95.2 11.1 %collective-permute-start.20 = (bf16[64,2560]{1,0:T(8,128)(2,1)S(1)}, bf16[64,2560]{1,0:T(8,128)(2,1)S(1)}, u32[]{:S(2)}, u32[]{:S(2)}) collective-permute-start(bf16[64,2560]{1,0:T(8,128)(2,1)S(1)} %get-tuple-element.73), channel_id=1, source_target_pairs={{0,128},{64,192},{128,0},{192,64},{1,129},{65,193},{129,1},{193,65... | collective-permute-start | bytes 983048 | tf_op jit(solution)/shard_map/ppermute | solution.py:465
  95.6 17.8 %collective-permute-start.21 = (bf16[64,2560]{1,0:T(8,128)(2,1)S(1)}, bf16[64,2560]{1,0:T(8,128)(2,1)S(1)}, u32[]{:S(2)}, u32[]{:S(2)}) collective-permute-start(bf16[64,2560]{1,0:T(8,128)(2,1)S(1)} %get-tuple-element.74), channel_id=1, source_target_pairs={{0,192},{64,0},{128,64},{192,128},{1,193},{65,1},{129,65},{193,129... | collective-permute-start | bytes 983048 | tf_op jit(solution)/shard_map/ppermute | solution.py:465
  100.7 13.7 %collective-permute-start.16 = (bf16[64,1536]{1,0:T(8,128)(2,1)S(1)}, bf16[64,1536]{1,0:T(8,128)(2,1)S(1)}, u32[]{:S(2)}, u32[]{:S(2)}) collective-permute-start(bf16[64,1536]{1,0:T(8,128)(2,1)S(1)} %get-tuple-element.58), channel_id=1, source_target_pairs={{0,64},{64,128},{128,192},{192,0},{1,65},{65,129},{129,193},{193,1... | collective-permute-start | bytes 589832 | tf_op jit(solution)/shard_map/ppermute | solution.py:465
  101.2 13.5 %collective-permute-start.17 = (bf16[64,1536]{1,0:T(8,128)(2,1)S(1)}, bf16[64,1536]{1,0:T(8,128)(2,1)S(1)}, u32[]{:S(2)}, u32[]{:S(2)}) collective-permute-start(bf16[64,1536]{1,0:T(8,128)(2,1)S(1)} %get-tuple-element.59), channel_id=1, source_target_pairs={{0,128},{64,192},{128,0},{192,64},{1,129},{65,193},{129,1},{193,65... | collective-permute-start | bytes 589832 | tf_op jit(solution)/shard_map/ppermute | solution.py:465
  103.1 18.7 %collective-permute-start.18 = (bf16[64,1536]{1,0:T(8,128)(2,1)S(1)}, bf16[64,1536]{1,0:T(8,128)(2,1)S(1)}, u32[]{:S(2)}, u32[]{:S(2)}) collective-permute-start(bf16[64,1536]{1,0:T(8,128)(2,1)S(1)} %get-tuple-element.60), channel_id=1, source_target_pairs={{0,192},{64,0},{128,64},{192,128},{1,193},{65,1},{129,65},{193,129... | collective-permute-start | bytes 589832 | tf_op jit(solution)/shard_map/ppermute | solution.py:465
